TPU v7x, 128 devices: a whole 4x4x4 slice. The times are simulated.
128 devices in a mesh: uly: 4 (over x), blk: 32 (over z, y, core).
Axes of the slice: x: 4, y: 4, z: 4, core: 2. Of those that a mesh axis runs over, the one named last changes fastest.
Arguments:
- video_q: bfloat16 [36864, 3072], P(('blk', 'uly')), may hold values from -16 to 16
- video_k: bfloat16 [36864, 3072], P(('blk', 'uly')), may hold values from -16 to 16
- video_v: bfloat16 [36864, 3072], P(('blk', 'uly')), may hold values from -6 to 6
- text_q: bfloat16 [256, 3072], P('uly'), may hold values from -16 to 16
- text_k: bfloat16 [256, 3072], P('uly'), may hold values from -16 to 16
- text_v: bfloat16 [256, 3072], P('uly'), may hold values from -6 to 6
- window_tiles: int32 [96, 6], P('blk'), may hold values from 0 to 95, as said below
- text_len: int32 [1], replicated, may hold values from 64 to 256
Outputs:
- video_out: bfloat16 [36864, 3072], P(('blk', 'uly'))
- text_out: bfloat16 [256, 3072], P('uly')
Inputs may be any that keep to these rules, and one draw needn't show every extreme that they name: `window_tiles`: tile j lies in time slice j // 3 of 32; row j lists, each once and in any order, the 6 tiles of two consecutive time slices, one of which is the slice of tile j.
All inputs are finite; a program needn't handle non-finite values.
Results may differ from a plain program's by a relative error of at most 0.0036.
Values may be sent and summed in bfloat16 or wider, within the bound.
No kernel may reach another device: no remote copies, remote signals or barrier semaphores. Data moves between devices by JAX's collectives and lax.ppermute only.
A program may use at most 128 MiB of HBM per device.

v0:
```python
import math

import jax
import jax.numpy as jnp
from jax import lax
from jax.sharding import PartitionSpec as P

HEADS = 24
D_HEAD = 128
TILE = 384


def passed_along(block, axis, distance):
    devices = range(lax.axis_size(axis))
    route = [(i - distance, i) for i in devices if i - distance in devices]
    return lax.ppermute(block, axis, route)


def split_heads(matrix):
    return matrix.reshape(matrix.shape[0], HEADS, D_HEAD)


def head_major(tensor):
    return jnp.transpose(tensor, (1, 0, 2))


def local(video_q, video_k, video_v, text_q, text_k, text_v, window_tiles, text_len):
    inv_root = 1.0 / math.sqrt(D_HEAD)
    regrouped = (
        lax.all_to_all(split_heads(video_q), "uly", split_axis=1, concat_axis=0, tiled=True),
        lax.all_to_all(split_heads(video_k), "uly", split_axis=1, concat_axis=0, tiled=True),
        lax.all_to_all(split_heads(video_v), "uly", split_axis=1, concat_axis=0, tiled=True),
        lax.all_to_all(split_heads(text_q), "uly", split_axis=1, concat_axis=0, tiled=True),
        lax.all_to_all(split_heads(text_k), "uly", split_axis=1, concat_axis=0, tiled=True),
        lax.all_to_all(split_heads(text_v), "uly", split_axis=1, concat_axis=0, tiled=True),
    )
    own_q, own_k, own_v, text_qh, text_kh, text_vh = regrouped
    head_queries = head_major(own_q)
    own_kv = jnp.stack([head_major(own_k), head_major(own_v)])
    text_queries = head_major(text_qh)
    text_keys = head_major(text_kh)
    text_values = head_major(text_vh)
    beside = []
    for offset in (1, -1):
        beside.append(passed_along(own_kv, "blk", offset))
    blocks = [beside[0], own_kv, beside[1]]
    heads_dev = own_kv.shape[1]
    row_count = own_kv.shape[2]
    tiles_dev = row_count // TILE
    window_size = window_tiles.shape[1]
    gathered = jnp.concatenate(blocks, axis=2).reshape(2, heads_dev, 3 * tiles_dev, TILE, D_HEAD)
    local_tiles = window_tiles - (lax.axis_index("blk") - 1) * tiles_dev
    live_text = jnp.arange(text_keys.shape[1], dtype=jnp.int32) < text_len[0]

    def video_attention(inputs):
        queries, keys_all, values_all, keys_text, values_text = inputs
        keys_win = jnp.take(keys_all, local_tiles, axis=0).reshape(
            tiles_dev, window_size * TILE, D_HEAD
        )
        values_win = jnp.take(values_all, local_tiles, axis=0).reshape(
            tiles_dev, window_size * TILE, D_HEAD
        )
        tile_queries = queries.reshape(tiles_dev, TILE, D_HEAD)
        win_scores = (
            jnp.einsum("tqd,tkd->tqk", tile_queries, keys_win, preferred_element_type=jnp.float32)
            * inv_root
        )
        txt_scores = (
            jnp.einsum("tqd,kd->tqk", tile_queries, keys_text, preferred_element_type=jnp.float32)
            * inv_root
        )
        txt_scores = jnp.where(live_text, txt_scores, -jnp.inf)
        row_top = jnp.maximum(jnp.max(win_scores, axis=2), jnp.max(txt_scores, axis=2))[:, :, None]
        win_weights = jnp.exp(win_scores - row_top)
        txt_weights = jnp.exp(txt_scores - row_top)
        weight_sum = jnp.sum(win_weights, axis=2) + jnp.sum(txt_weights, axis=2)
        numerator = jnp.einsum(
            "tqk,tkd->tqd",
            win_weights.astype(jnp.bfloat16),
            values_win,
            preferred_element_type=jnp.float32,
        )
        numerator = numerator + jnp.einsum(
            "tqk,kd->tqd",
            txt_weights.astype(jnp.bfloat16),
            values_text,
            preferred_element_type=jnp.float32,
        )
        return (numerator / weight_sum[:, :, None]).astype(jnp.bfloat16).reshape(row_count, D_HEAD)

    video_heads = lax.map(
        video_attention, (head_queries, gathered[0], gathered[1], text_keys, text_values)
    )
    vid_scores = (
        jnp.einsum("hqd,hkd->hqk", text_queries, own_kv[0], preferred_element_type=jnp.float32)
        * inv_root
    )
    txt_scores = (
        jnp.einsum("hqd,hkd->hqk", text_queries, text_keys, preferred_element_type=jnp.float32)
        * inv_root
    )
    txt_scores = jnp.where(live_text, txt_scores, -jnp.inf)
    video_top = lax.pmax(jnp.max(vid_scores, axis=2), "blk")
    row_top = jnp.maximum(video_top, jnp.max(txt_scores, axis=2))[:, :, None]
    vid_weights = jnp.exp(vid_scores - row_top)
    vid_numer = jnp.einsum(
        "hqk,hkd->hqd",
        vid_weights.astype(jnp.bfloat16),
        own_kv[1],
        preferred_element_type=jnp.float32,
    )
    vid_total, vid_numer = lax.psum((jnp.sum(vid_weights, axis=2), vid_numer), "blk")
    txt_weights = jnp.exp(txt_scores - row_top)
    weight_sum = vid_total + jnp.sum(txt_weights, axis=2)
    numerator = vid_numer + jnp.einsum(
        "hqk,hkd->hqd",
        txt_weights.astype(jnp.bfloat16),
        text_values,
        preferred_element_type=jnp.float32,
    )
    text_heads = (numerator / weight_sum[:, :, None]).astype(jnp.bfloat16)
    returned = (
        lax.all_to_all(head_major(video_heads), "uly", split_axis=0, concat_axis=1, tiled=True),
        lax.all_to_all(head_major(text_heads), "uly", split_axis=0, concat_axis=1, tiled=True),
    )
    video_out = returned[0].reshape(returned[0].shape[0], HEADS * D_HEAD)
    text_out = returned[1].reshape(returned[1].shape[0], HEADS * D_HEAD)
    return (video_out, text_out)


def solution(mesh):
    in_specs = (
        P(("blk", "uly"), None),
        P(("blk", "uly"), None),
        P(("blk", "uly"), None),
        P("uly", None),
        P("uly", None),
        P("uly", None),
        P("blk", None),
        P(),
    )
    out_specs = (P(("blk", "uly"), None), P("uly", None))
    return jax.shard_map(local, mesh=mesh, in_specs=in_specs, out_specs=out_specs, check_vma=False)
```

profile of v0, /device:TPU:0, one launch (start us, length us, event | category | flops | bytes accessed | tf_op | source)
XLA Modules:
  0.0 487.6 jit_solution(7533299210076339952)
XLA Ops:
  10.2 4.5 all-to-all-start.1
  16.2 21.3 %all-to-all-done.1 = bf16[288,24,128]{2,0,1:T(8,128)(2,1)S(1)} async-done(((bf16[288,24,128]{2,0,1:T(8,128)(2,1)}), bf16[288,24,128]{2,0,1:T(8,128)(2,1)S(1)}, u32[]{:S(2)}, u32[]{:S(2)}) %all-to-all-start.1) | async-done | bytes 1769504 | tf_op jit(solution)/shard_map/all_to_all | solution.py:31
  37.5 4.4 all-to-all-start.2
  42.1 21.9 %all-to-all-done.2 = bf16[288,24,128]{2,0,1:T(8,128)(2,1)} async-done(((bf16[288,24,128]{2,0,1:T(8,128)(2,1)}), bf16[288,24,128]{2,0,1:T(8,128)(2,1)}, u32[]{:S(2)}, u32[]{:S(2)}) %all-to-all-start.2) | async-done | bytes 1769504 | tf_op jit(solution)/shard_map/all_to_all | solution.py:32
  65.6 2.2 pad_maximum_fusion.1
  67.8 3.1 collective-permute-start
  73.0 4.1 all-to-all-start.6
  77.8 1.9 copy_bitcast_fusion.8
  79.6 6.8 %all-to-all-done.6 = bf16[64,24,128]{2,0,1:T(8,128)(2,1)} async-done(((bf16[64,24,128]{2,0,1:T(8,128)(2,1)}), bf16[64,24,128]{2,0,1:T(8,128)(2,1)}, u32[]{:S(2)}, u32[]{:S(2)}) %all-to-all-start.6) | async-done | bytes 393248 | tf_op jit(solution)/shard_map/all_to_all | solution.py:33
  86.5 4.1 all-to-all-start.3
  90.6 1.9 copy_bitcast_fusion.7
  92.5 6.8 %all-to-all-done.3 = bf16[64,24,128]{2,0,1:T(8,128)(2,1)} async-done(((bf16[64,24,128]{2,0,1:T(8,128)(2,1)}), bf16[64,24,128]{2,0,1:T(8,128)(2,1)}, u32[]{:S(2)}, u32[]{:S(2)}) %all-to-all-start.3) | async-done | bytes 393248 | tf_op jit(solution)/shard_map/all_to_all | solution.py:34
  99.3 4.1 all-to-all-start.4
  103.4 3.0 copy_bitcast_fusion.4
  106.4 1.8 copy.53
  108.2 1.8 copy.47
  111.2 4.4 all-to-all-start
  115.7 1.8 copy.49
  117.5 3.3 fusion.38
  120.7 3.9 multiply_reduce_fusion.1
  124.6 68.0 %pmax.7 = f32[6,256]{1,0:T(8,128)} all-reduce(f32[6,256]{1,0:T(8,128)S(1)} %get-tuple-element.100), channel_id=1, replica_groups=mesh['uly'=4,'blk'=32] {'blk'}, use_global_device_ids=true, to_apply=%region_7.9 | all-reduce | flops 1536 | bytes 12288 | tf_op jit(solution)/shard_map/pmax | solution.py:103
  193.4 5.5 %fusion.24 = f32[6,256,128]{2,1,0:T(8,128)} fusion(bf16[6,1152,128]{2,1,0:T(8,128)(2,1)S(1)} %bitcast.155, f32[6,256,1152]{2,1,0:T(8,128)} %get-tuple-element.101, f32[6,256]{1,0:T(8,128)S(1)} %max.12), kind=kOutput, calls=%fused_computation.41 | convolution fusion | flops 458293248 | bytes 9639936 | tf_op jit(solution)/shard_map/hqk,hkd->hqd/dot_general | solution.py:106
  198.9 5.0 %fusion.22 = f32[6,256]{1,0:T(8,128)} fusion(f32[6,256,1152]{2,1,0:T(8,128)} %get-tuple-element.101, f32[6,256]{1,0:T(8,128)S(1)} %max.12), kind=kLoop, calls=%fused_computation.39 | loop fusion | flops 5306880 | bytes 7090176 | tf_op jit(solution)/shard_map/reduce_sum | solution.py:112
  203.9 2.9 copy.41
  206.7 64.4 %psum.15 = f32[6,256]{1,0:T(8,128)} all-reduce(f32[6,256]{1,0:T(8,128)} %fusion.22), channel_id=1, replica_groups=mesh['uly'=4,'blk'=32] {'blk'}, use_global_device_ids=true, to_apply=%region_11.13 | all-reduce | flops 1536 | bytes 12288 | tf_op jit(solution)/shard_map/psum | solution.py:112
  271.2 1.6 fusion.28
  274.1 25.9 %all-reduce.2.cloned.1.call-done = f32[6,256,128]{2,1,0:T(8,128)} async-done(((f32[6,256,128]{2,1,0:T(8,128)}), f32[6,256,128]{2,1,0:T(8,128)}) %all-reduce.2.cloned.1.call-update) | async-done | bytes 786448 | tf_op jit(solution)/shard_map/psum | solution.py:112
  300.1 2.3 fusion.32
  303.4 4.3 all-to-all-start.7
  307.8 8.0 %pad_maximum_fusion = bf16[2,6,3456,128]{3,2,1,0:T(8,128)(2,1)} fusion(bf16[2,6,1152,128]{3,2,1,0:T(8,128)(2,1)} %collective-permute-done.1, bf16[1,6,1152,128]{3,2,1,0:T(8,128)(2,1)S(1)} %bitcast.156, bf16[1,6,1152,128]{3,2,1,0:T(8,128)(2,1)S(1)} %bitcast.153, bf16[2,6,1152,128]{3,2,1,0:T(8,128)(2,1)} %collective-permute-done), kind=kLoop, calls=%fused_computation.36 | loop fusion | flops 42467328 | bytes 21233664 | tf_op jit(solution)/shard_map/concatenate | solution.py:51
  315.8 8.8 %fusion.37 = (bf16[1,6,3456,128]{3,2,1,0:T(8,128)(2,1)}, bf16[1,6,3456,128]{3,2,1,0:T(8,128)(2,1)}) fusion(bf16[2,6,3456,128]{3,2,1,0:T(8,128)(2,1)} %pad_maximum_fusion), kind=kLoop, calls=%fused_computation.67 | loop fusion | bytes 21233664 | tf_op jit(solution)/shard_map/slice | solution.py:92
  324.6 106.3 %while.11 = (s32[]{:T(128)}, bf16[6,1152,128]{2,1,0:T(8,128)(2,1)}, bf16[6,1152,128]{2,1,0:T(8,128)(2,1)}, bf16[6,9,384,128]{3,2,1,0:T(8,128)(2,1)}, s32[3,6]{1,...) while((s32[]{:T(128)}, bf16[6,1152,128]{2,1,0:T(8,128)(2,1)}, ...), condition=%wide.region_5.7_spmd.clone, body=%wide.region_0.6_spmd.clone.sunk | while | flops 1535458432 | bytes 60074196 | solution.py:91
  327.2 2.1 gather_fusion.1
  329.3 1.9 broadcast_select_fusion.3
  335.8 1.9 fusion.76
  337.7 2.6 fusion.75
  344.9 2.1 gather_fusion.1
  347.0 1.9 broadcast_select_fusion.3
  349.8 1.6 multiply_reduce_fusion.3
  353.5 1.9 fusion.76
  355.4 2.6 fusion.75
  362.6 2.1 gather_fusion.1
  364.7 1.9 broadcast_select_fusion.3
  367.5 1.6 multiply_reduce_fusion.3
  371.2 1.9 fusion.76
  373.1 2.6 fusion.75
  380.3 2.1 gather_fusion.1
  382.4 1.9 broadcast_select_fusion.3
  388.9 1.9 fusion.76
  390.8 2.6 fusion.75
  398.0 2.1 gather_fusion.1
  400.1 1.9 broadcast_select_fusion.3
  406.6 1.9 fusion.76
  408.5 2.6 fusion.75
  415.7 2.1 gather_fusion.1
  417.8 1.9 broadcast_select_fusion.3
  420.7 1.6 multiply_reduce_fusion.3
  424.4 1.9 fusion.76
  426.2 2.6 fusion.75
  430.8 7.7 %copy.75 = bf16[6,1152,128]{2,0,1:T(8,128)(2,1)} copy(bf16[6,1152,128]{2,1,0:T(8,128)(2,1)} %get-tuple-element.50) | data formatting | bytes 3538944 | tf_op jit(solution)/shard_map/while | solution.py:91
  438.5 4.7 all-to-all-start.5
  445.5 27.0 %all-to-all-done.5 = bf16[1152,6,128]{2,1,0:T(8,128)(2,1)} async-done(((bf16[1152,6,128]{2,1,0:T(8,128)(2,1)}), bf16[1152,6,128]{2,1,0:T(8,128)(2,1)}, u32[]{:S(2)}, u32[]{:S(2)}) %all-to-all-start.5) | async-done | bytes 1769504 | tf_op jit(solution)/shard_map/all_to_all | solution.py:123
  472.6 3.5 copy.74
  476.1 4.7 reshape.69
  (120 shorter events, 65.8 us)
Async XLA Ops:
  7.2 1.5 copy-start
  10.2 4.5 copy-start.3
  10.2 27.4 %all-to-all-start.1 = ((bf16[288,24,128]{2,0,1:T(8,128)(2,1)}), bf16[288,24,128]{2,0,1:T(8,128)(2,1)S(1)}, u32[]{:S(2)}, u32[]{:S(2)}) async-start(bf16[288,24,128]{2,0,1:T(8,128)(2,1)} %copy_bitcast_fusion.3), calls=%async_computation.1 | async-start | bytes 3538944 | tf_op jit(solution)/shard_map/all_to_all | solution.py:31
  37.5 26.4 %all-to-all-start.2 = ((bf16[288,24,128]{2,0,1:T(8,128)(2,1)}), bf16[288,24,128]{2,0,1:T(8,128)(2,1)}, u32[]{:S(2)}, u32[]{:S(2)}) async-start(bf16[288,24,128]{2,0,1:T(8,128)(2,1)} %copy_bitcast_fusion.2), calls=%async_computation.2 | async-start | bytes 3538944 | tf_op jit(solution)/shard_map/all_to_all | solution.py:32
  65.6 6.6 %copy-start.4 = (bf16[64,3072]{1,0:T(8,128)(2,1)S(1)}, bf16[64,3072]{1,0:T(8,128)(2,1)}, u32[]{:S(2)}) copy-start(bf16[64,3072]{1,0:T(8,128)(2,1)} %param.15) | copy-start | bytes 1179652
  65.6 11.5 %copy-start.5 = (s32[3,6]{1,0:T(4,128)S(1)}, s32[3,6]{1,0:T(4,128)}, u32[]{:S(2)}) copy-start(s32[3,6]{1,0:T(4,128)} %param.18) | copy-start | bytes 220
  67.8 240.0 %collective-permute-start = (bf16[2,6,1152,128]{3,2,1,0:T(8,128)(2,1)}, bf16[2,6,1152,128]{3,2,1,0:T(8,128)(2,1)}, u32[]{:S(2)}, u32[]{:S(2)}) collective-permute-start(bf16[2,6,1152,128]{3,2,1,0:T(8,128)(2,1)} %pad_maximum_fusion.1), channel_id=1, source_target_pairs={{0,1},{1,2},{2,3},{3,4},{4,5},{5,6},{6,7},{7,8},{8,9},{9,10},{10,1... | collective-permute-start | bytes 10616840 | tf_op jit(solution)/shard_map/ppermute | solution.py:16
  70.8 236.9 %collective-permute-start.1 = (bf16[2,6,1152,128]{3,2,1,0:T(8,128)(2,1)}, bf16[2,6,1152,128]{3,2,1,0:T(8,128)(2,1)}, u32[]{:S(2)}, u32[]{:S(2)}) collective-permute-start(bf16[2,6,1152,128]{3,2,1,0:T(8,128)(2,1)} %pad_maximum_fusion.1), channel_id=1, source_target_pairs={{1,0},{2,1},{3,2},{4,3},{5,4},{6,5},{7,6},{8,7},{9,8},{10,9},{11,1... | collective-permute-start | bytes 10616840 | tf_op jit(solution)/shard_map/ppermute | solution.py:16
  73.0 13.5 %all-to-all-start.6 = ((bf16[64,24,128]{2,0,1:T(8,128)(2,1)}), bf16[64,24,128]{2,0,1:T(8,128)(2,1)}, u32[]{:S(2)}, u32[]{:S(2)}) async-start(bf16[64,24,128]{2,0,1:T(8,128)(2,1)} %copy_bitcast_fusion.6), calls=%async_computation.6 | async-start | bytes 786432 | tf_op jit(solution)/shard_map/all_to_all | solution.py:33
  86.5 12.8 %all-to-all-start.3 = ((bf16[64,24,128]{2,0,1:T(8,128)(2,1)}), bf16[64,24,128]{2,0,1:T(8,128)(2,1)}, u32[]{:S(2)}, u32[]{:S(2)}) async-start(bf16[64,24,128]{2,0,1:T(8,128)(2,1)} %copy_bitcast_fusion.8), calls=%async_computation.3 | async-start | bytes 786432 | tf_op jit(solution)/shard_map/all_to_all | solution.py:34
  99.3 12.0 %all-to-all-start.4 = ((bf16[64,24,128]{2,0,1:T(8,128)(2,1)}), bf16[64,24,128]{2,0,1:T(8,128)(2,1)}, u32[]{:S(2)}, u32[]{:S(2)}) async-start(bf16[64,24,128]{2,0,1:T(8,128)(2,1)} %copy_bitcast_fusion.7), calls=%async_computation.4 | async-start | bytes 786432 | tf_op jit(solution)/shard_map/all_to_all | solution.py:35
  111.2 92.7 %all-to-all-start = ((bf16[288,24,128]{2,0,1:T(8,128)(2,1)}), bf16[288,24,128]{2,0,1:T(8,128)(2,1)}, u32[]{:S(2)}, u32[]{:S(2)}) async-start(bf16[288,24,128]{2,0,1:T(8,128)(2,1)} %copy_bitcast_fusion.4), calls=%async_computation | async-start | bytes 3538944 | tf_op jit(solution)/shard_map/all_to_all | solution.py:30
  115.6 184.5 %all-reduce.2.cloned.1.call-start = ((), (), s32[]{:S(2)}) async-start(), calls=%async_computation.8 | async-start | bytes 1572864 | tf_op jit(solution)/shard_map/psum | solution.py:112
  115.7 5.1 %copy-start.2 = (bf16[4,64,6,128]{3,1,0,2:T(8,128)(2,1)S(1)}, bf16[4,64,6,128]{3,1,0,2:T(8,128)(2,1)}, u32[]{:S(2)}) copy-start(bf16[4,64,6,128]{3,1,0,2:T(8,128)(2,1)} %copy.53) | copy-start | bytes 1179652
  303.4 135.1 %all-to-all-start.7 = ((bf16[256,6,128]{2,1,0:T(8,128)(2,1)}), bf16[256,6,128]{2,1,0:T(8,128)(2,1)}, u32[]{:S(2)}, u32[]{:S(2)}) async-start(bf16[256,6,128]{2,1,0:T(8,128)(2,1)} %copy.55), calls=%async_computation.7 | async-start | bytes 1048576 | tf_op jit(solution)/shard_map/all_to_all | solution.py:124
  438.5 34.1 %all-to-all-start.5 = ((bf16[1152,6,128]{2,1,0:T(8,128)(2,1)}), bf16[1152,6,128]{2,1,0:T(8,128)(2,1)}, u32[]{:S(2)}, u32[]{:S(2)}) async-start(bf16[1152,6,128]{2,1,0:T(8,128)(2,1)} %bitcast.159), calls=%async_computation.5 | async-start | bytes 4718592 | tf_op jit(solution)/shard_map/all_to_all | solution.py:123
  476.1 4.7 copy-start.1
Sparse Core Ops, SparseCore 0:
  199.0 101.0 all-reduce.1
where the time goes:
time: 490 us; the launch traced here: 488 us
  blocking collectives  132 us (27%)
  waiting for transfers between devices  111 us (23%)
  local copies, waits for them, and re-layouts  88.4 us (18%)
  matrix products  54.9 us (11%)
  other arithmetic  46.4 us (9%)
  starting transfers between devices  39 us (8%)
  between operations  14.9 us (3%)
    pmax x1, blocking collectives, local(): video_top = lax.pmax(jnp.max(vid_scores, axis=2), 'blk')  68 us
    psum x1, blocking collectives, local(): lax.psum((jnp.sum(vid_weights, axis=2), vid_numer), 'blk')  64.4 us
    all_to_all x1, waiting for transfers between devices, local(): lax.all_to_all(head_major(video_heads), 'uly', split_axis=0, concat_axis=...  27 us
    psum x1, waiting for transfers between devices, local(): lax.psum((jnp.sum(vid_weights, axis=2), vid_numer), 'blk')  25.9 us
    all_to_all x1, waiting for transfers between devices, local(): lax.all_to_all(split_heads(video_v), 'uly', split_axis=1, concat_axis=0,...  21.9 us
    all_to_all x1, waiting for transfers between devices, local(): lax.all_to_all(split_heads(video_k), 'uly', split_axis=1, concat_axis=0,...  21.3 us
    dot_general x6, matrix products, video_attention(): jnp.einsum('tqk,tkd->tqd', win_weights.astype(jnp.bfloat16), values_win,...  15.3 us
    gather x6, local copies, waits for them, and re-layouts, video_attention(): jnp.take(values_all, local_tiles, axis=0)  12.6 us
  transfers between devices with their start and end apart: 11, of which 7 were waited for; matrix products, arithmetic and copies ran while one was open for 36% of the time, Pallas kernels for 0%

commit v1 on v0

v1 whole, which is shorter than its diff:
```python
import functools
import math

import jax
import jax.numpy as jnp
from jax import lax
from jax.experimental import pallas as pl
from jax.experimental.pallas import tpu as pltpu
from jax.sharding import PartitionSpec as P


HEADS = 24
D = 128
TXT = 256
GROUP = 4
HD = HEADS // GROUP
ROWS = 288
SLICE = ROWS * GROUP
TILE = 384
TROWS = TXT // GROUP
BLK = 32
DEVS = GROUP * BLK
RB = 128
KEYS = 2 * SLICE + TXT
SCALE = math.log2(math.e) / math.sqrt(D)
CHUNKS = ((0, 3), (3, 3))
BF = jnp.bfloat16
F32 = jnp.float32


HBM = pl.BlockSpec(memory_space=pltpu.HBM)
SMEM = pl.BlockSpec(memory_space=pltpu.SMEM)
VMEM = pl.BlockSpec(memory_space=pltpu.VMEM)


def place(distance):
    return (lax.axis_index("uly") + distance + GROUP) % GROUP


def column(head):
    return pl.ds(pl.multiple_of(head * D, D), D)


def rows_of(position, count):
    return pl.ds(pl.multiple_of(position * count, 32), count)


def run(moves):
    for move in moves:
        move.start()


def wait(moves):
    for move in moves:
        move.wait()


def copy_list(pairs, sems):
    return [pltpu.make_async_copy(a, b, sems.at[i]) for i, (a, b) in enumerate(pairs)]


def pack(arrays, jobs):
    outs = []
    for numbers, _, heads, together in jobs:
        shape = (len(numbers), heads, arrays[numbers[0]].shape[0], D)
        if together:
            outs.append(jax.ShapeDtypeStruct((GROUP, *shape), BF))
        else:
            outs += [jax.ShapeDtypeStruct(shape, BF)] * GROUP

    def body(*refs):
        ins, rest = refs[: len(arrays)], refs[len(arrays) :]
        dst, held, in_sems, out_sems = rest[: len(outs)], rest[len(outs) : -2], rest[-2], rest[-1]
        reads, writes, n = [], [], 0
        for numbers, first, heads, together in jobs:
            for d in range(GROUP):
                group = d if together else place(d)
                here = held[n].at[d] if together else held[n]
                there = dst[n].at[d] if together else dst[n]
                pairs = [
                    (ins[k].at[:, column(group * HD + first + h)], here.at[i, h])
                    for i, k in enumerate(numbers)
                    for h in range(heads)
                ]
                base = sum(len(r) for r in reads)
                reads.append([pltpu.make_async_copy(x, y, in_sems.at[base + i]) for i, (x, y) in enumerate(pairs)])
                writes.append(pltpu.make_async_copy(here, there, out_sems.at[len(writes)]))
                n += not together
            n += together
        for read in reads:
            run(read)
        for read, write in zip(reads, writes):
            wait(read)
            write.start()
        wait(writes)

    got = pl.pallas_call(
        body,
        in_specs=[HBM] * len(arrays),
        out_specs=[HBM] * len(outs),
        out_shape=outs,
        scratch_shapes=[pltpu.VMEM(o.shape, BF) for o in outs]
        + [pltpu.SemaphoreType.DMA((160,)), pltpu.SemaphoreType.DMA((32,))],
    )(*arrays)
    result, n = [], 0
    for job in jobs:
        result.append(got[n] if job[3] else got[n : n + GROUP])
        n += 1 if job[3] else GROUP
    return result


def around(block, distance):
    return lax.ppermute(block, "uly", [(i, (i + distance) % GROUP) for i in range(GROUP)])


def exchange(pieces):
    got = [pieces[0]]
    for d in range(1, GROUP):
        got.append(around(pieces[d], d))
    return got


def swap(array, axes):
    return lax.all_to_all(array, axes, 0, 0, tiled=True)


def beside(block, distance):
    return lax.ppermute(block, "blk", [(i, i + distance) for i in range(BLK) if 0 <= i + distance < BLK])


def text_bias(length):
    lane = lax.broadcasted_iota(jnp.int32, (1, TXT), 1)
    position = (lax.axis_index("uly") + GROUP - lane // TROWS) % GROUP * TROWS + lane % TROWS
    return jnp.where(position < length, 0.0, -jnp.inf).astype(F32)


def weigh(q, keys, values, masked):
    s = lax.dot_general(q, keys(), (((1,), (1,)), ((), ())), preferred_element_type=F32)
    return s, lambda: finish(s, values, masked)


def finish(s, values, masked):
    parts, at = [], 0
    for start, bias in masked:
        parts += [s[:, at:start], s[:, start : start + TXT] + bias]
        at = start + TXT
    if at < s.shape[1]:
        parts.append(s[:, at:])
    s = jnp.concatenate([p for p in parts if p.shape[1]], axis=1)
    top = jnp.max(s, axis=1, keepdims=True)
    p = jnp.exp2(s * SCALE - top * SCALE)
    total = jnp.sum(p, axis=1, keepdims=True)
    o = jnp.dot(p.astype(BF), values(), preferred_element_type=F32)
    return o / total, top * SCALE + jnp.log2(total)


SLOT = 16
PAIRS = 12


def text_body(length, *refs):
    text, kv, refs = refs[:GROUP], refs[GROUP : GROUP + len(CHUNKS)], refs[GROUP + len(CHUNKS) :]
    out_ref, q_sc, kv_sc, o_sc, log_sc, sc, slots, sems = refs
    pairs = []
    for d in range(GROUP):
        pairs.append((text[d].at[0], q_sc.at[:, rows_of(place(-d), TROWS)]))
        pairs.append((text[d].at[pl.ds(1, 2)], kv_sc.at[:, :, pl.ds(SLICE + d * TROWS, TROWS)]))
    for c, (first, heads) in enumerate(CHUNKS):
        for g in range(GROUP):
            pairs.append((kv[c].at[g], kv_sc.at[:, pl.ds(first, heads), pl.ds(g * ROWS, ROWS)]))
    moves = copy_list(pairs, sems)
    run(moves)
    sc[...] = jnp.zeros_like(sc)
    bias = jnp.where(lax.axis_index("blk") == 0, text_bias(length[0]), -jnp.inf)
    wait(moves)
    steps = [(h, i) for h in range(HD) for i in range(TXT // RB)]

    def begin(h, i):
        q = q_sc[h, i * RB : (i + 1) * RB]
        return weigh(q, lambda: kv_sc[0, h], lambda: kv_sc[1, h], [(SLICE, bias)])[1]

    rest = begin(*steps[0])
    for n, (h, i) in enumerate(steps):
        following = begin(*steps[n + 1]) if n + 1 < len(steps) else None
        o, log = rest()
        o_sc[h, i * RB : (i + 1) * RB] = o
        log_sc[h, i * RB : (i + 1) * RB] = jnp.broadcast_to(log, (RB, D))
        rest = following
    lane = lax.broadcasted_iota(jnp.int32, (TROWS, D), 1)
    for p in range(2):
        logs = jnp.zeros((TROWS, D), F32)
        for u2 in range(GROUP):
            rows = pl.ds(u2 * TROWS, TROWS)
            for i in range(3):
                s = 3 * u2 + i
                sc[pl.ds(SLOT * p + s, TROWS, stride=2 * SLOT), :] = o_sc[3 * p + i, rows, :]
                logs = jnp.where(lane == s, log_sc[3 * p + i, rows, :], logs)
        for part in range(3):
            rounded = logs.astype(BF).astype(F32)
            sc[pl.ds(SLOT * p + PAIRS + part, TROWS, stride=2 * SLOT), :] = rounded
            logs = logs - rounded
    slots[...] = sc[...].astype(BF).reshape(DEVS, SLOT, D)
    leave(slots, out_ref, sems)


def leave(held, out_ref, sems):
    size = held.shape[0] // 4
    parts = [pl.ds(i * size, size) for i in range(4)]
    moves = copy_list([(held.at[x], out_ref.at[x]) for x in parts], sems)
    run(moves)
    wait(moves)


def text_attention(length, text, kv):
    return pl.pallas_call(
        text_body,
        in_specs=[SMEM] + [HBM] * (GROUP + len(CHUNKS)),
        out_specs=HBM,
        out_shape=jax.ShapeDtypeStruct((DEVS, SLOT, D), BF),
        scratch_shapes=[
            pltpu.VMEM((HD, TXT, D), BF),
            pltpu.VMEM((2, HD, SLICE + TXT, D), BF),
            pltpu.VMEM((HD, TXT, D), F32),
            pltpu.VMEM((HD, TXT, D), F32),
            pltpu.VMEM((DEVS * SLOT, D), F32),
            pltpu.VMEM((DEVS, SLOT, D), BF),
            pltpu.SemaphoreType.DMA((32,)),
        ],
        name="text_attention",
    )(length, *text, *kv)


def combine_body(in_ref, out_ref, sc, res, slots, sems):
    sc[...] = in_ref[...].astype(F32).reshape(DEVS * SLOT, D)
    logs = sc[pl.ds(PAIRS, DEVS, stride=SLOT), :]
    for part in range(1, 3):
        logs = logs + sc[pl.ds(PAIRS + part, DEVS, stride=SLOT), :]
    logs = jnp.transpose(logs)[:SLOT]
    group = lax.broadcasted_iota(jnp.int32, (SLOT, DEVS), 1) % GROUP
    top = jnp.zeros((SLOT, DEVS), F32)
    for u in range(GROUP):
        best = jnp.max(jnp.where(group == u, logs, -jnp.inf), axis=1, keepdims=True)
        top = jnp.where(group == u, best, top)
    weights = jnp.exp2(logs - top)
    total = jnp.ones((SLOT, DEVS), F32)
    for u in range(GROUP):
        all_u = jnp.sum(jnp.where(group == u, weights, 0.0), axis=1, keepdims=True)
        total = jnp.where(group == u, all_u, total)
    weights = weights / total
    mine = lax.broadcasted_iota(jnp.int32, (8, DEVS), 1) % GROUP == lax.broadcasted_iota(jnp.int32, (8, DEVS), 0)
    res[...] = jnp.zeros_like(res)
    for u2 in range(GROUP):
        for i in range(3):
            s = 3 * u2 + i
            left = jnp.where(mine, jnp.broadcast_to(weights[s : s + 1], (8, DEVS)), 0.0)
            values = sc[pl.ds(s, DEVS, stride=SLOT), :]
            got = jnp.dot(left, values, preferred_element_type=F32, precision=lax.Precision.HIGHEST)
            for u in range(GROUP):
                res[u2, pl.ds(3 * u + i, 1), :] = got[u : u + 1]
    done = res[...].astype(BF)
    for b in range(BLK):
        slots[b] = done
    leave(slots, out_ref, sems)


def combine(received):
    return pl.pallas_call(
        combine_body,
        in_specs=[VMEM],
        out_specs=HBM,
        out_shape=jax.ShapeDtypeStruct((BLK, GROUP, SLOT, D), BF),
        scratch_shapes=[
            pltpu.VMEM((DEVS * SLOT, D), F32),
            pltpu.VMEM((GROUP, SLOT, D), F32),
            pltpu.VMEM((BLK, GROUP, SLOT, D), BF),
            pltpu.SemaphoreType.DMA((4,)),
        ],
        name="combine",
    )(received).reshape(DEVS, SLOT, D)


def video_body(first, heads, tiles, length, *refs):
    q_refs, text, refs = refs[:GROUP], refs[GROUP : 2 * GROUP], refs[2 * GROUP :]
    before, own, after, refs = refs[0], refs[1], refs[2], refs[3:]
    o_refs, refs = refs[:GROUP], refs[GROUP:]
    q_sc, k_sc, v_sc, o_sc, side_sc, sems, o_sems = refs

    def loads(start, count, slot):
        some = pl.ds(start, count)
        parts = []
        for a, sc in ((0, k_sc), (1, v_sc)):
            pairs = []
            for base, kv in ((0, before), (SLICE, own), (KEYS, after)):
                for g in range(GROUP):
                    pairs.append((kv.at[g, a, some], sc.at[some, pl.ds(base + g * ROWS, ROWS)]))
            for d in range(GROUP):
                rows = pl.ds(2 * SLICE + d * TROWS, TROWS)
                pairs.append((text[d].at[1 + a, pl.ds(first + start, count)], sc.at[some, rows]))
            parts.append(pairs)
        queries = [(q_refs[d].at[0, some], q_sc.at[some, rows_of(place(-d), ROWS)]) for d in range(GROUP)]
        pairs = queries + parts[0] + parts[1]
        return copy_list(pairs, sems.at[slot]), len(queries + parts[0])

    def stores(h):
        return [
            pltpu.make_async_copy(o_sc.at[h, rows_of(place(d), ROWS)], o_refs[d].at[h], o_sems.at[h, d])
            for d in range(GROUP)
        ]

    head, keys_only = loads(0, 1, 0)
    others, _ = loads(1, heads - 1, 1)
    run(head)
    run(others)
    limit = (lax.axis_index("blk") + 1) * tiles.shape[0]
    for j in range(tiles.shape[0]):
        last = tiles[j, 0]
        for w in range(1, tiles.shape[1]):
            last = jnp.maximum(last, tiles[j, w])
        side_sc[j] = (last >= limit).astype(jnp.int32)
    live = text_bias(length[0])

    def step(h, i):
        f = side_sc[i * RB // TILE]
        window = pl.ds(pl.multiple_of(f * SLICE, RB), KEYS)
        masked = [(SLICE, jnp.where(f == 1, live, 0.0)), (2 * SLICE, jnp.where(f == 1, 0.0, live))]
        q = q_sc[h, i * RB : (i + 1) * RB, :]
        return weigh(q, lambda: k_sc[h, window], lambda: v_sc[h, window], masked)[1]

    steps = SLICE // RB
    wait(head[:keys_only])

    def one(h, _):
        @pl.when(h == 1)
        def _():
            wait(others)

        rest = step(h, 0)

        @pl.when(h == 0)
        def _():
            wait(head[keys_only:])

        for i in range(steps):
            following = step(h, i + 1) if i + 1 < steps else None
            o, _ = rest()
            o_sc[h, i * RB : (i + 1) * RB, :] = o.astype(BF)
            rest = following
        run(stores(h))
        return 0

    lax.fori_loop(0, heads, one, 0)
    for h in range(heads):
        wait(stores(h))


def video_attention(first, heads, tiles, length, q, text, before, own, after):
    return pl.pallas_call(
        functools.partial(video_body, first, heads),
        in_specs=[SMEM, SMEM] + [HBM] * (2 * GROUP + 3),
        out_specs=[HBM] * GROUP,
        out_shape=[jax.ShapeDtypeStruct((heads, ROWS, D), BF)] * GROUP,
        scratch_shapes=[
            pltpu.VMEM((heads, SLICE, D), BF),
            pltpu.VMEM((heads, KEYS + SLICE, D), BF),
            pltpu.VMEM((heads, KEYS + SLICE, D), BF),
            pltpu.VMEM((heads, SLICE, D), BF),
            pltpu.SMEM((8,), jnp.int32),
            pltpu.SemaphoreType.DMA((2, 40)),
            pltpu.SemaphoreType.DMA((heads, GROUP)),
        ],
        name="video_attention",
    )(tiles, length, *q, *text, before, own, after)


SLABS = 6


def rows_body(*refs):
    count = len(CHUNKS) * GROUP
    pieces, slots, video_out, text_out, held, sc, in_sems, out_sems = (refs[:count], *refs[count:])
    pairs = []
    for c, (first, heads) in enumerate(CHUNKS):
        for d in range(GROUP):
            for h in range(heads):
                pairs.append((pieces[c * GROUP + d].at[h], held.at[:, column(place(-d) * HD + first + h)]))
    reads = copy_list(pairs, in_sems)
    run(reads)
    wait(reads)
    size = ROWS // SLABS
    slabs = [pl.ds(i * size, size) for i in range(SLABS)]
    writes = copy_list([(held.at[x], video_out.at[x]) for x in slabs], out_sems)
    run(writes)
    sc[...] = slots[...].astype(F32).reshape(DEVS * SLOT, D)
    for p in range(2):
        for u in range(GROUP):
            for i in range(3):
                rows = sc[pl.ds(SLOT * p + 3 * u + i, TROWS, stride=2 * SLOT), :]
                head = HD * u + 3 * p + i
                text_out[:, head * D : (head + 1) * D] = rows.astype(BF)
    wait(writes)


def side_by_side(chunks, slots):
    flat = [piece for chunk in chunks for piece in chunk]
    return pl.pallas_call(
        rows_body,
        in_specs=[HBM] * len(flat) + [VMEM],
        out_specs=[HBM, VMEM],
        out_shape=[
            jax.ShapeDtypeStruct((ROWS, HEADS * D), BF),
            jax.ShapeDtypeStruct((TROWS, HEADS * D), BF),
        ],
        scratch_shapes=[
            pltpu.VMEM((ROWS, HEADS * D), BF),
            pltpu.VMEM((DEVS * SLOT, D), F32),
            pltpu.SemaphoreType.DMA((HEADS,)),
            pltpu.SemaphoreType.DMA((SLABS,)),
        ],
        name="side_by_side",
    )(*flat, slots)


def local(video_q, video_k, video_v, text_q, text_k, text_v, window_tiles, text_len):
    video, words = (video_q, video_k, video_v), (text_q, text_k, text_v)
    (f0, n0), (f1, n1) = CHUNKS
    (kv0,) = pack(video, [((1, 2), f0, n0, True)])
    text, q0, kv1, q1 = pack(
        video + words, [((3, 4, 5), 0, HD, False), ((0,), f0, n0, False), ((1, 2), f1, n1, True), ((0,), f1, n1, False)]
    )
    own, before, after = [], [], []
    for kv in (kv0, kv1):
        own.append(swap(kv, "uly"))
        before.append(beside(own[-1], 1))
        after.append(beside(own[-1], -1))
    text = exchange(text)
    q = [exchange(q0), exchange(q1)]
    slots = text_attention(text_len, text, own)
    slots = swap(slots, ("blk", "uly"))
    slots = combine(slots)
    slots = swap(slots, ("blk", "uly"))
    back = []
    for c, (first, heads) in enumerate(CHUNKS):
        o = video_attention(first, heads, window_tiles, text_len, q[c], text, before[c], own[c], after[c])
        back.append(exchange(o))
    return side_by_side(back, slots)


def solution(mesh):
    in_specs = (
        P(("blk", "uly"), None),
        P(("blk", "uly"), None),
        P(("blk", "uly"), None),
        P("uly", None),
        P("uly", None),
        P("uly", None),
        P("blk", None),
        P(),
    )
    out_specs = (P(("blk", "uly"), None), P("uly", None))

    return jax.shard_map(local, mesh=mesh, in_specs=in_specs, out_specs=out_specs, check_vma=False)
```

time: 490 us -> 195 us (0.40)
  blocking collectives: 132 us -> 0 us
  local copies, waits for them, and re-layouts: 88.4 us -> 0.76 us
  Pallas kernels: 0 us -> 58.9 us
  matrix products: 54.9 us -> 0 us
  other arithmetic: 46.4 us -> 0 us
  waiting for transfers between devices: 111 us -> 72.8 us
  starting transfers between devices: 39 us -> 59.8 us
  between operations: 14.9 us -> 1.64 us
    pmax x1 -> x0, blocking collectives: 68 us -> none  [local(): video_top = lax.pmax(jnp.max(vid_scores, axis=2), 'blk')]
    psum x1 -> x0, blocking collectives: 64.4 us -> none  [local(): lax.psum((jnp.sum(vid_weights, axis=2), vid_numer), 'blk')]
    pallas_call x0 -> x7, Pallas kernels: none -> 58.9 us  [the longest x2 33.2 us: video_attention(): pl.pallas_call(functools.partial(video_body, first, heads), in_specs=[SME...]
    dot_general x28 -> x0, matrix products: 54.9 us -> none  [the longest x6 15.3 us: video_attention(): jnp.einsum('tqk,tkd->tqd', win_weights.astype(jnp.bfloat16), values_win,...]
    all_to_all x8 -> x4, waiting for transfers between devices: 85.1 us -> 35.8 us  [swap(): return lax.all_to_all(array, axes, 0, 0, tiled=True)]
    ppermute x2 -> x19, waiting for transfers between devices: 0.01 us -> 37 us  [the longest x15 37 us: around(): lax.ppermute(block, 'uly', [(i, (i + distance) % GROUP) for i in range(GR...]
    psum x1 -> x0, waiting for transfers between devices: 25.9 us -> none  [local(): lax.psum((jnp.sum(vid_weights, axis=2), vid_numer), 'blk')]
    ppermute x2 -> x19, starting transfers between devices: 4.36 us -> 29.3 us  [the longest x15 21.7 us: around(): lax.ppermute(block, 'uly', [(i, (i + distance) % GROUP) for i in range(GR...]
  transfers between devices with their start and end apart: 11 -> 23, of which waited for: 7 -> 10; matrix products, arithmetic and copies ran while one was open for 36% -> 0% of each run, Pallas kernels for 0% -> 25%
where the time goes in v1:
time: 195 us; the launch traced here: 194 us
  waiting for transfers between devices  72.8 us (37%)
  starting transfers between devices  59.8 us (31%)
  Pallas kernels  58.9 us (30%)
    ppermute x15, waiting for transfers between devices, around(): lax.ppermute(block, 'uly', [(i, (i + distance) % GROUP) for i in range(GR...  37 us
    all_to_all x4, waiting for transfers between devices, swap(): return lax.all_to_all(array, axes, 0, 0, tiled=True)  35.8 us
    pallas_call x2, Pallas kernels, video_attention(): pl.pallas_call(functools.partial(video_body, first, heads), in_specs=[SME...  33.2 us
    all_to_all x4, starting transfers between devices, swap(): return lax.all_to_all(array, axes, 0, 0, tiled=True)  30.5 us
    ppermute x15, starting transfers between devices, around(): lax.ppermute(block, 'uly', [(i, (i + distance) % GROUP) for i in range(GR...  21.7 us
    pallas_call x2, Pallas kernels, pack(): pl.pallas_call(body, in_specs=[HBM] * len(arrays), out_specs=[HBM] * len(...  10.2 us
    pallas_call x1, Pallas kernels, text_attention(): pl.pallas_call(text_body, in_specs=[SMEM] + [HBM] * (GROUP + len(CHUNKS))...  7.83 us
    ppermute x4, starting transfers between devices, beside(): lax.ppermute(block, 'blk', [(i, i + distance) for i in range(BLK) if 0 <=...  7.62 us
  transfers between devices with their start and end apart: 23, of which 10 were waited for; matrix products, arithmetic and copies ran while one was open for 0% of the time, Pallas kernels for 25%

profile of v1, /device:TPU:0, one launch (start us, length us, event | category | flops | bytes accessed | tf_op | source)
XLA Modules:
  0.0 193.9 jit_solution(7847391317222049031)
XLA Ops:
  0.6 6.1 %shard_map.95 = (bf16[3,6,64,128]{3,2,1,0:T(8,128)(2,1)}, bf16[3,6,64,128]{3,2,1,0:T(8,128)(2,1)}, bf16[3,6,64,128]{3,2,1,0:T(8,128)(2,1)}, bf16[3,6,64,128]{3,2...) custom-call(bf16[288,3072]{1,0:T(8,128)(2,1)} %refs_0_.3, ...), custom_call_target="tpu_custom_call" | custom-call | tf_op jit(solution)/shard_map/pallas_call | solution.py:97
  6.7 4.4 %all-to-all-start.1 = ((bf16[4,2,3,288,128]{4,3,2,1,0:T(8,128)(2,1)}), bf16[4,2,3,288,128]{4,3,2,1,0:T(8,128)(2,1)S(1)}, u32[]{:S(2)}, u32[]{:S(2)}) async-start(bf16[4,2,3,288,128]{4,3,2,1,0:T(8,128)(2,1)} %get-tuple-element.39), calls=%async_computation.1 | async-start | bytes 3538944 | tf_op jit(solution)/shard_map/all_to_all | solution.py:124
  11.1 4.1 %shard_map.96 = bf16[4,2,3,288,128]{4,3,2,1,0:T(8,128)(2,1)} custom-call(bf16[288,3072]{1,0:T(8,128)(2,1)} %refs_0_.3, bf16[288,3072]{1,0:T(8,128)(2,1)} %refs_1_.3, bf16[288,3072]{1,0:T(8,128)(2,1)} %refs_2_.3), custom_call_target="tpu_custom_call" | custom-call | tf_op jit(solution)/shard_map/pallas_call | solution.py:97
  15.2 18.7 %all-to-all-done.1.refs_9_.refs_5_ = bf16[4,2,3,288,128]{4,3,2,1,0:T(8,128)(2,1)S(1)} async-done(((bf16[4,2,3,288,128]{4,3,2,1,0:T(8,128)(2,1)}), bf16[4,2,3,288,128]{4,3,2,1,0:T(8,128)(2,1)S(1)}, u32[]{:S(2)}, u32[]{:S(2)}) %all-to-all-start.1) | async-done | bytes 1769504 | tf_op jit(solution)/shard_map/all_to_all | solution.py:124
  34.0 0.0 copy-start.1
  34.0 3.6 %all-to-all-start = ((bf16[4,2,3,288,128]{4,3,2,1,0:T(8,128)(2,1)}), bf16[4,2,3,288,128]{4,3,2,1,0:T(8,128)(2,1)S(1)}, u32[]{:S(2)}, u32[]{:S(2)}) async-start(bf16[4,2,3,288,128]{4,3,2,1,0:T(8,128)(2,1)} %shard_map.96), calls=%async_computation | async-start | bytes 3538944 | tf_op jit(solution)/shard_map/all_to_all | solution.py:124
  37.5 2.5 %collective-permute-start.14 = (bf16[4,2,3,288,128]{4,3,2,1,0:T(8,128)(2,1)S(1)}, bf16[4,2,3,288,128]{4,3,2,1,0:T(8,128)(2,1)}, u32[]{:S(2)}, u32[]{:S(2)}) collective-permute-start(bf16[4,2,3,288,128]{4,3,2,1,0:T(8,128)(2,1)S(1)} %all-to-all-done.1.refs_9_.refs_5_), channel_id=1, source_target_pairs={{0,1},{1,2},{2,3},{3,4},{4,5},{5,6},{6,7},{7,8},{8,9},{9,10},{10,1... | collective-permute-start | bytes 5308424 | tf_op jit(solution)/shard_map/ppermute | solution.py:128
  40.1 1.3 collective-permute-start.15
  41.4 0.0 copy-done.1
  41.4 2.0 %collective-permute-start.11 = (bf16[1,3,288,128]{3,2,1,0:T(8,128)(2,1)}, bf16[1,3,288,128]{3,2,1,0:T(8,128)(2,1)}, u32[]{:S(2)}, u32[]{:S(2)}) collective-permute-start(bf16[1,3,288,128]{3,2,1,0:T(8,128)(2,1)} %get-tuple-element.36), channel_id=1, source_target_pairs={{0,32},{32,64},{64,96},{96,0},{1,33},{33,65},{65,97},{97,1},{2,34}... | collective-permute-start | bytes 663560 | tf_op jit(solution)/shard_map/ppermute | solution.py:113
  43.4 1.5 collective-permute-start.3
  44.9 16.9 %all-to-all-done.refs_9_.refs_4_ = bf16[4,2,3,288,128]{4,3,2,1,0:T(8,128)(2,1)S(1)} async-done(((bf16[4,2,3,288,128]{4,3,2,1,0:T(8,128)(2,1)}), bf16[4,2,3,288,128]{4,3,2,1,0:T(8,128)(2,1)S(1)}, u32[]{:S(2)}, u32[]{:S(2)}) %all-to-all-start) | async-done | bytes 1769504 | tf_op jit(solution)/shard_map/all_to_all | solution.py:124
  61.8 2.5 %collective-permute-start.6 = (bf16[4,2,3,288,128]{4,3,2,1,0:T(8,128)(2,1)S(1)}, bf16[4,2,3,288,128]{4,3,2,1,0:T(8,128)(2,1)}, u32[]{:S(2)}, u32[]{:S(2)}) collective-permute-start(bf16[4,2,3,288,128]{4,3,2,1,0:T(8,128)(2,1)S(1)} %all-to-all-done.refs_9_.refs_4_), channel_id=1, source_target_pairs={{0,1},{1,2},{2,3},{3,4},{4,5},{5,6},{6,7},{7,8},{8,9},{9,10},{10,1... | collective-permute-start | bytes 5308424 | tf_op jit(solution)/shard_map/ppermute | solution.py:128
  64.3 2.0 %collective-permute-done.11.refs_1_ = bf16[1,3,288,128]{3,2,1,0:T(8,128)(2,1)} collective-permute-done((bf16[1,3,288,128]{3,2,1,0:T(8,128)(2,1)}, bf16[1,3,288,128]{3,2,1,0:T(8,128)(2,1)}, u32[]{:S(2)}, u32[]{:S(2)}) %collective-permute-start.11) | collective-permute-done | bytes 221216 | tf_op jit(solution)/shard_map/ppermute | solution.py:113
  66.3 1.3 collective-permute-start.7
  67.6 2.8 %collective-permute-done.3.refs_5_.refs_1_ = bf16[3,6,64,128]{3,2,1,0:T(8,128)(2,1)} collective-permute-done((bf16[3,6,64,128]{3,2,1,0:T(8,128)(2,1)}, bf16[3,6,64,128]{3,2,1,0:T(8,128)(2,1)}, u32[]{:S(2)}, u32[]{:S(2)}) %collective-permute-start.3) | collective-permute-done | bytes 294944 | tf_op jit(solution)/shard_map/ppermute | solution.py:113
  70.3 0.9 collective-permute-start.4
  71.2 8.3 %collective-permute-done.4.refs_6_.refs_2_ = bf16[3,6,64,128]{3,2,1,0:T(8,128)(2,1)} collective-permute-done((bf16[3,6,64,128]{3,2,1,0:T(8,128)(2,1)}, bf16[3,6,64,128]{3,2,1,0:T(8,128)(2,1)}, u32[]{:S(2)}, u32[]{:S(2)}) %collective-permute-start.4) | collective-permute-done | bytes 294944 | tf_op jit(solution)/shard_map/ppermute | solution.py:113
  79.5 0.9 collective-permute-start.5
  80.4 6.1 %collective-permute-done.5.refs_7_.refs_3_ = bf16[3,6,64,128]{3,2,1,0:T(8,128)(2,1)} collective-permute-done((bf16[3,6,64,128]{3,2,1,0:T(8,128)(2,1)}, bf16[3,6,64,128]{3,2,1,0:T(8,128)(2,1)}, u32[]{:S(2)}, u32[]{:S(2)}) %collective-permute-start.5) | collective-permute-done | bytes 294944 | tf_op jit(solution)/shard_map/ppermute | solution.py:113
  86.6 0.8 collective-permute-start.12
  88.1 0.0 copy-done
  88.1 7.8 %text_attention.1 = bf16[128,16,128]{2,1,0:T(8,128)(2,1)} custom-call(s32[1]{0:T(128)S(6)} %copy.10.length, bf16[3,6,64,128]{3,2,1,0:T(8,128)(2,1)} %get-tuple-element.27.refs_4_.refs_0_, bf16[3,6,64,128]{3,2,1,0:T(8,128)(2,1)} %collective-permute-done.3.refs_5_.refs_1_, bf16[3,6,64,128]{3,2,1,0:T(8,128)(2,1)} %collective-permute-done.4.refs_6_.refs_2_, ...), custom_call_target="tpu_custom_call" | custom-call | tf_op jit(solution)/shard_map/text_attention/pallas_call | solution.py:215
  95.9 13.1 %all-to-all-start.2 = ((bf16[128,16,128]{2,1,0:T(8,128)(2,1)}), bf16[128,16,128]{2,1,0:T(8,128)(2,1)}, u32[]{:S(2)}, u32[]{:S(2)}) async-start(bf16[128,16,128]{2,1,0:T(8,128)(2,1)} %text_attention.1), calls=%async_computation.2 | async-start | bytes 1048576 | tf_op jit(solution)/shard_map/all_to_all | solution.py:124
  109.0 0.0 collective-permute-done.12.refs_2_
  109.0 2.2 %collective-permute-start.13 = (bf16[1,3,288,128]{3,2,1,0:T(8,128)(2,1)}, bf16[1,3,288,128]{3,2,1,0:T(8,128)(2,1)}, u32[]{:S(2)}, u32[]{:S(2)}) collective-permute-start(bf16[1,3,288,128]{3,2,1,0:T(8,128)(2,1)} %get-tuple-element.38), channel_id=1, source_target_pairs={{0,96},{32,0},{64,32},{96,64},{1,97},{33,1},{65,33},{97,65},{2,98}... | collective-permute-start | bytes 663560 | tf_op jit(solution)/shard_map/ppermute | solution.py:113
  111.1 9.0 %collective-permute-done.13.refs_3_ = bf16[1,3,288,128]{3,2,1,0:T(8,128)(2,1)} collective-permute-done((bf16[1,3,288,128]{3,2,1,0:T(8,128)(2,1)}, bf16[1,3,288,128]{3,2,1,0:T(8,128)(2,1)}, u32[]{:S(2)}, u32[]{:S(2)}) %collective-permute-start.13) | collective-permute-done | bytes 221216 | tf_op jit(solution)/shard_map/ppermute | solution.py:113
  120.2 1.5 collective-permute-start
  121.6 0.1 all-to-all-done.2.in_ref
  121.8 2.9 %combine.1 = bf16[32,4,16,128]{3,2,1,0:T(8,128)(2,1)} custom-call(bf16[128,16,128]{2,1,0:T(8,128)(2,1)} %all-to-all-done.2.in_ref), custom_call_target="tpu_custom_call" | custom-call | tf_op jit(solution)/shard_map/combine/pallas_call | solution.py:267
  124.7 9.5 %all-to-all-start.3 = ((bf16[128,16,128]{2,1,0:T(8,128)(2,1)}), bf16[128,16,128]{2,1,0:T(8,128)(2,1)}, u32[]{:S(2)}, u32[]{:S(2)}) async-start(bf16[128,16,128]{2,1,0:T(8,128)(2,1)} %bitcast.1), calls=%async_computation.3 | async-start | bytes 1048576 | tf_op jit(solution)/shard_map/all_to_all | solution.py:124
  134.2 0.0 collective-permute-done.14.refs_8_
  134.2 2.5 %collective-permute-start.1 = (bf16[1,3,288,128]{3,2,1,0:T(8,128)(2,1)}, bf16[1,3,288,128]{3,2,1,0:T(8,128)(2,1)}, u32[]{:S(2)}, u32[]{:S(2)}) collective-permute-start(bf16[1,3,288,128]{3,2,1,0:T(8,128)(2,1)} %get-tuple-element.25), channel_id=1, source_target_pairs={{0,64},{32,96},{64,0},{96,32},{1,65},{33,97},{65,1},{97,33},{2,66}... | collective-permute-start | bytes 663560 | tf_op jit(solution)/shard_map/ppermute | solution.py:113
  136.7 0.0 collective-permute-done.15.refs_10_
  136.7 1.2 collective-permute-start.2
  137.8 16.6 %video_attention.3 = (bf16[3,288,128]{2,1,0:T(8,128)(2,1)}, bf16[3,288,128]{2,1,0:T(8,128)(2,1)}, bf16[3,288,128]{2,1,0:T(8,128)(2,1)}, bf16[3,288,128]{2,1,0:T(8,128)(2,1)}) custom-call(s32[3,6]{1,0:T(4,128)} %tiles.3, s32[1]{0:T(128)S(6)} %copy.10.length, bf16[1,3,288,128]{3,2,1,0:T(8,128)(2,1)} %get-tuple-element.35.refs_0_, ...), custom_call_target="tpu_custom_call" | custom-call | tf_op jit(solution)/shard_map/video_attention/pallas_call | solution.py:357
  154.4 0.0 collective-permute-done.refs_1_
  154.5 0.9 collective-permute-start.16
  155.4 0.0 collective-permute-done.1.refs_2_
  155.4 1.1 collective-permute-start.17
  156.5 0.0 collective-permute-done.2.refs_3_
  156.5 2.1 %collective-permute-start.18 = (bf16[3,288,128]{2,1,0:T(8,128)(2,1)}, bf16[3,288,128]{2,1,0:T(8,128)(2,1)S(1)}, u32[]{:S(2)}, u32[]{:S(2)}) collective-permute-start(bf16[3,288,128]{2,1,0:T(8,128)(2,1)} %get-tuple-element.43), channel_id=1, source_target_pairs={{0,96},{32,0},{64,32},{96,64},{1,97},{33,1},{65,33},{97,65},{2,98}... | collective-permute-start | bytes 663560 | tf_op jit(solution)/shard_map/ppermute | solution.py:113
  158.6 0.0 collective-permute-done.6.refs_8_
  158.6 0.0 collective-permute-done.7.refs_10_
  158.6 0.0 copy-done.8
  158.7 16.6 %video_attention.2 = (bf16[3,288,128]{2,1,0:T(8,128)(2,1)}, bf16[3,288,128]{2,1,0:T(8,128)(2,1)}, bf16[3,288,128]{2,1,0:T(8,128)(2,1)}, bf16[3,288,128]{2,1,0:T(8,128)(2,1)}) custom-call(s32[3,6]{1,0:T(4,128)} %tiles.3, s32[1]{0:T(128)S(6)} %copy.10.length, bf16[1,3,288,128]{3,2,1,0:T(8,128)(2,1)} %get-tuple-element.23.refs_0_, ...), custom_call_target="tpu_custom_call" | custom-call | tf_op jit(solution)/shard_map/video_attention/pallas_call | solution.py:357
  175.3 0.9 collective-permute-start.10
  176.2 1.2 collective-permute-start.8
  177.4 0.0 collective-permute-done.16.refs_5_
  177.4 2.1 %collective-permute-start.9 = (bf16[3,288,128]{2,1,0:T(8,128)(2,1)}, bf16[3,288,128]{2,1,0:T(8,128)(2,1)S(1)}, u32[]{:S(2)}, u32[]{:S(2)}) collective-permute-start(bf16[3,288,128]{2,1,0:T(8,128)(2,1)} %get-tuple-element.33), channel_id=1, source_target_pairs={{0,64},{32,96},{64,0},{96,32},{1,65},{33,97},{65,1},{97,33},{2,66}... | collective-permute-start | bytes 663560 | tf_op jit(solution)/shard_map/ppermute | solution.py:113
  179.4 0.0 all-to-all-done.3.refs_8_
  179.4 0.0 collective-permute-done.17.refs_6_
  179.4 0.0 collective-permute-done.18.refs_7_
  179.5 0.0 copy-start.4
  179.5 4.4 %collective-permute-done.10.refs_3_ = bf16[3,288,128]{2,1,0:T(8,128)(2,1)S(1)} collective-permute-done((bf16[3,288,128]{2,1,0:T(8,128)(2,1)}, bf16[3,288,128]{2,1,0:T(8,128)(2,1)S(1)}, u32[]{:S(2)}, u32[]{:S(2)}) %collective-permute-start.10) | collective-permute-done | bytes 221216 | tf_op jit(solution)/shard_map/ppermute | solution.py:113
  183.9 4.3 %collective-permute-done.8.refs_1_ = bf16[3,288,128]{2,1,0:T(8,128)(2,1)S(1)} collective-permute-done((bf16[3,288,128]{2,1,0:T(8,128)(2,1)}, bf16[3,288,128]{2,1,0:T(8,128)(2,1)S(1)}, u32[]{:S(2)}, u32[]{:S(2)}) %collective-permute-start.8) | collective-permute-done | bytes 221216 | tf_op jit(solution)/shard_map/ppermute | solution.py:113
  188.2 0.0 collective-permute-done.9.refs_2_
  188.2 0.0 copy-done.2
  188.2 0.0 copy-done.3
  188.2 0.0 copy-done.4
  188.2 0.0 copy-done.5
  188.3 0.6 copy-done.6
  188.9 0.1 copy-done.7
  189.0 4.8 %side_by_side.1 = (bf16[288,3072]{1,0:T(8,128)(2,1)}, bf16[64,3072]{1,0:T(8,128)(2,1)}) custom-call(bf16[3,288,128]{2,1,0:T(8,128)(2,1)} %get-tuple-element.31.refs_0_, bf16[3,288,128]{2,1,0:T(8,128)(2,1)} %copy-done.6, bf16[3,288,128]{2,1,0:T(8,128)(2,1)} %copy-done.7, bf16[3,288,128]{2,1,0:T(8,128)(2,1)} %copy-done.5, ...), custom_call_target="tpu_custom_call" | custom-call | tf_op jit(solution)/shard_map/side_by_side/pallas_call | solution.py:405
  (7 shorter events, 0.0 us)
Async XLA Ops:
  6.7 27.2 %all-to-all-start.1 = ((bf16[4,2,3,288,128]{4,3,2,1,0:T(8,128)(2,1)}), bf16[4,2,3,288,128]{4,3,2,1,0:T(8,128)(2,1)S(1)}, u32[]{:S(2)}, u32[]{:S(2)}) async-start(bf16[4,2,3,288,128]{4,3,2,1,0:T(8,128)(2,1)} %get-tuple-element.39), calls=%async_computation.1 | async-start | bytes 3538944 | tf_op jit(solution)/shard_map/all_to_all | solution.py:124
  34.0 7.4 %copy-start.1 = (bf16[4,2,3,288,128]{4,3,2,1,0:T(8,128)(2,1)}, bf16[4,2,3,288,128]{4,3,2,1,0:T(8,128)(2,1)S(1)}, u32[]{:S(2)}) copy-start(bf16[4,2,3,288,128]{4,3,2,1,0:T(8,128)(2,1)S(1)} %all-to-all-done.1.refs_9_.refs_5_) | copy-start | bytes 5308420
  34.0 27.8 %all-to-all-start = ((bf16[4,2,3,288,128]{4,3,2,1,0:T(8,128)(2,1)}), bf16[4,2,3,288,128]{4,3,2,1,0:T(8,128)(2,1)S(1)}, u32[]{:S(2)}, u32[]{:S(2)}) async-start(bf16[4,2,3,288,128]{4,3,2,1,0:T(8,128)(2,1)} %shard_map.96), calls=%async_computation | async-start | bytes 3538944 | tf_op jit(solution)/shard_map/all_to_all | solution.py:124
  37.5 96.6 %collective-permute-start.14 = (bf16[4,2,3,288,128]{4,3,2,1,0:T(8,128)(2,1)S(1)}, bf16[4,2,3,288,128]{4,3,2,1,0:T(8,128)(2,1)}, u32[]{:S(2)}, u32[]{:S(2)}) collective-permute-start(bf16[4,2,3,288,128]{4,3,2,1,0:T(8,128)(2,1)S(1)} %all-to-all-done.1.refs_9_.refs_5_), channel_id=1, source_target_pairs={{0,1},{1,2},{2,3},{3,4},{4,5},{5,6},{6,7},{7,8},{8,9},{9,10},{10,1... | collective-permute-start | bytes 5308424 | tf_op jit(solution)/shard_map/ppermute | solution.py:128
  40.1 96.6 %collective-permute-start.15 = (bf16[4,2,3,288,128]{4,3,2,1,0:T(8,128)(2,1)S(1)}, bf16[4,2,3,288,128]{4,3,2,1,0:T(8,128)(2,1)}, u32[]{:S(2)}, u32[]{:S(2)}) collective-permute-start(bf16[4,2,3,288,128]{4,3,2,1,0:T(8,128)(2,1)S(1)} %all-to-all-done.1.refs_9_.refs_5_), channel_id=1, source_target_pairs={{1,0},{2,1},{3,2},{4,3},{5,4},{6,5},{7,6},{8,7},{9,8},{10,9},{11,1... | collective-permute-start | bytes 5308424 | tf_op jit(solution)/shard_map/ppermute | solution.py:128
  41.4 24.9 %collective-permute-start.11 = (bf16[1,3,288,128]{3,2,1,0:T(8,128)(2,1)}, bf16[1,3,288,128]{3,2,1,0:T(8,128)(2,1)}, u32[]{:S(2)}, u32[]{:S(2)}) collective-permute-start(bf16[1,3,288,128]{3,2,1,0:T(8,128)(2,1)} %get-tuple-element.36), channel_id=1, source_target_pairs={{0,32},{32,64},{64,96},{96,0},{1,33},{33,65},{65,97},{97,1},{2,34}... | collective-permute-start | bytes 663560 | tf_op jit(solution)/shard_map/ppermute | solution.py:113
  43.4 26.9 %collective-permute-start.3 = (bf16[3,6,64,128]{3,2,1,0:T(8,128)(2,1)}, bf16[3,6,64,128]{3,2,1,0:T(8,128)(2,1)}, u32[]{:S(2)}, u32[]{:S(2)}) collective-permute-start(bf16[3,6,64,128]{3,2,1,0:T(8,128)(2,1)} %get-tuple-element.28), channel_id=1, source_target_pairs={{0,32},{32,64},{64,96},{96,0},{1,33},{33,65},{65,97},{97,1},{2,34}... | collective-permute-start | bytes 884744 | tf_op jit(solution)/shard_map/ppermute | solution.py:113
  61.8 26.3 %copy-start = (bf16[4,2,3,288,128]{4,3,2,1,0:T(8,128)(2,1)}, bf16[4,2,3,288,128]{4,3,2,1,0:T(8,128)(2,1)S(1)}, u32[]{:S(2)}) copy-start(bf16[4,2,3,288,128]{4,3,2,1,0:T(8,128)(2,1)S(1)} %all-to-all-done.refs_9_.refs_4_) | copy-start | bytes 5308420
  61.8 96.9 %collective-permute-start.6 = (bf16[4,2,3,288,128]{4,3,2,1,0:T(8,128)(2,1)S(1)}, bf16[4,2,3,288,128]{4,3,2,1,0:T(8,128)(2,1)}, u32[]{:S(2)}, u32[]{:S(2)}) collective-permute-start(bf16[4,2,3,288,128]{4,3,2,1,0:T(8,128)(2,1)S(1)} %all-to-all-done.refs_9_.refs_4_), channel_id=1, source_target_pairs={{0,1},{1,2},{2,3},{3,4},{4,5},{5,6},{6,7},{7,8},{8,9},{9,10},{10,1... | collective-permute-start | bytes 5308424 | tf_op jit(solution)/shard_map/ppermute | solution.py:128
  66.3 92.4 %collective-permute-start.7 = (bf16[4,2,3,288,128]{4,3,2,1,0:T(8,128)(2,1)S(1)}, bf16[4,2,3,288,128]{4,3,2,1,0:T(8,128)(2,1)}, u32[]{:S(2)}, u32[]{:S(2)}) collective-permute-start(bf16[4,2,3,288,128]{4,3,2,1,0:T(8,128)(2,1)S(1)} %all-to-all-done.refs_9_.refs_4_), channel_id=1, source_target_pairs={{1,0},{2,1},{3,2},{4,3},{5,4},{6,5},{7,6},{8,7},{9,8},{10,9},{11,1... | collective-permute-start | bytes 5308424 | tf_op jit(solution)/shard_map/ppermute | solution.py:128
  70.3 9.2 %collective-permute-start.4 = (bf16[3,6,64,128]{3,2,1,0:T(8,128)(2,1)}, bf16[3,6,64,128]{3,2,1,0:T(8,128)(2,1)}, u32[]{:S(2)}, u32[]{:S(2)}) collective-permute-start(bf16[3,6,64,128]{3,2,1,0:T(8,128)(2,1)} %get-tuple-element.29), channel_id=1, source_target_pairs={{0,64},{32,96},{64,0},{96,32},{1,65},{33,97},{65,1},{97,33},{2,66}... | collective-permute-start | bytes 884744 | tf_op jit(solution)/shard_map/ppermute | solution.py:113
  79.5 7.0 %collective-permute-start.5 = (bf16[3,6,64,128]{3,2,1,0:T(8,128)(2,1)}, bf16[3,6,64,128]{3,2,1,0:T(8,128)(2,1)}, u32[]{:S(2)}, u32[]{:S(2)}) collective-permute-start(bf16[3,6,64,128]{3,2,1,0:T(8,128)(2,1)} %get-tuple-element.30), channel_id=1, source_target_pairs={{0,96},{32,0},{64,32},{96,64},{1,97},{33,1},{65,33},{97,65},{2,98}... | collective-permute-start | bytes 884744 | tf_op jit(solution)/shard_map/ppermute | solution.py:113
  86.6 22.4 %collective-permute-start.12 = (bf16[1,3,288,128]{3,2,1,0:T(8,128)(2,1)}, bf16[1,3,288,128]{3,2,1,0:T(8,128)(2,1)}, u32[]{:S(2)}, u32[]{:S(2)}) collective-permute-start(bf16[1,3,288,128]{3,2,1,0:T(8,128)(2,1)} %get-tuple-element.37), channel_id=1, source_target_pairs={{0,64},{32,96},{64,0},{96,32},{1,65},{33,97},{65,1},{97,33},{2,66}... | collective-permute-start | bytes 663560 | tf_op jit(solution)/shard_map/ppermute | solution.py:113
  95.9 25.9 %all-to-all-start.2 = ((bf16[128,16,128]{2,1,0:T(8,128)(2,1)}), bf16[128,16,128]{2,1,0:T(8,128)(2,1)}, u32[]{:S(2)}, u32[]{:S(2)}) async-start(bf16[128,16,128]{2,1,0:T(8,128)(2,1)} %text_attention.1), calls=%async_computation.2 | async-start | bytes 1048576 | tf_op jit(solution)/shard_map/all_to_all | solution.py:124
  109.0 11.2 %collective-permute-start.13 = (bf16[1,3,288,128]{3,2,1,0:T(8,128)(2,1)}, bf16[1,3,288,128]{3,2,1,0:T(8,128)(2,1)}, u32[]{:S(2)}, u32[]{:S(2)}) collective-permute-start(bf16[1,3,288,128]{3,2,1,0:T(8,128)(2,1)} %get-tuple-element.38), channel_id=1, source_target_pairs={{0,96},{32,0},{64,32},{96,64},{1,97},{33,1},{65,33},{97,65},{2,98}... | collective-permute-start | bytes 663560 | tf_op jit(solution)/shard_map/ppermute | solution.py:113
  120.2 34.3 %collective-permute-start = (bf16[1,3,288,128]{3,2,1,0:T(8,128)(2,1)}, bf16[1,3,288,128]{3,2,1,0:T(8,128)(2,1)}, u32[]{:S(2)}, u32[]{:S(2)}) collective-permute-start(bf16[1,3,288,128]{3,2,1,0:T(8,128)(2,1)} %get-tuple-element.24), channel_id=1, source_target_pairs={{0,32},{32,64},{64,96},{96,0},{1,33},{33,65},{65,97},{97,1},{2,34}... | collective-permute-start | bytes 663560 | tf_op jit(solution)/shard_map/ppermute | solution.py:113
  124.7 54.7 %all-to-all-start.3 = ((bf16[128,16,128]{2,1,0:T(8,128)(2,1)}), bf16[128,16,128]{2,1,0:T(8,128)(2,1)}, u32[]{:S(2)}, u32[]{:S(2)}) async-start(bf16[128,16,128]{2,1,0:T(8,128)(2,1)} %bitcast.1), calls=%async_computation.3 | async-start | bytes 1048576 | tf_op jit(solution)/shard_map/all_to_all | solution.py:124
  134.2 21.2 %collective-permute-start.1 = (bf16[1,3,288,128]{3,2,1,0:T(8,128)(2,1)}, bf16[1,3,288,128]{3,2,1,0:T(8,128)(2,1)}, u32[]{:S(2)}, u32[]{:S(2)}) collective-permute-start(bf16[1,3,288,128]{3,2,1,0:T(8,128)(2,1)} %get-tuple-element.25), channel_id=1, source_target_pairs={{0,64},{32,96},{64,0},{96,32},{1,65},{33,97},{65,1},{97,33},{2,66}... | collective-permute-start | bytes 663560 | tf_op jit(solution)/shard_map/ppermute | solution.py:113
  136.7 19.9 %collective-permute-start.2 = (bf16[1,3,288,128]{3,2,1,0:T(8,128)(2,1)}, bf16[1,3,288,128]{3,2,1,0:T(8,128)(2,1)S(1)}, u32[]{:S(2)}, u32[]{:S(2)}) collective-permute-start(bf16[1,3,288,128]{3,2,1,0:T(8,128)(2,1)} %get-tuple-element.26), channel_id=1, source_target_pairs={{0,96},{32,0},{64,32},{96,64},{1,97},{33,1},{65,33},{97,65},{2,98}... | collective-permute-start | bytes 663560 | tf_op jit(solution)/shard_map/ppermute | solution.py:113
  154.5 22.9 %collective-permute-start.16 = (bf16[3,288,128]{2,1,0:T(8,128)(2,1)}, bf16[3,288,128]{2,1,0:T(8,128)(2,1)S(1)}, u32[]{:S(2)}, u32[]{:S(2)}) collective-permute-start(bf16[3,288,128]{2,1,0:T(8,128)(2,1)} %get-tuple-element.41), channel_id=1, source_target_pairs={{0,32},{32,64},{64,96},{96,0},{1,33},{33,65},{65,97},{97,1},{2,34}... | collective-permute-start | bytes 663560 | tf_op jit(solution)/shard_map/ppermute | solution.py:113
  155.4 24.0 %collective-permute-start.17 = (bf16[3,288,128]{2,1,0:T(8,128)(2,1)}, bf16[3,288,128]{2,1,0:T(8,128)(2,1)S(1)}, u32[]{:S(2)}, u32[]{:S(2)}) collective-permute-start(bf16[3,288,128]{2,1,0:T(8,128)(2,1)} %get-tuple-element.42), channel_id=1, source_target_pairs={{0,64},{32,96},{64,0},{96,32},{1,65},{33,97},{65,1},{97,33},{2,66}... | collective-permute-start | bytes 663560 | tf_op jit(solution)/shard_map/ppermute | solution.py:113
  156.5 2.1 %copy-start.8 = (bf16[1,3,288,128]{3,2,1,0:T(8,128)(2,1)}, bf16[1,3,288,128]{3,2,1,0:T(8,128)(2,1)S(1)}, u32[]{:S(2)}) copy-start(bf16[1,3,288,128]{3,2,1,0:T(8,128)(2,1)S(1)} %collective-permute-done.2.refs_3_) | copy-start | bytes 663556
  156.5 22.9 %collective-permute-start.18 = (bf16[3,288,128]{2,1,0:T(8,128)(2,1)}, bf16[3,288,128]{2,1,0:T(8,128)(2,1)S(1)}, u32[]{:S(2)}, u32[]{:S(2)}) collective-permute-start(bf16[3,288,128]{2,1,0:T(8,128)(2,1)} %get-tuple-element.43), channel_id=1, source_target_pairs={{0,96},{32,0},{64,32},{96,64},{1,97},{33,1},{65,33},{97,65},{2,98}... | collective-permute-start | bytes 663560 | tf_op jit(solution)/shard_map/ppermute | solution.py:113
  175.3 8.6 %collective-permute-start.10 = (bf16[3,288,128]{2,1,0:T(8,128)(2,1)}, bf16[3,288,128]{2,1,0:T(8,128)(2,1)S(1)}, u32[]{:S(2)}, u32[]{:S(2)}) collective-permute-start(bf16[3,288,128]{2,1,0:T(8,128)(2,1)} %get-tuple-element.34), channel_id=1, source_target_pairs={{0,96},{32,0},{64,32},{96,64},{1,97},{33,1},{65,33},{97,65},{2,98}... | collective-permute-start | bytes 663560 | tf_op jit(solution)/shard_map/ppermute | solution.py:113
  176.2 12.0 %collective-permute-start.8 = (bf16[3,288,128]{2,1,0:T(8,128)(2,1)}, bf16[3,288,128]{2,1,0:T(8,128)(2,1)S(1)}, u32[]{:S(2)}, u32[]{:S(2)}) collective-permute-start(bf16[3,288,128]{2,1,0:T(8,128)(2,1)} %get-tuple-element.32), channel_id=1, source_target_pairs={{0,32},{32,64},{64,96},{96,0},{1,33},{33,65},{65,97},{97,1},{2,34}... | collective-permute-start | bytes 663560 | tf_op jit(solution)/shard_map/ppermute | solution.py:113
  177.4 10.8 %copy-start.2 = (bf16[3,288,128]{2,1,0:T(8,128)(2,1)}, bf16[3,288,128]{2,1,0:T(8,128)(2,1)S(1)}, u32[]{:S(2)}) copy-start(bf16[3,288,128]{2,1,0:T(8,128)(2,1)S(1)} %collective-permute-done.16.refs_5_) | copy-start | bytes 663556
  177.4 10.8 %collective-permute-start.9 = (bf16[3,288,128]{2,1,0:T(8,128)(2,1)}, bf16[3,288,128]{2,1,0:T(8,128)(2,1)S(1)}, u32[]{:S(2)}, u32[]{:S(2)}) collective-permute-start(bf16[3,288,128]{2,1,0:T(8,128)(2,1)} %get-tuple-element.33), channel_id=1, source_target_pairs={{0,64},{32,96},{64,0},{96,32},{1,65},{33,97},{65,1},{97,33},{2,66}... | collective-permute-start | bytes 663560 | tf_op jit(solution)/shard_map/ppermute | solution.py:113
  179.4 8.8 %copy-start.3 = (bf16[3,288,128]{2,1,0:T(8,128)(2,1)}, bf16[3,288,128]{2,1,0:T(8,128)(2,1)S(1)}, u32[]{:S(2)}) copy-start(bf16[3,288,128]{2,1,0:T(8,128)(2,1)S(1)} %collective-permute-done.17.refs_6_) | copy-start | bytes 663556
  179.5 8.8 %copy-start.4 = (bf16[3,288,128]{2,1,0:T(8,128)(2,1)}, bf16[3,288,128]{2,1,0:T(8,128)(2,1)S(1)}, u32[]{:S(2)}) copy-start(bf16[3,288,128]{2,1,0:T(8,128)(2,1)S(1)} %collective-permute-done.18.refs_7_) | copy-start | bytes 663556
  183.9 4.4 %copy-start.5 = (bf16[3,288,128]{2,1,0:T(8,128)(2,1)}, bf16[3,288,128]{2,1,0:T(8,128)(2,1)S(1)}, u32[]{:S(2)}) copy-start(bf16[3,288,128]{2,1,0:T(8,128)(2,1)S(1)} %collective-permute-done.10.refs_3_) | copy-start | bytes 663556
  188.2 0.7 copy-start.6
  188.2 0.8 copy-start.7

commit v2 on v1

--- a/solution.py
+++ b/solution.py
@@ -18,12 +18,13 @@
 SLICE = ROWS * GROUP
 TILE = 384
 TROWS = TXT // GROUP
+HALF = TROWS // 2
 BLK = 32
 DEVS = GROUP * BLK
 RB = 128
 KEYS = 2 * SLICE + TXT
 SCALE = math.log2(math.e) / math.sqrt(D)
-CHUNKS = ((0, 3), (3, 3))
+CHUNKS = ((0, 2), (2, 4))
 BF = jnp.bfloat16
 F32 = jnp.float32
 
@@ -37,6 +38,10 @@
     return (lax.axis_index("uly") + distance + GROUP) % GROUP
 
 
+def half(which):
+    return (lax.axis_index("blk") + which) % 2
+
+
 def column(head):
     return pl.ds(pl.multiple_of(head * D, D), D)
 
@@ -61,24 +66,25 @@
 
 def pack(arrays, jobs):
     outs = []
-    for numbers, _, heads, together in jobs:
-        shape = (len(numbers), heads, arrays[numbers[0]].shape[0], D)
+    for numbers, _, heads, rows, together in jobs:
+        shape = (len(numbers), heads, rows, D)
         if together:
             outs.append(jax.ShapeDtypeStruct((GROUP, *shape), BF))
         else:
-            outs += [jax.ShapeDtypeStruct(shape, BF)] * GROUP
+            outs += [jax.ShapeDtypeStruct(shape, BF)] * (GROUP + (rows == HALF))
 
     def body(*refs):
         ins, rest = refs[: len(arrays)], refs[len(arrays) :]
         dst, held, in_sems, out_sems = rest[: len(outs)], rest[len(outs) : -2], rest[-2], rest[-1]
         reads, writes, n = [], [], 0
-        for numbers, first, heads, together in jobs:
-            for d in range(GROUP):
-                group = d if together else place(d)
+        for numbers, first, heads, rows, together in jobs:
+            for d in range(GROUP + (rows == HALF)):
+                which = slice(None) if rows == ROWS else rows_of(half(d // GROUP), rows)
+                group = d if together else place(d % GROUP)
                 here = held[n].at[d] if together else held[n]
                 there = dst[n].at[d] if together else dst[n]
                 pairs = [
-                    (ins[k].at[:, column(group * HD + first + h)], here.at[i, h])
+                    (ins[k].at[which, column(group * HD + first + h)], here.at[i, h])
                     for i, k in enumerate(numbers)
                     for h in range(heads)
                 ]
@@ -104,8 +110,9 @@
     )(*arrays)
     result, n = [], 0
     for job in jobs:
-        result.append(got[n] if job[3] else got[n : n + GROUP])
-        n += 1 if job[3] else GROUP
+        count = 1 if job[4] else GROUP + (job[3] == HALF)
+        result.append(got[n] if job[4] else got[n : n + count])
+        n += count
     return result
 
 
@@ -130,7 +137,9 @@
 
 def text_bias(length):
     lane = lax.broadcasted_iota(jnp.int32, (1, TXT), 1)
-    position = (lax.axis_index("uly") + GROUP - lane // TROWS) % GROUP * TROWS + lane % TROWS
+    which = (lane // (TXT // 2) + half(0)) % 2
+    source = (lax.axis_index("uly") + GROUP - lane % (TXT // 2) // HALF) % GROUP
+    position = source * TROWS + which * HALF + lane % HALF
     return jnp.where(position < length, 0.0, -jnp.inf).astype(F32)
 
 
@@ -159,12 +168,12 @@
 
 
 def text_body(length, *refs):
-    text, kv, refs = refs[:GROUP], refs[GROUP : GROUP + len(CHUNKS)], refs[GROUP + len(CHUNKS) :]
+    text, kv, refs = refs[: 2 * GROUP], refs[2 * GROUP :][: len(CHUNKS)], refs[2 * GROUP + len(CHUNKS) :]
     out_ref, q_sc, kv_sc, o_sc, log_sc, sc, slots, sems = refs
     pairs = []
-    for d in range(GROUP):
-        pairs.append((text[d].at[0], q_sc.at[:, rows_of(place(-d), TROWS)]))
-        pairs.append((text[d].at[pl.ds(1, 2)], kv_sc.at[:, :, pl.ds(SLICE + d * TROWS, TROWS)]))
+    for n, piece in enumerate(text):
+        pairs.append((piece.at[0], q_sc.at[:, rows_of(2 * place(-(n % GROUP)) + half(n // GROUP), HALF)]))
+        pairs.append((piece.at[pl.ds(1, 2)], kv_sc.at[:, :, pl.ds(SLICE + n * HALF, HALF)]))
     for c, (first, heads) in enumerate(CHUNKS):
         for g in range(GROUP):
             pairs.append((kv[c].at[g], kv_sc.at[:, pl.ds(first, heads), pl.ds(g * ROWS, ROWS)]))
@@ -214,7 +223,7 @@
 def text_attention(length, text, kv):
     return pl.pallas_call(
         text_body,
-        in_specs=[SMEM] + [HBM] * (GROUP + len(CHUNKS)),
+        in_specs=[SMEM] + [HBM] * (2 * GROUP + len(CHUNKS)),
         out_specs=HBM,
         out_shape=jax.ShapeDtypeStruct((DEVS, SLOT, D), BF),
         scratch_shapes=[
@@ -280,7 +289,7 @@
 
 
 def video_body(first, heads, tiles, length, *refs):
-    q_refs, text, refs = refs[:GROUP], refs[GROUP : 2 * GROUP], refs[2 * GROUP :]
+    q_refs, text, refs = refs[:GROUP], refs[GROUP : 3 * GROUP], refs[3 * GROUP :]
     before, own, after, refs = refs[0], refs[1], refs[2], refs[3:]
     o_refs, refs = refs[:GROUP], refs[GROUP:]
     q_sc, k_sc, v_sc, o_sc, side_sc, sems, o_sems = refs
@@ -293,9 +302,9 @@
             for base, kv in ((0, before), (SLICE, own), (KEYS, after)):
                 for g in range(GROUP):
                     pairs.append((kv.at[g, a, some], sc.at[some, pl.ds(base + g * ROWS, ROWS)]))
-            for d in range(GROUP):
-                rows = pl.ds(2 * SLICE + d * TROWS, TROWS)
-                pairs.append((text[d].at[1 + a, pl.ds(first + start, count)], sc.at[some, rows]))
+            for n, piece in enumerate(text):
+                rows = pl.ds(2 * SLICE + n * HALF, HALF)
+                pairs.append((piece.at[1 + a, pl.ds(first + start, count)], sc.at[some, rows]))
             parts.append(pairs)
         queries = [(q_refs[d].at[0, some], q_sc.at[some, rows_of(place(-d), ROWS)]) for d in range(GROUP)]
         pairs = queries + parts[0] + parts[1]
@@ -356,7 +365,7 @@
 def video_attention(first, heads, tiles, length, q, text, before, own, after):
     return pl.pallas_call(
         functools.partial(video_body, first, heads),
-        in_specs=[SMEM, SMEM] + [HBM] * (2 * GROUP + 3),
+        in_specs=[SMEM, SMEM] + [HBM] * (3 * GROUP + 3),
         out_specs=[HBM] * GROUP,
         out_shape=[jax.ShapeDtypeStruct((heads, ROWS, D), BF)] * GROUP,
         scratch_shapes=[
@@ -365,31 +374,33 @@
             pltpu.VMEM((heads, KEYS + SLICE, D), BF),
             pltpu.VMEM((heads, SLICE, D), BF),
             pltpu.SMEM((8,), jnp.int32),
-            pltpu.SemaphoreType.DMA((2, 40)),
+            pltpu.SemaphoreType.DMA((2, 48)),
             pltpu.SemaphoreType.DMA((heads, GROUP)),
         ],
         name="video_attention",
     )(tiles, length, *q, *text, before, own, after)
 
 
-SLABS = 6
-
-
-def rows_body(*refs):
-    count = len(CHUNKS) * GROUP
-    pieces, slots, video_out, text_out, held, sc, in_sems, out_sems = (refs[:count], *refs[count:])
-    pairs = []
-    for c, (first, heads) in enumerate(CHUNKS):
-        for d in range(GROUP):
-            for h in range(heads):
-                pairs.append((pieces[c * GROUP + d].at[h], held.at[:, column(place(-d) * HD + first + h)]))
-    reads = copy_list(pairs, in_sems)
+def rows_body(first, heads, *refs):
+    pieces, refs = refs[:GROUP], refs[-4:]
+    video_out, held, in_sems, out_sems = refs
+    reads, writes = [], []
+    for d in range(GROUP):
+        for h in range(heads):
+            n = len(reads)
+            reads.append(pltpu.make_async_copy(pieces[d].at[h], held.at[n], in_sems.at[n]))
+            there = video_out.at[:, column(place(-d) * HD + first + h)]
+            writes.append(pltpu.make_async_copy(held.at[n], there, out_sems.at[n]))
     run(reads)
-    wait(reads)
-    size = ROWS // SLABS
-    slabs = [pl.ds(i * size, size) for i in range(SLABS)]
-    writes = copy_list([(held.at[x], video_out.at[x]) for x in slabs], out_sems)
-    run(writes)
+    for read, write in zip(reads, writes):
+        read.wait()
+        write.start()
+    return writes
+
+
+def first_body(first, heads, *refs):
+    pieces, slots, video_out, text_out, held, sc, in_sems, out_sems = refs[:GROUP], *refs[GROUP:]
+    writes = rows_body(first, heads, *pieces, video_out, held, in_sems, out_sems)
     sc[...] = slots[...].astype(F32).reshape(DEVS * SLOT, D)
     for p in range(2):
         for u in range(GROUP):
@@ -400,39 +411,68 @@
     wait(writes)
 
 
-def side_by_side(chunks, slots):
-    flat = [piece for chunk in chunks for piece in chunk]
+def later_body(first, heads, *refs):
+    wait(rows_body(first, heads, *refs))
+
+
+def first_rows(pieces, slots, first, heads):
     return pl.pallas_call(
-        rows_body,
-        in_specs=[HBM] * len(flat) + [VMEM],
+        functools.partial(first_body, first, heads),
+        in_specs=[HBM] * GROUP + [VMEM],
         out_specs=[HBM, VMEM],
         out_shape=[
             jax.ShapeDtypeStruct((ROWS, HEADS * D), BF),
             jax.ShapeDtypeStruct((TROWS, HEADS * D), BF),
         ],
         scratch_shapes=[
-            pltpu.VMEM((ROWS, HEADS * D), BF),
+            pltpu.VMEM((GROUP * heads, ROWS, D), BF),
             pltpu.VMEM((DEVS * SLOT, D), F32),
-            pltpu.SemaphoreType.DMA((HEADS,)),
-            pltpu.SemaphoreType.DMA((SLABS,)),
-        ],
-        name="side_by_side",
-    )(*flat, slots)
+            pltpu.SemaphoreType.DMA((GROUP * heads,)),
+            pltpu.SemaphoreType.DMA((GROUP * heads,)),
+        ],
+        name="first_rows",
+    )(*pieces, slots)
+
+
+def later_rows(pieces, rows, first, heads):
+    return pl.pallas_call(
+        functools.partial(later_body, first, heads),
+        in_specs=[HBM] * (GROUP + 1),
+        out_specs=HBM,
+        out_shape=jax.ShapeDtypeStruct((ROWS, HEADS * D), BF),
+        scratch_shapes=[
+            pltpu.VMEM((GROUP * heads, ROWS, D), BF),
+            pltpu.SemaphoreType.DMA((GROUP * heads,)),
+            pltpu.SemaphoreType.DMA((GROUP * heads,)),
+        ],
+        input_output_aliases={GROUP: 0},
+        name="later_rows",
+    )(*pieces, rows)
 
 
 def local(video_q, video_k, video_v, text_q, text_k, text_v, window_tiles, text_len):
     video, words = (video_q, video_k, video_v), (text_q, text_k, text_v)
     (f0, n0), (f1, n1) = CHUNKS
-    (kv0,) = pack(video, [((1, 2), f0, n0, True)])
-    text, q0, kv1, q1 = pack(
-        video + words, [((3, 4, 5), 0, HD, False), ((0,), f0, n0, False), ((1, 2), f1, n1, True), ((0,), f1, n1, False)]
+    (kv0,) = pack(video, [((1, 2), f0, n0, ROWS, True)])
+    q0, text, kv1, q1 = pack(
+        video + words,
+        [
+            ((0,), f0, n0, ROWS, False),
+            ((3, 4, 5), 0, HD, HALF, False),
+            ((1, 2), f1, n1, ROWS, True),
+            ((0,), f1, n1, ROWS, False),
+        ],
     )
     own, before, after = [], [], []
     for kv in (kv0, kv1):
         own.append(swap(kv, "uly"))
         before.append(beside(own[-1], 1))
         after.append(beside(own[-1], -1))
-    text = exchange(text)
+    mine = exchange(text[:GROUP])
+    other = [text[GROUP]]
+    for d in range(1, GROUP):
+        other.append(lax.ppermute(mine[d], "blk", [(i, i ^ 1) for i in range(BLK)]))
+    text = mine + other
     q = [exchange(q0), exchange(q1)]
     slots = text_attention(text_len, text, own)
     slots = swap(slots, ("blk", "uly"))
@@ -442,7 +482,8 @@
     for c, (first, heads) in enumerate(CHUNKS):
         o = video_attention(first, heads, window_tiles, text_len, q[c], text, before[c], own[c], after[c])
         back.append(exchange(o))
-    return side_by_side(back, slots)
+    rows, text_out = first_rows(back[0], slots, f0, n0)
+    return later_rows(back[1], rows, f1, n1), text_out
 
 
 def solution(mesh):

time: 195 us -> 206 us (1.056)
  waiting for transfers between devices: 72.8 us -> 79.4 us
  local copies, waits for them, and re-layouts: 0.76 us -> 4.1 us
    ppermute x15, waiting for transfers between devices: 37 us -> 42.3 us  [around(): lax.ppermute(block, 'uly', [(i, (i + distance) % GROUP) for i in range(GR...]
    unnamed x18 -> x38, local copies, waits for them, and re-layouts: 0.76 us -> 4.1 us
    ppermute x0 -> x3, waiting for transfers between devices: none -> 2.6 us  [local(): other.append(lax.ppermute(mine[d], 'blk', [(i, i ^ 1) for i in range(BLK)]))]
    pallas_call x2 -> x3, Pallas kernels: 12.6 us -> 13.8 us  [the longest x1 7.9 us: text_attention(): pl.pallas_call(text_body, in_specs=[SMEM] + [HBM] * (2 * GROUP + len(CHUN...]
  transfers between devices with their start and end apart: 23 -> 26, of which waited for: 10 -> 12; matrix products, arithmetic and copies ran while one was open for 0% -> 0% of each run, Pallas kernels for 25% -> 25%
where the time goes in v2:
time: 206 us; the launch traced here: 205 us
  waiting for transfers between devices  79.4 us (39%)
  Pallas kernels  60.8 us (30%)
  starting transfers between devices  58.7 us (28%)
  local copies, waits for them, and re-layouts  4.1 us (2%)
    ppermute x15, waiting for transfers between devices, around(): lax.ppermute(block, 'uly', [(i, (i + distance) % GROUP) for i in range(GR...  42.3 us
    all_to_all x4, waiting for transfers between devices, swap(): return lax.all_to_all(array, axes, 0, 0, tiled=True)  34.6 us
    pallas_call x2, Pallas kernels, video_attention(): pl.pallas_call(functools.partial(video_body, first, heads), in_specs=[SME...  33.8 us
    all_to_all x4, starting transfers between devices, swap(): return lax.all_to_all(array, axes, 0, 0, tiled=True)  29.3 us
    ppermute x15, starting transfers between devices, around(): lax.ppermute(block, 'uly', [(i, (i + distance) % GROUP) for i in range(GR...  20.8 us
    pallas_call x2, Pallas kernels, pack(): pl.pallas_call(body, in_specs=[HBM] * len(arrays), out_specs=[HBM] * len(...  10.1 us
    pallas_call x1, Pallas kernels, text_attention(): pl.pallas_call(text_body, in_specs=[SMEM] + [HBM] * (2 * GROUP + len(CHUN...  7.9 us
    ppermute x4, starting transfers between devices, beside(): lax.ppermute(block, 'blk', [(i, i + distance) for i in range(BLK) if 0 <=...  7.68 us
  transfers between devices with their start and end apart: 26, of which 12 were waited for; matrix products, arithmetic and copies ran while one was open for 0% of the time, Pallas kernels for 25%

profile of v2, /device:TPU:0, one launch (start us, length us, event | category | flops | bytes accessed | tf_op | source)
XLA Modules:
  0.0 204.7 jit_solution(613149392924042327)
XLA Ops:
  0.6 6.3 %shard_map.95 = (bf16[1,2,288,128]{3,2,1,0:T(8,128)(2,1)}, bf16[1,2,288,128]{3,2,1,0:T(8,128)(2,1)}, bf16[1,2,288,128]{3,2,1,0:T(8,128)(2,1)}, bf16[1,2,288,128]...) custom-call(bf16[288,3072]{1,0:T(8,128)(2,1)} %refs_0_.3, ...), custom_call_target="tpu_custom_call" | custom-call | tf_op jit(solution)/shard_map/pallas_call | solution.py:103
  7.0 4.4 %all-to-all-start = ((bf16[4,2,4,288,128]{4,3,2,1,0:T(8,128)(2,1)}), bf16[4,2,4,288,128]{4,3,2,1,0:T(8,128)(2,1)S(1)}, u32[]{:S(2)}, u32[]{:S(2)}) async-start(bf16[4,2,4,288,128]{4,3,2,1,0:T(8,128)(2,1)} %get-tuple-element.35), calls=%async_computation | async-start | bytes 4718592 | tf_op jit(solution)/shard_map/all_to_all | solution.py:131
  11.4 3.8 %shard_map.96 = bf16[4,2,2,288,128]{4,3,2,1,0:T(8,128)(2,1)} custom-call(bf16[288,3072]{1,0:T(8,128)(2,1)} %refs_0_.3, bf16[288,3072]{1,0:T(8,128)(2,1)} %refs_1_.3, bf16[288,3072]{1,0:T(8,128)(2,1)} %refs_2_.3), custom_call_target="tpu_custom_call" | custom-call | tf_op jit(solution)/shard_map/pallas_call | solution.py:103
  15.2 25.3 %all-to-all-done.refs_13_.refs_9_ = bf16[4,2,4,288,128]{4,3,2,1,0:T(8,128)(2,1)S(1)} async-done(((bf16[4,2,4,288,128]{4,3,2,1,0:T(8,128)(2,1)}), bf16[4,2,4,288,128]{4,3,2,1,0:T(8,128)(2,1)S(1)}, u32[]{:S(2)}, u32[]{:S(2)}) %all-to-all-start) | async-done | bytes 2359328 | tf_op jit(solution)/shard_map/all_to_all | solution.py:131
  40.5 3.5 %all-to-all-start.1 = ((bf16[4,2,2,288,128]{4,3,2,1,0:T(8,128)(2,1)}), bf16[4,2,2,288,128]{4,3,2,1,0:T(8,128)(2,1)S(1)}, u32[]{:S(2)}, u32[]{:S(2)}) async-start(bf16[4,2,2,288,128]{4,3,2,1,0:T(8,128)(2,1)} %shard_map.96), calls=%async_computation.1 | async-start | bytes 2359296 | tf_op jit(solution)/shard_map/all_to_all | solution.py:131
  44.1 2.7 %collective-permute-start.9 = (bf16[4,2,4,288,128]{4,3,2,1,0:T(8,128)(2,1)S(1)}, bf16[4,2,4,288,128]{4,3,2,1,0:T(8,128)(2,1)}, u32[]{:S(2)}, u32[]{:S(2)}) collective-permute-start(bf16[4,2,4,288,128]{4,3,2,1,0:T(8,128)(2,1)S(1)} %all-to-all-done.refs_13_.refs_9_), channel_id=1, source_target_pairs={{0,1},{1,2},{2,3},{3,4},{4,5},{5,6},{6,7},{7,8},{8,9},{9,10},{10,1... | collective-permute-start | bytes 7077896 | tf_op jit(solution)/shard_map/ppermute | solution.py:135
  46.8 1.3 collective-permute-start.10
  48.1 2.0 collective-permute-start.3
  50.1 2.7 %collective-permute-start.4 = (bf16[3,6,32,128]{3,2,1,0:T(8,128)(2,1)}, bf16[3,6,32,128]{3,2,1,0:T(8,128)(2,1)}, u32[]{:S(2)}, u32[]{:S(2)}) collective-permute-start(bf16[3,6,32,128]{3,2,1,0:T(8,128)(2,1)} %get-tuple-element.32), channel_id=1, source_target_pairs={{0,64},{32,96},{64,0},{96,32},{1,65},{33,97},{65,1},{97,33},{2,66}... | collective-permute-start | bytes 442376 | tf_op jit(solution)/shard_map/ppermute | solution.py:120
  52.8 9.2 %all-to-all-done.1.refs_13_.refs_8_ = bf16[4,2,2,288,128]{4,3,2,1,0:T(8,128)(2,1)S(1)} async-done(((bf16[4,2,2,288,128]{4,3,2,1,0:T(8,128)(2,1)}), bf16[4,2,2,288,128]{4,3,2,1,0:T(8,128)(2,1)S(1)}, u32[]{:S(2)}, u32[]{:S(2)}) %all-to-all-start.1) | async-done | bytes 1179680 | tf_op jit(solution)/shard_map/all_to_all | solution.py:131
  62.0 2.4 %collective-permute-start.17 = (bf16[4,2,2,288,128]{4,3,2,1,0:T(8,128)(2,1)S(1)}, bf16[4,2,2,288,128]{4,3,2,1,0:T(8,128)(2,1)}, u32[]{:S(2)}, u32[]{:S(2)}) collective-permute-start(bf16[4,2,2,288,128]{4,3,2,1,0:T(8,128)(2,1)S(1)} %all-to-all-done.1.refs_13_.refs_8_), channel_id=1, source_target_pairs={{0,1},{1,2},{2,3},{3,4},{4,5},{5,6},{6,7},{7,8},{8,9},{9,10},{10,1... | collective-permute-start | bytes 3538952 | tf_op jit(solution)/shard_map/ppermute | solution.py:135
  64.4 0.0 collective-permute-done.3.refs_5_.refs_1_
  64.4 1.3 collective-permute-start.18
  65.7 0.5 collective-permute-done.4.refs_6_.refs_2_
  66.2 0.4 collective-permute-start.5
  66.5 6.1 %collective-permute-done.5.refs_7_.refs_3_ = bf16[3,6,32,128]{3,2,1,0:T(8,128)(2,1)S(1)} collective-permute-done((bf16[3,6,32,128]{3,2,1,0:T(8,128)(2,1)}, bf16[3,6,32,128]{3,2,1,0:T(8,128)(2,1)S(1)}, u32[]{:S(2)}, u32[]{:S(2)}) %collective-permute-start.5) | collective-permute-done | bytes 147488 | tf_op jit(solution)/shard_map/ppermute | solution.py:120
  72.6 0.3 collective-permute-start.6
  72.9 1.3 collective-permute-done.6.refs_9_.refs_5_
  74.2 0.3 collective-permute-start.7
  74.5 0.3 copy-done.4
  74.8 0.9 collective-permute-done.7.refs_10_.refs_6_
  75.8 0.7 copy-done.5
  76.4 0.3 collective-permute-start.8
  77.4 0.4 collective-permute-done.8.refs_11_.refs_7_
  77.8 0.6 copy-done.6
  78.5 7.9 %text_attention.1 = bf16[128,16,128]{2,1,0:T(8,128)(2,1)} custom-call(s32[1]{0:T(128)S(6)} %copy.12.length, bf16[3,6,32,128]{3,2,1,0:T(8,128)(2,1)} %get-tuple-element.30.refs_4_.refs_0_, bf16[3,6,32,128]{3,2,1,0:T(8,128)(2,1)} %collective-permute-done.3.refs_5_.refs_1_, bf16[3,6,32,128]{3,2,1,0:T(8,128)(2,1)} %collective-permute-done.4.refs_6_.refs_2_, ...), custom_call_target="tpu_custom_call" | custom-call | tf_op jit(solution)/shard_map/text_attention/pallas_call | solution.py:224
  86.4 11.5 %all-to-all-start.2 = ((bf16[128,16,128]{2,1,0:T(8,128)(2,1)}), bf16[128,16,128]{2,1,0:T(8,128)(2,1)}, u32[]{:S(2)}, u32[]{:S(2)}) async-start(bf16[128,16,128]{2,1,0:T(8,128)(2,1)} %text_attention.1), calls=%async_computation.2 | async-start | bytes 1048576 | tf_op jit(solution)/shard_map/all_to_all | solution.py:131
  97.9 1.0 collective-permute-start.14
  98.9 9.8 %collective-permute-done.14.refs_1_ = bf16[1,2,288,128]{3,2,1,0:T(8,128)(2,1)S(1)} collective-permute-done((bf16[1,2,288,128]{3,2,1,0:T(8,128)(2,1)}, bf16[1,2,288,128]{3,2,1,0:T(8,128)(2,1)S(1)}, u32[]{:S(2)}, u32[]{:S(2)}) %collective-permute-start.14) | collective-permute-done | bytes 147488 | tf_op jit(solution)/shard_map/ppermute | solution.py:120
  108.6 0.8 collective-permute-start.15
  109.4 6.4 %collective-permute-done.15.refs_2_ = bf16[1,2,288,128]{3,2,1,0:T(8,128)(2,1)S(1)} collective-permute-done((bf16[1,2,288,128]{3,2,1,0:T(8,128)(2,1)}, bf16[1,2,288,128]{3,2,1,0:T(8,128)(2,1)S(1)}, u32[]{:S(2)}, u32[]{:S(2)}) %collective-permute-start.15) | collective-permute-done | bytes 147488 | tf_op jit(solution)/shard_map/ppermute | solution.py:120
  115.8 0.8 collective-permute-start.16
  116.6 4.6 %collective-permute-done.16.refs_3_ = bf16[1,2,288,128]{3,2,1,0:T(8,128)(2,1)S(1)} collective-permute-done((bf16[1,2,288,128]{3,2,1,0:T(8,128)(2,1)}, bf16[1,2,288,128]{3,2,1,0:T(8,128)(2,1)S(1)}, u32[]{:S(2)}, u32[]{:S(2)}) %collective-permute-start.16) | collective-permute-done | bytes 147488 | tf_op jit(solution)/shard_map/ppermute | solution.py:120
  121.2 0.0 collective-permute-start
  121.2 0.0 collective-permute-done.17.refs_12_
  121.2 3.4 %collective-permute-start.1 = (bf16[1,4,288,128]{3,2,1,0:T(8,128)(2,1)}, bf16[1,4,288,128]{3,2,1,0:T(8,128)(2,1)}, u32[]{:S(2)}, u32[]{:S(2)}) collective-permute-start(bf16[1,4,288,128]{3,2,1,0:T(8,128)(2,1)} %get-tuple-element.28), channel_id=1, source_target_pairs={{0,64},{32,96},{64,0},{96,32},{1,65},{33,97},{65,1},{97,33},{2,66}... | collective-permute-start | bytes 884744 | tf_op jit(solution)/shard_map/ppermute | solution.py:120
  124.6 0.0 collective-permute-done.18.refs_14_
  124.7 0.2 collective-permute-start.2
  124.9 0.0 all-to-all-done.2.in_ref
  124.9 3.0 %combine.1 = bf16[32,4,16,128]{3,2,1,0:T(8,128)(2,1)} custom-call(bf16[128,16,128]{2,1,0:T(8,128)(2,1)} %all-to-all-done.2.in_ref), custom_call_target="tpu_custom_call" | custom-call | tf_op jit(solution)/shard_map/combine/pallas_call | solution.py:276
  127.9 9.8 %all-to-all-start.3 = ((bf16[128,16,128]{2,1,0:T(8,128)(2,1)}), bf16[128,16,128]{2,1,0:T(8,128)(2,1)S(1)}, u32[]{:S(2)}, u32[]{:S(2)}) async-start(bf16[128,16,128]{2,1,0:T(8,128)(2,1)} %bitcast.1), calls=%async_computation.3 | async-start | bytes 1048576 | tf_op jit(solution)/shard_map/all_to_all | solution.py:131
  137.7 12.5 %video_attention.3 = (bf16[2,288,128]{2,1,0:T(8,128)(2,1)}, bf16[2,288,128]{2,1,0:T(8,128)(2,1)}, bf16[2,288,128]{2,1,0:T(8,128)(2,1)}, bf16[2,288,128]{2,1,0:T(8,128)(2,1)}) custom-call(s32[3,6]{1,0:T(4,128)} %tiles.3, s32[1]{0:T(128)S(6)} %copy.12.length, bf16[1,2,288,128]{3,2,1,0:T(8,128)(2,1)} %get-tuple-element.40.refs_0_, ...), custom_call_target="tpu_custom_call" | custom-call | tf_op jit(solution)/shard_map/video_attention/pallas_call | solution.py:366
  150.2 0.0 collective-permute-done.refs_1_
  150.2 1.0 collective-permute-start.19
  151.2 0.0 collective-permute-done.9.refs_12_
  151.2 0.7 copy-done.10
  151.9 21.4 %video_attention.2 = (bf16[4,288,128]{2,1,0:T(8,128)(2,1)}, bf16[4,288,128]{2,1,0:T(8,128)(2,1)}, bf16[4,288,128]{2,1,0:T(8,128)(2,1)}, bf16[4,288,128]{2,1,0:T(8,128)(2,1)}) custom-call(s32[3,6]{1,0:T(4,128)} %tiles.3, s32[1]{0:T(128)S(6)} %copy.12.length, bf16[1,4,288,128]{3,2,1,0:T(8,128)(2,1)} %get-tuple-element.26.refs_0_, ...), custom_call_target="tpu_custom_call" | custom-call | tf_op jit(solution)/shard_map/video_attention/pallas_call | solution.py:366
  173.3 1.5 collective-permute-start.11
  174.8 2.3 %collective-permute-start.12 = (bf16[4,288,128]{2,1,0:T(8,128)(2,1)}, bf16[4,288,128]{2,1,0:T(8,128)(2,1)S(1)}, u32[]{:S(2)}, u32[]{:S(2)}) collective-permute-start(bf16[4,288,128]{2,1,0:T(8,128)(2,1)} %get-tuple-element.38), channel_id=1, source_target_pairs={{0,64},{32,96},{64,0},{96,32},{1,65},{33,97},{65,1},{97,33},{2,66}... | collective-permute-start | bytes 884744 | tf_op jit(solution)/shard_map/ppermute | solution.py:120
  177.1 1.6 collective-permute-start.13
  178.7 0.8 collective-permute-start.20
  179.5 0.0 collective-permute-done.19.refs_1_
  179.5 2.3 %collective-permute-start.21 = (bf16[2,288,128]{2,1,0:T(8,128)(2,1)S(1)}, bf16[2,288,128]{2,1,0:T(8,128)(2,1)S(1)}, u32[]{:S(2)}, u32[]{:S(2)}) collective-permute-start(bf16[2,288,128]{2,1,0:T(8,128)(2,1)S(1)} %copy-done.17), channel_id=1, source_target_pairs={{0,96},{32,0},{64,32},{96,64},{1,97},{33,1},{65,33},{97,65},{2,98}... | collective-permute-start | bytes 442376 | tf_op jit(solution)/shard_map/ppermute | solution.py:120
  181.9 11.1 %collective-permute-done.20.refs_2_ = bf16[2,288,128]{2,1,0:T(8,128)(2,1)S(1)} collective-permute-done((bf16[2,288,128]{2,1,0:T(8,128)(2,1)S(1)}, bf16[2,288,128]{2,1,0:T(8,128)(2,1)S(1)}, u32[]{:S(2)}, u32[]{:S(2)}) %collective-permute-start.20) | collective-permute-done | bytes 147488 | tf_op jit(solution)/shard_map/ppermute | solution.py:120
  192.9 3.8 %collective-permute-done.21.refs_3_ = bf16[2,288,128]{2,1,0:T(8,128)(2,1)S(1)} collective-permute-done((bf16[2,288,128]{2,1,0:T(8,128)(2,1)S(1)}, bf16[2,288,128]{2,1,0:T(8,128)(2,1)S(1)}, u32[]{:S(2)}, u32[]{:S(2)}) %collective-permute-start.21) | collective-permute-done | bytes 147488 | tf_op jit(solution)/shard_map/ppermute | solution.py:120
  196.8 0.6 copy-done.16
  197.4 0.2 copy-done.2
  197.6 3.7 %first_rows.1 = (bf16[288,3072]{1,0:T(8,128)(2,1)}, bf16[64,3072]{1,0:T(8,128)(2,1)}) custom-call(bf16[2,288,128]{2,1,0:T(8,128)(2,1)} %get-tuple-element.44.refs_0_, bf16[2,288,128]{2,1,0:T(8,128)(2,1)} %copy-done.11, bf16[2,288,128]{2,1,0:T(8,128)(2,1)} %copy-done.15, bf16[2,288,128]{2,1,0:T(8,128)(2,1)} %copy-done.16, bf16[128,16,128]{2,1,0:T(8,128)(2,1)} %copy-done.2), custom_call_target="tpu_custom_call" | custom-call | tf_op jit(solution)/shard_map/first_rows/pallas_call | solution.py:419
  201.4 0.0 collective-permute-done.12.refs_2_
  201.4 0.0 collective-permute-done.13.refs_3_
  201.4 0.7 copy-done.7
  202.1 0.1 copy-done.8
  202.2 0.1 copy-done.9
  202.3 2.3 %later_rows.1 = bf16[288,3072]{1,0:T(8,128)(2,1)} custom-call(bf16[4,288,128]{2,1,0:T(8,128)(2,1)} %get-tuple-element.36.refs_0_, bf16[4,288,128]{2,1,0:T(8,128)(2,1)} %copy-done.7, bf16[4,288,128]{2,1,0:T(8,128)(2,1)} %copy-done.8, bf16[4,288,128]{2,1,0:T(8,128)(2,1)} %copy-done.9, ...), custom_call_target="tpu_custom_call", output_to_operand_aliasing={{}: (4, {})} | custom-call | tf_op jit(solution)/shard_map/later_rows/pallas_call | solution.py:438
  (34 shorter events, 0.1 us)
Async XLA Ops:
  7.0 33.6 %all-to-all-start = ((bf16[4,2,4,288,128]{4,3,2,1,0:T(8,128)(2,1)}), bf16[4,2,4,288,128]{4,3,2,1,0:T(8,128)(2,1)S(1)}, u32[]{:S(2)}, u32[]{:S(2)}) async-start(bf16[4,2,4,288,128]{4,3,2,1,0:T(8,128)(2,1)} %get-tuple-element.35), calls=%async_computation | async-start | bytes 4718592 | tf_op jit(solution)/shard_map/all_to_all | solution.py:131
  40.5 37.9 %copy-start = (bf16[4,2,4,288,128]{4,3,2,1,0:T(8,128)(2,1)}, bf16[4,2,4,288,128]{4,3,2,1,0:T(8,128)(2,1)S(1)}, u32[]{:S(2)}) copy-start(bf16[4,2,4,288,128]{4,3,2,1,0:T(8,128)(2,1)S(1)} %all-to-all-done.refs_13_.refs_9_) | copy-start | bytes 7077892
  40.5 21.5 %all-to-all-start.1 = ((bf16[4,2,2,288,128]{4,3,2,1,0:T(8,128)(2,1)}), bf16[4,2,2,288,128]{4,3,2,1,0:T(8,128)(2,1)S(1)}, u32[]{:S(2)}, u32[]{:S(2)}) async-start(bf16[4,2,2,288,128]{4,3,2,1,0:T(8,128)(2,1)} %shard_map.96), calls=%async_computation.1 | async-start | bytes 2359296 | tf_op jit(solution)/shard_map/all_to_all | solution.py:131
  44.1 107.1 %collective-permute-start.9 = (bf16[4,2,4,288,128]{4,3,2,1,0:T(8,128)(2,1)S(1)}, bf16[4,2,4,288,128]{4,3,2,1,0:T(8,128)(2,1)}, u32[]{:S(2)}, u32[]{:S(2)}) collective-permute-start(bf16[4,2,4,288,128]{4,3,2,1,0:T(8,128)(2,1)S(1)} %all-to-all-done.refs_13_.refs_9_), channel_id=1, source_target_pairs={{0,1},{1,2},{2,3},{3,4},{4,5},{5,6},{6,7},{7,8},{8,9},{9,10},{10,1... | collective-permute-start | bytes 7077896 | tf_op jit(solution)/shard_map/ppermute | solution.py:135
  46.8 104.4 %collective-permute-start.10 = (bf16[4,2,4,288,128]{4,3,2,1,0:T(8,128)(2,1)S(1)}, bf16[4,2,4,288,128]{4,3,2,1,0:T(8,128)(2,1)}, u32[]{:S(2)}, u32[]{:S(2)}) collective-permute-start(bf16[4,2,4,288,128]{4,3,2,1,0:T(8,128)(2,1)S(1)} %all-to-all-done.refs_13_.refs_9_), channel_id=1, source_target_pairs={{1,0},{2,1},{3,2},{4,3},{5,4},{6,5},{7,6},{8,7},{9,8},{10,9},{11,1... | collective-permute-start | bytes 7077896 | tf_op jit(solution)/shard_map/ppermute | solution.py:135
  48.1 16.3 %collective-permute-start.3 = (bf16[3,6,32,128]{3,2,1,0:T(8,128)(2,1)}, bf16[3,6,32,128]{3,2,1,0:T(8,128)(2,1)}, u32[]{:S(2)}, u32[]{:S(2)}) collective-permute-start(bf16[3,6,32,128]{3,2,1,0:T(8,128)(2,1)} %get-tuple-element.31), channel_id=1, source_target_pairs={{0,32},{32,64},{64,96},{96,0},{1,33},{33,65},{65,97},{97,1},{2,34}... | collective-permute-start | bytes 442376 | tf_op jit(solution)/shard_map/ppermute | solution.py:120
  50.1 16.0 %collective-permute-start.4 = (bf16[3,6,32,128]{3,2,1,0:T(8,128)(2,1)}, bf16[3,6,32,128]{3,2,1,0:T(8,128)(2,1)}, u32[]{:S(2)}, u32[]{:S(2)}) collective-permute-start(bf16[3,6,32,128]{3,2,1,0:T(8,128)(2,1)} %get-tuple-element.32), channel_id=1, source_target_pairs={{0,64},{32,96},{64,0},{96,32},{1,65},{33,97},{65,1},{97,33},{2,66}... | collective-permute-start | bytes 442376 | tf_op jit(solution)/shard_map/ppermute | solution.py:120
  62.0 16.5 %copy-start.1 = (bf16[4,2,2,288,128]{4,3,2,1,0:T(8,128)(2,1)}, bf16[4,2,2,288,128]{4,3,2,1,0:T(8,128)(2,1)S(1)}, u32[]{:S(2)}) copy-start(bf16[4,2,2,288,128]{4,3,2,1,0:T(8,128)(2,1)S(1)} %all-to-all-done.1.refs_13_.refs_8_) | copy-start | bytes 3538948
  62.0 59.2 %collective-permute-start.17 = (bf16[4,2,2,288,128]{4,3,2,1,0:T(8,128)(2,1)S(1)}, bf16[4,2,2,288,128]{4,3,2,1,0:T(8,128)(2,1)}, u32[]{:S(2)}, u32[]{:S(2)}) collective-permute-start(bf16[4,2,2,288,128]{4,3,2,1,0:T(8,128)(2,1)S(1)} %all-to-all-done.1.refs_13_.refs_8_), channel_id=1, source_target_pairs={{0,1},{1,2},{2,3},{3,4},{4,5},{5,6},{6,7},{7,8},{8,9},{9,10},{10,1... | collective-permute-start | bytes 3538952 | tf_op jit(solution)/shard_map/ppermute | solution.py:135
  64.4 60.2 %collective-permute-start.18 = (bf16[4,2,2,288,128]{4,3,2,1,0:T(8,128)(2,1)S(1)}, bf16[4,2,2,288,128]{4,3,2,1,0:T(8,128)(2,1)}, u32[]{:S(2)}, u32[]{:S(2)}) collective-permute-start(bf16[4,2,2,288,128]{4,3,2,1,0:T(8,128)(2,1)S(1)} %all-to-all-done.1.refs_13_.refs_8_), channel_id=1, source_target_pairs={{1,0},{2,1},{3,2},{4,3},{5,4},{6,5},{7,6},{8,7},{9,8},{10,9},{11,1... | collective-permute-start | bytes 3538952 | tf_op jit(solution)/shard_map/ppermute | solution.py:135
  66.2 6.4 %collective-permute-start.5 = (bf16[3,6,32,128]{3,2,1,0:T(8,128)(2,1)}, bf16[3,6,32,128]{3,2,1,0:T(8,128)(2,1)S(1)}, u32[]{:S(2)}, u32[]{:S(2)}) collective-permute-start(bf16[3,6,32,128]{3,2,1,0:T(8,128)(2,1)} %get-tuple-element.33), channel_id=1, source_target_pairs={{0,96},{32,0},{64,32},{96,64},{1,97},{33,1},{65,33},{97,65},{2,98}... | collective-permute-start | bytes 442376 | tf_op jit(solution)/shard_map/ppermute | solution.py:120
  72.6 3.2 %copy-start.3 = (bf16[3,6,32,128]{3,2,1,0:T(8,128)(2,1)}, bf16[3,6,32,128]{3,2,1,0:T(8,128)(2,1)S(1)}, u32[]{:S(2)}) copy-start(bf16[3,6,32,128]{3,2,1,0:T(8,128)(2,1)S(1)} %collective-permute-done.5.refs_7_.refs_3_) | copy-start | bytes 442372
  72.6 1.6 collective-permute-start.6
  74.2 0.7 copy-start.4
  74.2 1.6 collective-permute-start.7
  75.8 0.7 copy-start.5
  76.4 1.4 collective-permute-start.8
  77.8 0.6 copy-start.6
  86.4 38.5 %all-to-all-start.2 = ((bf16[128,16,128]{2,1,0:T(8,128)(2,1)}), bf16[128,16,128]{2,1,0:T(8,128)(2,1)}, u32[]{:S(2)}, u32[]{:S(2)}) async-start(bf16[128,16,128]{2,1,0:T(8,128)(2,1)} %text_attention.1), calls=%async_computation.2 | async-start | bytes 1048576 | tf_op jit(solution)/shard_map/all_to_all | solution.py:131
  97.9 10.7 %collective-permute-start.14 = (bf16[1,2,288,128]{3,2,1,0:T(8,128)(2,1)}, bf16[1,2,288,128]{3,2,1,0:T(8,128)(2,1)S(1)}, u32[]{:S(2)}, u32[]{:S(2)}) collective-permute-start(bf16[1,2,288,128]{3,2,1,0:T(8,128)(2,1)} %get-tuple-element.41), channel_id=1, source_target_pairs={{0,32},{32,64},{64,96},{96,0},{1,33},{33,65},{65,97},{97,1},{2,34}... | collective-permute-start | bytes 442376 | tf_op jit(solution)/shard_map/ppermute | solution.py:120
  108.6 16.0 %copy-start.12 = (bf16[1,2,288,128]{3,2,1,0:T(8,128)(2,1)}, bf16[1,2,288,128]{3,2,1,0:T(8,128)(2,1)S(1)}, u32[]{:S(2)}) copy-start(bf16[1,2,288,128]{3,2,1,0:T(8,128)(2,1)S(1)} %collective-permute-done.14.refs_1_) | copy-start | bytes 442372
  108.6 7.2 %collective-permute-start.15 = (bf16[1,2,288,128]{3,2,1,0:T(8,128)(2,1)}, bf16[1,2,288,128]{3,2,1,0:T(8,128)(2,1)S(1)}, u32[]{:S(2)}, u32[]{:S(2)}) collective-permute-start(bf16[1,2,288,128]{3,2,1,0:T(8,128)(2,1)} %get-tuple-element.42), channel_id=1, source_target_pairs={{0,64},{32,96},{64,0},{96,32},{1,65},{33,97},{65,1},{97,33},{2,66}... | collective-permute-start | bytes 442376 | tf_op jit(solution)/shard_map/ppermute | solution.py:120
  115.8 8.8 %copy-start.13 = (bf16[1,2,288,128]{3,2,1,0:T(8,128)(2,1)}, bf16[1,2,288,128]{3,2,1,0:T(8,128)(2,1)S(1)}, u32[]{:S(2)}) copy-start(bf16[1,2,288,128]{3,2,1,0:T(8,128)(2,1)S(1)} %collective-permute-done.15.refs_2_) | copy-start | bytes 442372
  115.8 5.4 %collective-permute-start.16 = (bf16[1,2,288,128]{3,2,1,0:T(8,128)(2,1)}, bf16[1,2,288,128]{3,2,1,0:T(8,128)(2,1)S(1)}, u32[]{:S(2)}, u32[]{:S(2)}) collective-permute-start(bf16[1,2,288,128]{3,2,1,0:T(8,128)(2,1)} %get-tuple-element.43), channel_id=1, source_target_pairs={{0,96},{32,0},{64,32},{96,64},{1,97},{33,1},{65,33},{97,65},{2,98}... | collective-permute-start | bytes 442376 | tf_op jit(solution)/shard_map/ppermute | solution.py:120
  121.2 3.5 %copy-start.14 = (bf16[1,2,288,128]{3,2,1,0:T(8,128)(2,1)}, bf16[1,2,288,128]{3,2,1,0:T(8,128)(2,1)S(1)}, u32[]{:S(2)}) copy-start(bf16[1,2,288,128]{3,2,1,0:T(8,128)(2,1)S(1)} %collective-permute-done.16.refs_3_) | copy-start | bytes 442372
  121.2 29.0 %collective-permute-start = (bf16[1,4,288,128]{3,2,1,0:T(8,128)(2,1)}, bf16[1,4,288,128]{3,2,1,0:T(8,128)(2,1)}, u32[]{:S(2)}, u32[]{:S(2)}) collective-permute-start(bf16[1,4,288,128]{3,2,1,0:T(8,128)(2,1)} %get-tuple-element.27), channel_id=1, source_target_pairs={{0,32},{32,64},{64,96},{96,0},{1,33},{33,65},{65,97},{97,1},{2,34}... | collective-permute-start | bytes 884744 | tf_op jit(solution)/shard_map/ppermute | solution.py:120
  121.2 30.0 %collective-permute-start.1 = (bf16[1,4,288,128]{3,2,1,0:T(8,128)(2,1)}, bf16[1,4,288,128]{3,2,1,0:T(8,128)(2,1)}, u32[]{:S(2)}, u32[]{:S(2)}) collective-permute-start(bf16[1,4,288,128]{3,2,1,0:T(8,128)(2,1)} %get-tuple-element.28), channel_id=1, source_target_pairs={{0,64},{32,96},{64,0},{96,32},{1,65},{33,97},{65,1},{97,33},{2,66}... | collective-permute-start | bytes 884744 | tf_op jit(solution)/shard_map/ppermute | solution.py:120
  124.7 26.6 %collective-permute-start.2 = (bf16[1,4,288,128]{3,2,1,0:T(8,128)(2,1)}, bf16[1,4,288,128]{3,2,1,0:T(8,128)(2,1)S(1)}, u32[]{:S(2)}, u32[]{:S(2)}) collective-permute-start(bf16[1,4,288,128]{3,2,1,0:T(8,128)(2,1)} %get-tuple-element.29), channel_id=1, source_target_pairs={{0,96},{32,0},{64,32},{96,64},{1,97},{33,1},{65,33},{97,65},{2,98}... | collective-permute-start | bytes 884744 | tf_op jit(solution)/shard_map/ppermute | solution.py:120
  127.9 68.9 %all-to-all-start.3 = ((bf16[128,16,128]{2,1,0:T(8,128)(2,1)}), bf16[128,16,128]{2,1,0:T(8,128)(2,1)S(1)}, u32[]{:S(2)}, u32[]{:S(2)}) async-start(bf16[128,16,128]{2,1,0:T(8,128)(2,1)} %bitcast.1), calls=%async_computation.3 | async-start | bytes 1048576 | tf_op jit(solution)/shard_map/all_to_all | solution.py:131
  150.2 29.4 %collective-permute-start.19 = (bf16[2,288,128]{2,1,0:T(8,128)(2,1)}, bf16[2,288,128]{2,1,0:T(8,128)(2,1)S(1)}, u32[]{:S(2)}, u32[]{:S(2)}) collective-permute-start(bf16[2,288,128]{2,1,0:T(8,128)(2,1)} %get-tuple-element.45), channel_id=1, source_target_pairs={{0,32},{32,64},{64,96},{96,0},{1,33},{33,65},{65,97},{97,1},{2,34}... | collective-permute-start | bytes 442376 | tf_op jit(solution)/shard_map/ppermute | solution.py:120
  151.2 0.7 copy-start.10
  151.9 26.8 %copy-start.18 = (bf16[2,288,128]{2,1,0:T(8,128)(2,1)S(1)}, bf16[2,288,128]{2,1,0:T(8,128)(2,1)}, u32[]{:S(2)}) copy-start(bf16[2,288,128]{2,1,0:T(8,128)(2,1)} %get-tuple-element.46) | copy-start | bytes 442372
  151.9 27.6 %copy-start.17 = (bf16[2,288,128]{2,1,0:T(8,128)(2,1)S(1)}, bf16[2,288,128]{2,1,0:T(8,128)(2,1)}, u32[]{:S(2)}) copy-start(bf16[2,288,128]{2,1,0:T(8,128)(2,1)} %get-tuple-element.47) | copy-start | bytes 442372
  173.3 28.0 %collective-permute-start.11 = (bf16[4,288,128]{2,1,0:T(8,128)(2,1)}, bf16[4,288,128]{2,1,0:T(8,128)(2,1)S(1)}, u32[]{:S(2)}, u32[]{:S(2)}) collective-permute-start(bf16[4,288,128]{2,1,0:T(8,128)(2,1)} %get-tuple-element.37), channel_id=1, source_target_pairs={{0,32},{32,64},{64,96},{96,0},{1,33},{33,65},{65,97},{97,1},{2,34}... | collective-permute-start | bytes 884744 | tf_op jit(solution)/shard_map/ppermute | solution.py:120
  174.8 26.5 %collective-permute-start.12 = (bf16[4,288,128]{2,1,0:T(8,128)(2,1)}, bf16[4,288,128]{2,1,0:T(8,128)(2,1)S(1)}, u32[]{:S(2)}, u32[]{:S(2)}) collective-permute-start(bf16[4,288,128]{2,1,0:T(8,128)(2,1)} %get-tuple-element.38), channel_id=1, source_target_pairs={{0,64},{32,96},{64,0},{96,32},{1,65},{33,97},{65,1},{97,33},{2,66}... | collective-permute-start | bytes 884744 | tf_op jit(solution)/shard_map/ppermute | solution.py:120
  177.1 24.3 %collective-permute-start.13 = (bf16[4,288,128]{2,1,0:T(8,128)(2,1)}, bf16[4,288,128]{2,1,0:T(8,128)(2,1)S(1)}, u32[]{:S(2)}, u32[]{:S(2)}) collective-permute-start(bf16[4,288,128]{2,1,0:T(8,128)(2,1)} %get-tuple-element.39), channel_id=1, source_target_pairs={{0,96},{32,0},{64,32},{96,64},{1,97},{33,1},{65,33},{97,65},{2,98}... | collective-permute-start | bytes 884744 | tf_op jit(solution)/shard_map/ppermute | solution.py:120
  178.7 14.3 %collective-permute-start.20 = (bf16[2,288,128]{2,1,0:T(8,128)(2,1)S(1)}, bf16[2,288,128]{2,1,0:T(8,128)(2,1)S(1)}, u32[]{:S(2)}, u32[]{:S(2)}) collective-permute-start(bf16[2,288,128]{2,1,0:T(8,128)(2,1)S(1)} %copy-done.18), channel_id=1, source_target_pairs={{0,64},{32,96},{64,0},{96,32},{1,65},{33,97},{65,1},{97,33},{2,66}... | collective-permute-start | bytes 442376 | tf_op jit(solution)/shard_map/ppermute | solution.py:120
  179.5 17.3 %copy-start.11 = (bf16[2,288,128]{2,1,0:T(8,128)(2,1)}, bf16[2,288,128]{2,1,0:T(8,128)(2,1)S(1)}, u32[]{:S(2)}) copy-start(bf16[2,288,128]{2,1,0:T(8,128)(2,1)S(1)} %collective-permute-done.19.refs_1_) | copy-start | bytes 442372
  179.5 17.3 %collective-permute-start.21 = (bf16[2,288,128]{2,1,0:T(8,128)(2,1)S(1)}, bf16[2,288,128]{2,1,0:T(8,128)(2,1)S(1)}, u32[]{:S(2)}, u32[]{:S(2)}) collective-permute-start(bf16[2,288,128]{2,1,0:T(8,128)(2,1)S(1)} %copy-done.17), channel_id=1, source_target_pairs={{0,96},{32,0},{64,32},{96,64},{1,97},{33,1},{65,33},{97,65},{2,98}... | collective-permute-start | bytes 442376 | tf_op jit(solution)/shard_map/ppermute | solution.py:120
  192.9 3.9 %copy-start.15 = (bf16[2,288,128]{2,1,0:T(8,128)(2,1)}, bf16[2,288,128]{2,1,0:T(8,128)(2,1)S(1)}, u32[]{:S(2)}) copy-start(bf16[2,288,128]{2,1,0:T(8,128)(2,1)S(1)} %collective-permute-done.20.refs_2_) | copy-start | bytes 442372
  196.8 0.7 copy-start.16
  196.8 0.8 copy-start.2
  201.3 0.7 copy-start.7
  201.4 0.8 copy-start.8
  201.4 0.9 copy-start.9

commit v3 on v2

--- a/solution.py
+++ b/solution.py
@@ -24,7 +24,7 @@
 RB = 128
 KEYS = 2 * SLICE + TXT
 SCALE = math.log2(math.e) / math.sqrt(D)
-CHUNKS = ((0, 2), (2, 4))
+CHUNKS = ((0, 4), (4, 2))
 BF = jnp.bfloat16
 F32 = jnp.float32
 
@@ -306,7 +306,8 @@
                 rows = pl.ds(2 * SLICE + n * HALF, HALF)
                 pairs.append((piece.at[1 + a, pl.ds(first + start, count)], sc.at[some, rows]))
             parts.append(pairs)
-        queries = [(q_refs[d].at[0, some], q_sc.at[some, rows_of(place(-d), ROWS)]) for d in range(GROUP)]
+        asked = pl.ds(first + start, count)
+        queries = [(q_refs[d].at[0, asked], q_sc.at[some, rows_of(place(-d), ROWS)]) for d in range(GROUP)]
         pairs = queries + parts[0] + parts[1]
         return copy_list(pairs, sems.at[slot]), len(queries + parts[0])
 
@@ -454,13 +455,12 @@
     video, words = (video_q, video_k, video_v), (text_q, text_k, text_v)
     (f0, n0), (f1, n1) = CHUNKS
     (kv0,) = pack(video, [((1, 2), f0, n0, ROWS, True)])
-    q0, text, kv1, q1 = pack(
+    text, kv1, q = pack(
         video + words,
         [
-            ((0,), f0, n0, ROWS, False),
             ((3, 4, 5), 0, HD, HALF, False),
             ((1, 2), f1, n1, ROWS, True),
-            ((0,), f1, n1, ROWS, False),
+            ((0,), 0, HD, ROWS, False),
         ],
     )
     own, before, after = [], [], []
@@ -473,14 +473,14 @@
     for d in range(1, GROUP):
         other.append(lax.ppermute(mine[d], "blk", [(i, i ^ 1) for i in range(BLK)]))
     text = mine + other
-    q = [exchange(q0), exchange(q1)]
+    q = exchange(q)
     slots = text_attention(text_len, text, own)
     slots = swap(slots, ("blk", "uly"))
     slots = combine(slots)
     slots = swap(slots, ("blk", "uly"))
     back = []
     for c, (first, heads) in enumerate(CHUNKS):
-        o = video_attention(first, heads, window_tiles, text_len, q[c], text, before[c], own[c], after[c])
+        o = video_attention(first, heads, window_tiles, text_len, q, text, before[c], own[c], after[c])
         back.append(exchange(o))
     rows, text_out = first_rows(back[0], slots, f0, n0)
     return later_rows(back[1], rows, f1, n1), text_out

time: 206 us -> 184 us (0.89)
  waiting for transfers between devices: 79.4 us -> 37 us
  blocking collectives: 0 us -> 33.6 us
  starting transfers between devices: 58.7 us -> 49.4 us
  local copies, waits for them, and re-layouts: 4.1 us -> 1.5 us
    all_to_all x0 -> x1, blocking collectives: none -> 33.6 us  [swap(): return lax.all_to_all(array, axes, 0, 0, tiled=True)]
    all_to_all x4 -> x3, waiting for transfers between devices: 34.6 us -> 10.6 us  [swap(): return lax.all_to_all(array, axes, 0, 0, tiled=True)]
    ppermute x15 -> x12, waiting for transfers between devices: 42.3 us -> 25.5 us  [around(): lax.ppermute(block, 'uly', [(i, (i + distance) % GROUP) for i in range(GR...]
    all_to_all x4 -> x3, starting transfers between devices: 29.3 us -> 20.8 us  [swap(): return lax.all_to_all(array, axes, 0, 0, tiled=True)]
    ppermute x15 -> x12, starting transfers between devices: 20.8 us -> 17 us  [around(): lax.ppermute(block, 'uly', [(i, (i + distance) % GROUP) for i in range(GR...]
    ppermute x4, starting transfers between devices: 7.68 us -> 11.1 us  [beside(): lax.ppermute(block, 'blk', [(i, i + distance) for i in range(BLK) if 0 <=...]
    unnamed x38 -> x26, local copies, waits for them, and re-layouts: 4.1 us -> 1.5 us
  transfers between devices with their start and end apart: 26 -> 22, of which waited for: 12 -> 7; matrix products, arithmetic and copies ran while one was open for 0% -> 0% of each run, Pallas kernels for 25% -> 29%
where the time goes in v3:
time: 184 us
  Pallas kernels  60.3 us (33%)
  starting transfers between devices  49.4 us (27%)
  waiting for transfers between devices  37 us (20%)
  blocking collectives  33.6 us (18%)
    pallas_call x2, Pallas kernels, video_attention(): pl.pallas_call(functools.partial(video_body, first, heads), in_specs=[SME...  33.7 us
    all_to_all x1, blocking collectives, swap(): return lax.all_to_all(array, axes, 0, 0, tiled=True)  33.6 us
    ppermute x12, waiting for transfers between devices, around(): lax.ppermute(block, 'uly', [(i, (i + distance) % GROUP) for i in range(GR...  25.5 us
    all_to_all x3, starting transfers between devices, swap(): return lax.all_to_all(array, axes, 0, 0, tiled=True)  20.8 us
    ppermute x12, starting transfers between devices, around(): lax.ppermute(block, 'uly', [(i, (i + distance) % GROUP) for i in range(GR...  17 us
    ppermute x4, starting transfers between devices, beside(): lax.ppermute(block, 'blk', [(i, i + distance) for i in range(BLK) if 0 <=...  11.1 us
    all_to_all x3, waiting for transfers between devices, swap(): return lax.all_to_all(array, axes, 0, 0, tiled=True)  10.6 us
    pallas_call x2, Pallas kernels, pack(): pl.pallas_call(body, in_specs=[HBM] * len(arrays), out_specs=[HBM] * len(...  9.88 us
  transfers between devices with their start and end apart: 22, of which 7 were waited for; matrix products, arithmetic and copies ran while one was open for 0% of the time, Pallas kernels for 29%

profile of v3, /device:TPU:0, one launch (start us, length us, event | category | flops | bytes accessed | tf_op | source)
XLA Modules:
  0.0 183.5 jit_solution(15837758771186702973)
XLA Ops:
  0.6 4.3 %shard_map.96 = bf16[4,2,4,288,128]{4,3,2,1,0:T(8,128)(2,1)} custom-call(bf16[288,3072]{1,0:T(8,128)(2,1)} %refs_0_.3, bf16[288,3072]{1,0:T(8,128)(2,1)} %refs_1_.3, bf16[288,3072]{1,0:T(8,128)(2,1)} %refs_2_.3), custom_call_target="tpu_custom_call" | custom-call | tf_op jit(solution)/shard_map/pallas_call | solution.py:103
  5.0 33.6 %all_to_all.20.refs_13_.refs_8_ = bf16[4,2,4,288,128]{4,3,2,1,0:T(8,128)(2,1)S(1)} all-to-all(bf16[4,2,4,288,128]{4,3,2,1,0:T(8,128)(2,1)} %shard_map.96), channel_id=1, replica_groups=mesh['uly'=4,'blk'=32] {'uly'}, dimensions={0} | all-to-all | bytes 4718592 | tf_op jit(solution)/shard_map/all_to_all | solution.py:131
  38.5 1.3 collective-permute-start.15
  39.8 4.5 %collective-permute-start.14 = (bf16[4,2,4,288,128]{4,3,2,1,0:T(8,128)(2,1)S(1)}, bf16[4,2,4,288,128]{4,3,2,1,0:T(8,128)(2,1)}, u32[]{:S(2)}, u32[]{:S(2)}) collective-permute-start(bf16[4,2,4,288,128]{4,3,2,1,0:T(8,128)(2,1)S(1)} %all_to_all.20.refs_13_.refs_8_), channel_id=1, source_target_pairs={{0,1},{1,2},{2,3},{3,4},{4,5},{5,6},{6,7},{7,8},{8,9},{9,10},{10,1... | collective-permute-start | bytes 7077896 | tf_op jit(solution)/shard_map/ppermute | solution.py:135
  44.3 5.6 %shard_map.95 = (bf16[3,6,32,128]{3,2,1,0:T(8,128)(2,1)}, bf16[3,6,32,128]{3,2,1,0:T(8,128)(2,1)}, bf16[3,6,32,128]{3,2,1,0:T(8,128)(2,1)}, bf16[3,6,32,128]{3,2...) custom-call(bf16[288,3072]{1,0:T(8,128)(2,1)} %refs_0_.3, ...), custom_call_target="tpu_custom_call" | custom-call | tf_op jit(solution)/shard_map/pallas_call | solution.py:103
  49.8 0.0 copy-done
  49.8 3.5 %all-to-all-start = ((bf16[4,2,2,288,128]{4,3,2,1,0:T(8,128)(2,1)}), bf16[4,2,2,288,128]{4,3,2,1,0:T(8,128)(2,1)S(1)}, u32[]{:S(2)}, u32[]{:S(2)}) async-start(bf16[4,2,2,288,128]{4,3,2,1,0:T(8,128)(2,1)} %get-tuple-element.31), calls=%async_computation | async-start | bytes 2359296 | tf_op jit(solution)/shard_map/all_to_all | solution.py:131
  53.4 2.0 %collective-permute-start.3 = (bf16[3,6,32,128]{3,2,1,0:T(8,128)(2,1)}, bf16[3,6,32,128]{3,2,1,0:T(8,128)(2,1)S(1)}, u32[]{:S(2)}, u32[]{:S(2)}) collective-permute-start(bf16[3,6,32,128]{3,2,1,0:T(8,128)(2,1)} %get-tuple-element.27), channel_id=1, source_target_pairs={{0,32},{32,64},{64,96},{96,0},{1,33},{33,65},{65,97},{97,1},{2,34}... | collective-permute-start | bytes 442376 | tf_op jit(solution)/shard_map/ppermute | solution.py:120
  55.4 2.7 %collective-permute-start.4 = (bf16[3,6,32,128]{3,2,1,0:T(8,128)(2,1)}, bf16[3,6,32,128]{3,2,1,0:T(8,128)(2,1)S(1)}, u32[]{:S(2)}, u32[]{:S(2)}) collective-permute-start(bf16[3,6,32,128]{3,2,1,0:T(8,128)(2,1)} %get-tuple-element.28), channel_id=1, source_target_pairs={{0,64},{32,96},{64,0},{96,32},{1,65},{33,97},{65,1},{97,33},{2,66}... | collective-permute-start | bytes 442376 | tf_op jit(solution)/shard_map/ppermute | solution.py:120
  58.1 0.0 collective-permute-start
  58.1 18.9 %collective-permute-done.3.refs_5_.refs_1_ = bf16[3,6,32,128]{3,2,1,0:T(8,128)(2,1)S(1)} collective-permute-done((bf16[3,6,32,128]{3,2,1,0:T(8,128)(2,1)}, bf16[3,6,32,128]{3,2,1,0:T(8,128)(2,1)S(1)}, u32[]{:S(2)}, u32[]{:S(2)}) %collective-permute-start.3) | collective-permute-done | bytes 147488 | tf_op jit(solution)/shard_map/ppermute | solution.py:120
  77.0 0.0 collective-permute-start.5
  77.0 0.7 collective-permute-done.4.refs_6_.refs_2_
  77.6 0.0 collective-permute-start.6
  77.6 4.7 %collective-permute-done.5.refs_7_.refs_3_ = bf16[3,6,32,128]{3,2,1,0:T(8,128)(2,1)S(1)} collective-permute-done((bf16[3,6,32,128]{3,2,1,0:T(8,128)(2,1)}, bf16[3,6,32,128]{3,2,1,0:T(8,128)(2,1)S(1)}, u32[]{:S(2)}, u32[]{:S(2)}) %collective-permute-start.5) | collective-permute-done | bytes 147488 | tf_op jit(solution)/shard_map/ppermute | solution.py:120
  82.3 0.0 collective-permute-start.7
  82.3 0.0 collective-permute-done.6.refs_9_.refs_5_
  82.3 0.0 copy-start.5
  82.3 0.5 collective-permute-start.8
  82.8 0.9 collective-permute-done.7.refs_10_.refs_6_
  83.7 1.2 collective-permute-start.1
  84.9 0.0 copy-done.2
  84.9 0.0 collective-permute-done.8.refs_11_.refs_7_
  84.9 0.0 all-to-all-done.refs_13_.refs_9_
  84.9 0.0 copy-start.1
  84.9 1.3 collective-permute-start.10
  86.2 0.0 collective-permute-done.refs_1_
  86.3 4.1 %collective-permute-start.9 = (bf16[4,2,2,288,128]{4,3,2,1,0:T(8,128)(2,1)S(1)}, bf16[4,2,2,288,128]{4,3,2,1,0:T(8,128)(2,1)}, u32[]{:S(2)}, u32[]{:S(2)}) collective-permute-start(bf16[4,2,2,288,128]{4,3,2,1,0:T(8,128)(2,1)S(1)} %all-to-all-done.refs_13_.refs_9_), channel_id=1, source_target_pairs={{0,1},{1,2},{2,3},{3,4},{4,5},{5,6},{6,7},{7,8},{8,9},{9,10},{10,1... | collective-permute-start | bytes 3538952 | tf_op jit(solution)/shard_map/ppermute | solution.py:135
  91.0 7.9 %text_attention.1 = bf16[128,16,128]{2,1,0:T(8,128)(2,1)} custom-call(s32[1]{0:T(128)S(6)} %copy.12.length, bf16[3,6,32,128]{3,2,1,0:T(8,128)(2,1)} %get-tuple-element.26.refs_4_.refs_0_, bf16[3,6,32,128]{3,2,1,0:T(8,128)(2,1)} %copy-done.2, bf16[3,6,32,128]{3,2,1,0:T(8,128)(2,1)} %copy-done.3, bf16[3,6,32,128]{3,2,1,0:T(8,128)(2,1)} %copy-done.4, ...), custom_call_target="tpu_custom_call" | custom-call | tf_op jit(solution)/shard_map/text_attention/pallas_call | solution.py:224
  98.9 11.3 %all-to-all-start.2 = ((bf16[128,16,128]{2,1,0:T(8,128)(2,1)}), bf16[128,16,128]{2,1,0:T(8,128)(2,1)}, u32[]{:S(2)}, u32[]{:S(2)}) async-start(bf16[128,16,128]{2,1,0:T(8,128)(2,1)} %text_attention.1), calls=%async_computation.2 | async-start | bytes 1048576 | tf_op jit(solution)/shard_map/all_to_all | solution.py:131
  110.2 0.0 collective-permute-done.1.refs_2_
  110.2 2.2 %collective-permute-start.2 = (bf16[1,6,288,128]{3,2,1,0:T(8,128)(2,1)}, bf16[1,6,288,128]{3,2,1,0:T(8,128)(2,1)}, u32[]{:S(2)}, u32[]{:S(2)}) collective-permute-start(bf16[1,6,288,128]{3,2,1,0:T(8,128)(2,1)} %get-tuple-element.25), channel_id=1, source_target_pairs={{0,96},{32,0},{64,32},{96,64},{1,97},{33,1},{65,33},{97,65},{2,98}... | collective-permute-start | bytes 1327112 | tf_op jit(solution)/shard_map/ppermute | solution.py:120
  112.4 10.6 %all-to-all-done.2.in_ref = bf16[128,16,128]{2,1,0:T(8,128)(2,1)} async-done(((bf16[128,16,128]{2,1,0:T(8,128)(2,1)}), bf16[128,16,128]{2,1,0:T(8,128)(2,1)}, u32[]{:S(2)}, u32[]{:S(2)}) %all-to-all-start.2) | async-done | bytes 524320 | tf_op jit(solution)/shard_map/all_to_all | solution.py:131
  123.0 3.0 %combine.1 = bf16[32,4,16,128]{3,2,1,0:T(8,128)(2,1)} custom-call(bf16[128,16,128]{2,1,0:T(8,128)(2,1)} %all-to-all-done.2.in_ref), custom_call_target="tpu_custom_call" | custom-call | tf_op jit(solution)/shard_map/combine/pallas_call | solution.py:276
  126.0 5.9 %all-to-all-start.3 = ((bf16[128,16,128]{2,1,0:T(8,128)(2,1)}), bf16[128,16,128]{2,1,0:T(8,128)(2,1)}, u32[]{:S(2)}, u32[]{:S(2)}) async-start(bf16[128,16,128]{2,1,0:T(8,128)(2,1)} %bitcast.1), calls=%async_computation.3 | async-start | bytes 1048576 | tf_op jit(solution)/shard_map/all_to_all | solution.py:131
  132.0 0.0 collective-permute-done.2.refs_3_
  132.0 0.0 collective-permute-done.15.refs_14_
  132.0 0.0 collective-permute-done.14.refs_12_
  132.0 21.2 %video_attention.3 = (bf16[4,288,128]{2,1,0:T(8,128)(2,1)}, bf16[4,288,128]{2,1,0:T(8,128)(2,1)}, bf16[4,288,128]{2,1,0:T(8,128)(2,1)}, bf16[4,288,128]{2,1,0:T(8,128)(2,1)}) custom-call(s32[3,6]{1,0:T(4,128)} %tiles.3, s32[1]{0:T(128)S(6)} %copy.12.length, bf16[1,6,288,128]{3,2,1,0:T(8,128)(2,1)} %get-tuple-element.22.refs_0_, ...), custom_call_target="tpu_custom_call" | custom-call | tf_op jit(solution)/shard_map/video_attention/pallas_call | solution.py:367
  153.2 0.7 collective-permute-start.16
  153.9 2.7 %collective-permute-start.17 = (bf16[4,288,128]{2,1,0:T(8,128)(2,1)}, bf16[4,288,128]{2,1,0:T(8,128)(2,1)S(1)}, u32[]{:S(2)}, u32[]{:S(2)}) collective-permute-start(bf16[4,288,128]{2,1,0:T(8,128)(2,1)} %get-tuple-element.38), channel_id=1, source_target_pairs={{0,64},{32,96},{64,0},{96,32},{1,65},{33,97},{65,1},{97,33},{2,66}... | collective-permute-start | bytes 884744 | tf_op jit(solution)/shard_map/ppermute | solution.py:120
  156.6 1.4 collective-permute-start.18
  158.0 0.0 collective-permute-done.10.refs_14_
  158.0 0.0 collective-permute-done.9.refs_12_
  158.0 12.4 %video_attention.2 = (bf16[2,288,128]{2,1,0:T(8,128)(2,1)}, bf16[2,288,128]{2,1,0:T(8,128)(2,1)}, bf16[2,288,128]{2,1,0:T(8,128)(2,1)}, bf16[2,288,128]{2,1,0:T(8,128)(2,1)}) custom-call(s32[3,6]{1,0:T(4,128)} %tiles.3, s32[1]{0:T(128)S(6)} %copy.12.length, bf16[1,6,288,128]{3,2,1,0:T(8,128)(2,1)} %get-tuple-element.22.refs_0_, ...), custom_call_target="tpu_custom_call" | custom-call | tf_op jit(solution)/shard_map/video_attention/pallas_call | solution.py:367
  170.5 0.6 collective-permute-start.11
  171.1 0.9 collective-permute-start.12
  172.1 0.0 collective-permute-done.16.refs_1_
  172.1 2.5 %collective-permute-start.13 = (bf16[2,288,128]{2,1,0:T(8,128)(2,1)}, bf16[2,288,128]{2,1,0:T(8,128)(2,1)S(1)}, u32[]{:S(2)}, u32[]{:S(2)}) collective-permute-start(bf16[2,288,128]{2,1,0:T(8,128)(2,1)} %get-tuple-element.35), channel_id=1, source_target_pairs={{0,96},{32,0},{64,32},{96,64},{1,97},{33,1},{65,33},{97,65},{2,98}... | collective-permute-start | bytes 442376 | tf_op jit(solution)/shard_map/ppermute | solution.py:120
  174.6 0.0 all-to-all-done.3.refs_4_
  174.6 0.0 collective-permute-done.17.refs_2_
  174.6 0.0 collective-permute-done.18.refs_3_
  174.6 0.0 copy-start.9
  174.6 0.0 copy-done.7
  174.6 0.7 copy-done.8
  175.3 0.1 copy-done.9
  175.4 4.0 %first_rows.1 = (bf16[288,3072]{1,0:T(8,128)(2,1)}, bf16[64,3072]{1,0:T(8,128)(2,1)}) custom-call(bf16[4,288,128]{2,1,0:T(8,128)(2,1)} %get-tuple-element.36.refs_0_, bf16[4,288,128]{2,1,0:T(8,128)(2,1)} %copy-done.7, bf16[4,288,128]{2,1,0:T(8,128)(2,1)} %copy-done.8, bf16[4,288,128]{2,1,0:T(8,128)(2,1)} %copy-done.9, ...), custom_call_target="tpu_custom_call" | custom-call | tf_op jit(solution)/shard_map/first_rows/pallas_call | solution.py:420
  179.5 0.7 collective-permute-done.11.refs_1_
  180.2 0.0 collective-permute-done.12.refs_2_
  180.2 0.6 collective-permute-done.13.refs_3_
  180.8 0.0 copy-done.10
  180.8 0.1 copy-done.11
  180.9 0.6 copy-done.12
  181.4 1.9 %later_rows.1 = bf16[288,3072]{1,0:T(8,128)(2,1)} custom-call(bf16[2,288,128]{2,1,0:T(8,128)(2,1)} %get-tuple-element.32.refs_0_, bf16[2,288,128]{2,1,0:T(8,128)(2,1)} %copy-done.10, bf16[2,288,128]{2,1,0:T(8,128)(2,1)} %copy-done.11, bf16[2,288,128]{2,1,0:T(8,128)(2,1)} %copy-done.12, ...), custom_call_target="tpu_custom_call", output_to_operand_aliasing={{}: (4, {})} | custom-call | tf_op jit(solution)/shard_map/later_rows/pallas_call | solution.py:439
  (15 shorter events, 0.0 us)
Async XLA Ops:
  38.5 11.3 %copy-start = (bf16[4,2,4,288,128]{4,3,2,1,0:T(8,128)(2,1)}, bf16[4,2,4,288,128]{4,3,2,1,0:T(8,128)(2,1)S(1)}, u32[]{:S(2)}) copy-start(bf16[4,2,4,288,128]{4,3,2,1,0:T(8,128)(2,1)S(1)} %all_to_all.20.refs_13_.refs_8_) | copy-start | bytes 7077892
  38.5 93.5 %collective-permute-start.15 = (bf16[4,2,4,288,128]{4,3,2,1,0:T(8,128)(2,1)S(1)}, bf16[4,2,4,288,128]{4,3,2,1,0:T(8,128)(2,1)}, u32[]{:S(2)}, u32[]{:S(2)}) collective-permute-start(bf16[4,2,4,288,128]{4,3,2,1,0:T(8,128)(2,1)S(1)} %all_to_all.20.refs_13_.refs_8_), channel_id=1, source_target_pairs={{1,0},{2,1},{3,2},{4,3},{5,4},{6,5},{7,6},{8,7},{9,8},{10,9},{11,1... | collective-permute-start | bytes 7077896 | tf_op jit(solution)/shard_map/ppermute | solution.py:135
  39.8 92.2 %collective-permute-start.14 = (bf16[4,2,4,288,128]{4,3,2,1,0:T(8,128)(2,1)S(1)}, bf16[4,2,4,288,128]{4,3,2,1,0:T(8,128)(2,1)}, u32[]{:S(2)}, u32[]{:S(2)}) collective-permute-start(bf16[4,2,4,288,128]{4,3,2,1,0:T(8,128)(2,1)S(1)} %all_to_all.20.refs_13_.refs_8_), channel_id=1, source_target_pairs={{0,1},{1,2},{2,3},{3,4},{4,5},{5,6},{6,7},{7,8},{8,9},{9,10},{10,1... | collective-permute-start | bytes 7077896 | tf_op jit(solution)/shard_map/ppermute | solution.py:135
  49.8 35.1 %all-to-all-start = ((bf16[4,2,2,288,128]{4,3,2,1,0:T(8,128)(2,1)}), bf16[4,2,2,288,128]{4,3,2,1,0:T(8,128)(2,1)S(1)}, u32[]{:S(2)}, u32[]{:S(2)}) async-start(bf16[4,2,2,288,128]{4,3,2,1,0:T(8,128)(2,1)} %get-tuple-element.31), calls=%async_computation | async-start | bytes 2359296 | tf_op jit(solution)/shard_map/all_to_all | solution.py:131
  53.4 23.6 %collective-permute-start.3 = (bf16[3,6,32,128]{3,2,1,0:T(8,128)(2,1)}, bf16[3,6,32,128]{3,2,1,0:T(8,128)(2,1)S(1)}, u32[]{:S(2)}, u32[]{:S(2)}) collective-permute-start(bf16[3,6,32,128]{3,2,1,0:T(8,128)(2,1)} %get-tuple-element.27), channel_id=1, source_target_pairs={{0,32},{32,64},{64,96},{96,0},{1,33},{33,65},{65,97},{97,1},{2,34}... | collective-permute-start | bytes 442376 | tf_op jit(solution)/shard_map/ppermute | solution.py:120
  55.4 22.3 %collective-permute-start.4 = (bf16[3,6,32,128]{3,2,1,0:T(8,128)(2,1)}, bf16[3,6,32,128]{3,2,1,0:T(8,128)(2,1)S(1)}, u32[]{:S(2)}, u32[]{:S(2)}) collective-permute-start(bf16[3,6,32,128]{3,2,1,0:T(8,128)(2,1)} %get-tuple-element.28), channel_id=1, source_target_pairs={{0,64},{32,96},{64,0},{96,32},{1,65},{33,97},{65,1},{97,33},{2,66}... | collective-permute-start | bytes 442376 | tf_op jit(solution)/shard_map/ppermute | solution.py:120
  58.1 28.2 %collective-permute-start = (bf16[1,6,288,128]{3,2,1,0:T(8,128)(2,1)}, bf16[1,6,288,128]{3,2,1,0:T(8,128)(2,1)}, u32[]{:S(2)}, u32[]{:S(2)}) collective-permute-start(bf16[1,6,288,128]{3,2,1,0:T(8,128)(2,1)} %get-tuple-element.23), channel_id=1, source_target_pairs={{0,32},{32,64},{64,96},{96,0},{1,33},{33,65},{65,97},{97,1},{2,34}... | collective-permute-start | bytes 1327112 | tf_op jit(solution)/shard_map/ppermute | solution.py:120
  77.0 7.9 %copy-start.2 = (bf16[3,6,32,128]{3,2,1,0:T(8,128)(2,1)}, bf16[3,6,32,128]{3,2,1,0:T(8,128)(2,1)S(1)}, u32[]{:S(2)}) copy-start(bf16[3,6,32,128]{3,2,1,0:T(8,128)(2,1)S(1)} %collective-permute-done.3.refs_5_.refs_1_) | copy-start | bytes 442372
  77.0 5.4 %collective-permute-start.5 = (bf16[3,6,32,128]{3,2,1,0:T(8,128)(2,1)}, bf16[3,6,32,128]{3,2,1,0:T(8,128)(2,1)S(1)}, u32[]{:S(2)}, u32[]{:S(2)}) collective-permute-start(bf16[3,6,32,128]{3,2,1,0:T(8,128)(2,1)} %get-tuple-element.29), channel_id=1, source_target_pairs={{0,96},{32,0},{64,32},{96,64},{1,97},{33,1},{65,33},{97,65},{2,98}... | collective-permute-start | bytes 442376 | tf_op jit(solution)/shard_map/ppermute | solution.py:120
  77.6 7.2 %copy-start.3 = (bf16[3,6,32,128]{3,2,1,0:T(8,128)(2,1)}, bf16[3,6,32,128]{3,2,1,0:T(8,128)(2,1)S(1)}, u32[]{:S(2)}) copy-start(bf16[3,6,32,128]{3,2,1,0:T(8,128)(2,1)S(1)} %collective-permute-done.4.refs_6_.refs_2_) | copy-start | bytes 442372
  77.6 4.7 %collective-permute-start.6 = (bf16[3,6,32,128]{3,2,1,0:T(8,128)(2,1)S(1)}, bf16[3,6,32,128]{3,2,1,0:T(8,128)(2,1)S(1)}, u32[]{:S(2)}, u32[]{:S(2)}) collective-permute-start(bf16[3,6,32,128]{3,2,1,0:T(8,128)(2,1)S(1)} %collective-permute-done.3.refs_5_.refs_1_), channel_id=1, source_target_pairs={{0,1},{1,0},{2,3},{3,2},{4,5},{5,4},{6,7},{7,6},{8,9},{9,8},{10,11... | collective-permute-start | bytes 442376 | tf_op jit(solution)/shard_map/ppermute | solution.py:474
  82.3 2.6 %copy-start.4 = (bf16[3,6,32,128]{3,2,1,0:T(8,128)(2,1)}, bf16[3,6,32,128]{3,2,1,0:T(8,128)(2,1)S(1)}, u32[]{:S(2)}) copy-start(bf16[3,6,32,128]{3,2,1,0:T(8,128)(2,1)S(1)} %collective-permute-done.5.refs_7_.refs_3_) | copy-start | bytes 442372
  82.3 1.4 collective-permute-start.7
  82.3 2.6 %copy-start.5 = (bf16[3,6,32,128]{3,2,1,0:T(8,128)(2,1)}, bf16[3,6,32,128]{3,2,1,0:T(8,128)(2,1)S(1)}, u32[]{:S(2)}) copy-start(bf16[3,6,32,128]{3,2,1,0:T(8,128)(2,1)S(1)} %collective-permute-done.6.refs_9_.refs_5_) | copy-start | bytes 442372
  82.3 2.6 %collective-permute-start.8 = (bf16[3,6,32,128]{3,2,1,0:T(8,128)(2,1)S(1)}, bf16[3,6,32,128]{3,2,1,0:T(8,128)(2,1)}, u32[]{:S(2)}, u32[]{:S(2)}) collective-permute-start(bf16[3,6,32,128]{3,2,1,0:T(8,128)(2,1)S(1)} %collective-permute-done.5.refs_7_.refs_3_), channel_id=1, source_target_pairs={{0,1},{1,0},{2,3},{3,2},{4,5},{5,4},{6,7},{7,6},{8,9},{9,8},{10,11... | collective-permute-start | bytes 442376 | tf_op jit(solution)/shard_map/ppermute | solution.py:474
  83.7 1.2 copy-start.6
  83.7 26.6 %collective-permute-start.1 = (bf16[1,6,288,128]{3,2,1,0:T(8,128)(2,1)}, bf16[1,6,288,128]{3,2,1,0:T(8,128)(2,1)}, u32[]{:S(2)}, u32[]{:S(2)}) collective-permute-start(bf16[1,6,288,128]{3,2,1,0:T(8,128)(2,1)} %get-tuple-element.24), channel_id=1, source_target_pairs={{0,64},{32,96},{64,0},{96,32},{1,65},{33,97},{65,1},{97,33},{2,66}... | collective-permute-start | bytes 1327112 | tf_op jit(solution)/shard_map/ppermute | solution.py:120
  84.9 6.1 %copy-start.1 = (bf16[4,2,2,288,128]{4,3,2,1,0:T(8,128)(2,1)}, bf16[4,2,2,288,128]{4,3,2,1,0:T(8,128)(2,1)S(1)}, u32[]{:S(2)}) copy-start(bf16[4,2,2,288,128]{4,3,2,1,0:T(8,128)(2,1)S(1)} %all-to-all-done.refs_13_.refs_9_) | copy-start | bytes 3538948
  84.9 73.1 %collective-permute-start.10 = (bf16[4,2,2,288,128]{4,3,2,1,0:T(8,128)(2,1)S(1)}, bf16[4,2,2,288,128]{4,3,2,1,0:T(8,128)(2,1)}, u32[]{:S(2)}, u32[]{:S(2)}) collective-permute-start(bf16[4,2,2,288,128]{4,3,2,1,0:T(8,128)(2,1)S(1)} %all-to-all-done.refs_13_.refs_9_), channel_id=1, source_target_pairs={{1,0},{2,1},{3,2},{4,3},{5,4},{6,5},{7,6},{8,7},{9,8},{10,9},{11,1... | collective-permute-start | bytes 3538952 | tf_op jit(solution)/shard_map/ppermute | solution.py:135
  86.3 71.8 %collective-permute-start.9 = (bf16[4,2,2,288,128]{4,3,2,1,0:T(8,128)(2,1)S(1)}, bf16[4,2,2,288,128]{4,3,2,1,0:T(8,128)(2,1)}, u32[]{:S(2)}, u32[]{:S(2)}) collective-permute-start(bf16[4,2,2,288,128]{4,3,2,1,0:T(8,128)(2,1)S(1)} %all-to-all-done.refs_13_.refs_9_), channel_id=1, source_target_pairs={{0,1},{1,2},{2,3},{3,4},{4,5},{5,6},{6,7},{7,8},{8,9},{9,10},{10,1... | collective-permute-start | bytes 3538952 | tf_op jit(solution)/shard_map/ppermute | solution.py:135
  98.9 24.1 %all-to-all-start.2 = ((bf16[128,16,128]{2,1,0:T(8,128)(2,1)}), bf16[128,16,128]{2,1,0:T(8,128)(2,1)}, u32[]{:S(2)}, u32[]{:S(2)}) async-start(bf16[128,16,128]{2,1,0:T(8,128)(2,1)} %text_attention.1), calls=%async_computation.2 | async-start | bytes 1048576 | tf_op jit(solution)/shard_map/all_to_all | solution.py:131
  110.2 21.7 %collective-permute-start.2 = (bf16[1,6,288,128]{3,2,1,0:T(8,128)(2,1)}, bf16[1,6,288,128]{3,2,1,0:T(8,128)(2,1)}, u32[]{:S(2)}, u32[]{:S(2)}) collective-permute-start(bf16[1,6,288,128]{3,2,1,0:T(8,128)(2,1)} %get-tuple-element.25), channel_id=1, source_target_pairs={{0,96},{32,0},{64,32},{96,64},{1,97},{33,1},{65,33},{97,65},{2,98}... | collective-permute-start | bytes 1327112 | tf_op jit(solution)/shard_map/ppermute | solution.py:120
  126.0 48.6 %all-to-all-start.3 = ((bf16[128,16,128]{2,1,0:T(8,128)(2,1)}), bf16[128,16,128]{2,1,0:T(8,128)(2,1)}, u32[]{:S(2)}, u32[]{:S(2)}) async-start(bf16[128,16,128]{2,1,0:T(8,128)(2,1)} %bitcast.1), calls=%async_computation.3 | async-start | bytes 1048576 | tf_op jit(solution)/shard_map/all_to_all | solution.py:131
  153.2 18.8 %collective-permute-start.16 = (bf16[4,288,128]{2,1,0:T(8,128)(2,1)}, bf16[4,288,128]{2,1,0:T(8,128)(2,1)S(1)}, u32[]{:S(2)}, u32[]{:S(2)}) collective-permute-start(bf16[4,288,128]{2,1,0:T(8,128)(2,1)} %get-tuple-element.37), channel_id=1, source_target_pairs={{0,32},{32,64},{64,96},{96,0},{1,33},{33,65},{65,97},{97,1},{2,34}... | collective-permute-start | bytes 884744 | tf_op jit(solution)/shard_map/ppermute | solution.py:120
  153.9 20.7 %collective-permute-start.17 = (bf16[4,288,128]{2,1,0:T(8,128)(2,1)}, bf16[4,288,128]{2,1,0:T(8,128)(2,1)S(1)}, u32[]{:S(2)}, u32[]{:S(2)}) collective-permute-start(bf16[4,288,128]{2,1,0:T(8,128)(2,1)} %get-tuple-element.38), channel_id=1, source_target_pairs={{0,64},{32,96},{64,0},{96,32},{1,65},{33,97},{65,1},{97,33},{2,66}... | collective-permute-start | bytes 884744 | tf_op jit(solution)/shard_map/ppermute | solution.py:120
  156.6 18.0 %collective-permute-start.18 = (bf16[4,288,128]{2,1,0:T(8,128)(2,1)}, bf16[4,288,128]{2,1,0:T(8,128)(2,1)S(1)}, u32[]{:S(2)}, u32[]{:S(2)}) collective-permute-start(bf16[4,288,128]{2,1,0:T(8,128)(2,1)} %get-tuple-element.39), channel_id=1, source_target_pairs={{0,96},{32,0},{64,32},{96,64},{1,97},{33,1},{65,33},{97,65},{2,98}... | collective-permute-start | bytes 884744 | tf_op jit(solution)/shard_map/ppermute | solution.py:120
  170.5 9.7 %collective-permute-start.11 = (bf16[2,288,128]{2,1,0:T(8,128)(2,1)}, bf16[2,288,128]{2,1,0:T(8,128)(2,1)S(1)}, u32[]{:S(2)}, u32[]{:S(2)}) collective-permute-start(bf16[2,288,128]{2,1,0:T(8,128)(2,1)} %get-tuple-element.33), channel_id=1, source_target_pairs={{0,32},{32,64},{64,96},{96,0},{1,33},{33,65},{65,97},{97,1},{2,34}... | collective-permute-start | bytes 442376 | tf_op jit(solution)/shard_map/ppermute | solution.py:120
  171.1 9.0 %collective-permute-start.12 = (bf16[2,288,128]{2,1,0:T(8,128)(2,1)}, bf16[2,288,128]{2,1,0:T(8,128)(2,1)S(1)}, u32[]{:S(2)}, u32[]{:S(2)}) collective-permute-start(bf16[2,288,128]{2,1,0:T(8,128)(2,1)} %get-tuple-element.34), channel_id=1, source_target_pairs={{0,64},{32,96},{64,0},{96,32},{1,65},{33,97},{65,1},{97,33},{2,66}... | collective-permute-start | bytes 442376 | tf_op jit(solution)/shard_map/ppermute | solution.py:120
  172.1 2.6 %copy-start.7 = (bf16[4,288,128]{2,1,0:T(8,128)(2,1)}, bf16[4,288,128]{2,1,0:T(8,128)(2,1)S(1)}, u32[]{:S(2)}) copy-start(bf16[4,288,128]{2,1,0:T(8,128)(2,1)S(1)} %collective-permute-done.16.refs_1_) | copy-start | bytes 884740
  172.1 8.7 %collective-permute-start.13 = (bf16[2,288,128]{2,1,0:T(8,128)(2,1)}, bf16[2,288,128]{2,1,0:T(8,128)(2,1)S(1)}, u32[]{:S(2)}, u32[]{:S(2)}) collective-permute-start(bf16[2,288,128]{2,1,0:T(8,128)(2,1)} %get-tuple-element.35), channel_id=1, source_target_pairs={{0,96},{32,0},{64,32},{96,64},{1,97},{33,1},{65,33},{97,65},{2,98}... | collective-permute-start | bytes 442376 | tf_op jit(solution)/shard_map/ppermute | solution.py:120
  174.6 0.7 copy-start.8
  174.6 0.8 copy-start.9
  180.2 0.6 copy-start.10
  180.2 0.7 copy-start.11
  180.8 0.7 copy-start.12

commit v4 on v3

--- a/solution.py
+++ b/solution.py
@@ -22,14 +22,15 @@
 BLK = 32
 DEVS = GROUP * BLK
 RB = 128
-KEYS = 2 * SLICE + TXT
 SCALE = math.log2(math.e) / math.sqrt(D)
 CHUNKS = ((0, 4), (4, 2))
+LIMIT = 67043328
 BF = jnp.bfloat16
 F32 = jnp.float32
 
 
-HBM = pl.BlockSpec(memory_space=pltpu.HBM)
+ANY = pl.BlockSpec(memory_space=pl.ANY)
+PARAMS = pltpu.CompilerParams(vmem_limit_bytes=LIMIT)
 SMEM = pl.BlockSpec(memory_space=pltpu.SMEM)
 VMEM = pl.BlockSpec(memory_space=pltpu.VMEM)
 
@@ -102,11 +103,12 @@
 
     got = pl.pallas_call(
         body,
-        in_specs=[HBM] * len(arrays),
-        out_specs=[HBM] * len(outs),
+        in_specs=[ANY] * len(arrays),
+        out_specs=[ANY] * len(outs),
         out_shape=outs,
         scratch_shapes=[pltpu.VMEM(o.shape, BF) for o in outs]
         + [pltpu.SemaphoreType.DMA((160,)), pltpu.SemaphoreType.DMA((32,))],
+        compiler_params=PARAMS,
     )(*arrays)
     result, n = [], 0
     for job in jobs:
@@ -143,58 +145,102 @@
     return jnp.where(position < length, 0.0, -jnp.inf).astype(F32)
 
 
-def weigh(q, keys, values, masked):
-    s = lax.dot_general(q, keys(), (((1,), (1,)), ((), ())), preferred_element_type=F32)
-    return s, lambda: finish(s, values, masked)
-
-
-def finish(s, values, masked):
-    parts, at = [], 0
-    for start, bias in masked:
-        parts += [s[:, at:start], s[:, start : start + TXT] + bias]
-        at = start + TXT
-    if at < s.shape[1]:
-        parts.append(s[:, at:])
-    s = jnp.concatenate([p for p in parts if p.shape[1]], axis=1)
-    top = jnp.max(s, axis=1, keepdims=True)
-    p = jnp.exp2(s * SCALE - top * SCALE)
-    total = jnp.sum(p, axis=1, keepdims=True)
-    o = jnp.dot(p.astype(BF), values(), preferred_element_type=F32)
-    return o / total, top * SCALE + jnp.log2(total)
+def weigh(q, keys, values, text_keys, text_values, bias):
+    along = (((1,), (1,)), ((), ()))
+    s = lax.dot_general(q, keys(), along, preferred_element_type=F32)
+    t = lax.dot_general(q, text_keys(), along, preferred_element_type=F32)
+
+    def finish():
+        masked = t + bias
+        top = jnp.maximum(jnp.max(s, axis=1, keepdims=True), jnp.max(masked, axis=1, keepdims=True)) * SCALE
+        p = jnp.exp2(s * SCALE - top)
+        w = jnp.exp2(masked * SCALE - top)
+        total = jnp.sum(p, axis=1, keepdims=True) + jnp.sum(w, axis=1, keepdims=True)
+        o = jnp.dot(p.astype(BF), values(), preferred_element_type=F32)
+        o = o + jnp.dot(w.astype(BF), text_values(), preferred_element_type=F32)
+        return o / total, top + jnp.log2(total)
+
+    return finish
+
+
+def text_loads(text, first, heads, q_sc, t_sc):
+    some, pairs = pl.ds(first, heads), []
+    for n, piece in enumerate(text):
+        pairs.append((piece.at[pl.ds(1, 2), some], t_sc.at[:, :, pl.ds(n * HALF, HALF)]))
+        if q_sc is not None:
+            rows = rows_of(2 * place(-(n % GROUP)) + half(n // GROUP), HALF)
+            pairs.append((piece.at[0, some], q_sc.at[:, rows]))
+    return pairs
 
 
 SLOT = 16
 PAIRS = 12
 
 
-def text_body(length, *refs):
-    text, kv, refs = refs[: 2 * GROUP], refs[2 * GROUP :][: len(CHUNKS)], refs[2 * GROUP + len(CHUNKS) :]
-    out_ref, q_sc, kv_sc, o_sc, log_sc, sc, slots, sems = refs
-    pairs = []
-    for n, piece in enumerate(text):
-        pairs.append((piece.at[0], q_sc.at[:, rows_of(2 * place(-(n % GROUP)) + half(n // GROUP), HALF)]))
-        pairs.append((piece.at[pl.ds(1, 2)], kv_sc.at[:, :, pl.ds(SLICE + n * HALF, HALF)]))
-    for c, (first, heads) in enumerate(CHUNKS):
-        for g in range(GROUP):
-            pairs.append((kv[c].at[g], kv_sc.at[:, pl.ds(first, heads), pl.ds(g * ROWS, ROWS)]))
-    moves = copy_list(pairs, sems)
+def text_heads(length, first, heads, text, kv, extra, q_sc, kv_sc, t_sc, sems, o_sc, log_sc):
+    pairs = text_loads(text, first, heads, q_sc, t_sc)
+    pairs += [(kv.at[g], kv_sc.at[:, :, pl.ds(g * ROWS, ROWS)]) for g in range(GROUP)]
+    moves = copy_list(pairs + extra, sems)
     run(moves)
-    sc[...] = jnp.zeros_like(sc)
     bias = jnp.where(lax.axis_index("blk") == 0, text_bias(length[0]), -jnp.inf)
     wait(moves)
-    steps = [(h, i) for h in range(HD) for i in range(TXT // RB)]
+    steps = [(h, i) for h in range(heads) for i in range(TXT // RB)]
 
     def begin(h, i):
         q = q_sc[h, i * RB : (i + 1) * RB]
-        return weigh(q, lambda: kv_sc[0, h], lambda: kv_sc[1, h], [(SLICE, bias)])[1]
+        return weigh(q, lambda: kv_sc[0, h], lambda: kv_sc[1, h], lambda: t_sc[0, h], lambda: t_sc[1, h], bias)
 
     rest = begin(*steps[0])
     for n, (h, i) in enumerate(steps):
         following = begin(*steps[n + 1]) if n + 1 < len(steps) else None
         o, log = rest()
-        o_sc[h, i * RB : (i + 1) * RB] = o
-        log_sc[h, i * RB : (i + 1) * RB] = jnp.broadcast_to(log, (RB, D))
+        o_sc[first + h, i * RB : (i + 1) * RB] = o.astype(BF)
+        log_sc[first + h, i * RB : (i + 1) * RB] = jnp.broadcast_to(log, (RB, D))
         rest = following
+
+
+def early_body(length, *refs):
+    text, kv, refs = refs[: 2 * GROUP], refs[2 * GROUP], refs[2 * GROUP + 1 :]
+    o_ref, log_ref, q_sc, kv_sc, t_sc, o_sc, log_sc, sems = refs
+    text_heads(length, *CHUNKS[0], text, kv, [], q_sc, kv_sc, t_sc, sems, o_sc, log_sc)
+    moves = copy_list([(o_sc, o_ref), (log_sc, log_ref)], sems)
+    run(moves)
+    wait(moves)
+
+
+def text_scratch(heads):
+    return [
+        pltpu.VMEM((heads, TXT, D), BF),
+        pltpu.VMEM((2, heads, SLICE, D), BF),
+        pltpu.VMEM((2, heads, TXT, D), BF),
+    ]
+
+
+def early_text(length, text, kv):
+    heads = CHUNKS[0][1]
+    return pl.pallas_call(
+        early_body,
+        in_specs=[SMEM] + [ANY] * (2 * GROUP + 1),
+        out_specs=[ANY] * 2,
+        out_shape=[jax.ShapeDtypeStruct((heads, TXT, D), BF), jax.ShapeDtypeStruct((heads, TXT, D), F32)],
+        scratch_shapes=text_scratch(heads)
+        + [
+            pltpu.VMEM((heads, TXT, D), BF),
+            pltpu.VMEM((heads, TXT, D), F32),
+            pltpu.SemaphoreType.DMA((24,)),
+        ],
+        compiler_params=PARAMS,
+        name="early_text",
+    )(length, *text, kv)
+
+
+def text_body(length, *refs):
+    text, refs = refs[: 2 * GROUP], refs[2 * GROUP :]
+    kv, o_in, log_in, out_ref, q_sc, kv_sc, t_sc, o_sc, log_sc, sc, slots, sems = refs
+    done = pl.ds(0, CHUNKS[0][1])
+    extra = [(o_in, o_sc.at[done]), (log_in, log_sc.at[done])]
+    sc[...] = jnp.zeros_like(sc)
+    text_heads(length, *CHUNKS[1], text, kv, extra, q_sc, kv_sc, t_sc, sems, o_sc, log_sc)
     lane = lax.broadcasted_iota(jnp.int32, (TROWS, D), 1)
     for p in range(2):
         logs = jnp.zeros((TROWS, D), F32)
@@ -202,7 +248,7 @@
             rows = pl.ds(u2 * TROWS, TROWS)
             for i in range(3):
                 s = 3 * u2 + i
-                sc[pl.ds(SLOT * p + s, TROWS, stride=2 * SLOT), :] = o_sc[3 * p + i, rows, :]
+                sc[pl.ds(SLOT * p + s, TROWS, stride=2 * SLOT), :] = o_sc[3 * p + i, rows, :].astype(F32)
                 logs = jnp.where(lane == s, log_sc[3 * p + i, rows, :], logs)
         for part in range(3):
             rounded = logs.astype(BF).astype(F32)
@@ -212,6 +258,25 @@
     leave(slots, out_ref, sems)
 
 
+def text_attention(length, text, kv, o, log):
+    return pl.pallas_call(
+        text_body,
+        in_specs=[SMEM] + [ANY] * (2 * GROUP + 3),
+        out_specs=ANY,
+        out_shape=jax.ShapeDtypeStruct((DEVS, SLOT, D), BF),
+        scratch_shapes=text_scratch(CHUNKS[1][1])
+        + [
+            pltpu.VMEM((HD, TXT, D), BF),
+            pltpu.VMEM((HD, TXT, D), F32),
+            pltpu.VMEM((DEVS * SLOT, D), F32),
+            pltpu.VMEM((DEVS, SLOT, D), BF),
+            pltpu.SemaphoreType.DMA((24,)),
+        ],
+        compiler_params=PARAMS,
+        name="text_attention",
+    )(length, *text, kv, o, log)
+
+
 def leave(held, out_ref, sems):
     size = held.shape[0] // 4
     parts = [pl.ds(i * size, size) for i in range(4)]
@@ -220,27 +285,9 @@
     wait(moves)
 
 
-def text_attention(length, text, kv):
-    return pl.pallas_call(
-        text_body,
-        in_specs=[SMEM] + [HBM] * (2 * GROUP + len(CHUNKS)),
-        out_specs=HBM,
-        out_shape=jax.ShapeDtypeStruct((DEVS, SLOT, D), BF),
-        scratch_shapes=[
-            pltpu.VMEM((HD, TXT, D), BF),
-            pltpu.VMEM((2, HD, SLICE + TXT, D), BF),
-            pltpu.VMEM((HD, TXT, D), F32),
-            pltpu.VMEM((HD, TXT, D), F32),
-            pltpu.VMEM((DEVS * SLOT, D), F32),
-            pltpu.VMEM((DEVS, SLOT, D), BF),
-            pltpu.SemaphoreType.DMA((32,)),
-        ],
-        name="text_attention",
-    )(length, *text, *kv)
-
-
-def combine_body(in_ref, out_ref, sc, res, slots, sems):
-    sc[...] = in_ref[...].astype(F32).reshape(DEVS * SLOT, D)
+def combine_body(in_ref, out_ref, sc, res, slots, got, sems):
+    leave(in_ref, got, sems)
+    sc[...] = got[...].astype(F32).reshape(DEVS * SLOT, D)
     logs = sc[pl.ds(PAIRS, DEVS, stride=SLOT), :]
     for part in range(1, 3):
         logs = logs + sc[pl.ds(PAIRS + part, DEVS, stride=SLOT), :]
@@ -275,15 +322,17 @@
 def combine(received):
     return pl.pallas_call(
         combine_body,
-        in_specs=[VMEM],
-        out_specs=HBM,
+        in_specs=[ANY],
+        out_specs=ANY,
         out_shape=jax.ShapeDtypeStruct((BLK, GROUP, SLOT, D), BF),
         scratch_shapes=[
             pltpu.VMEM((DEVS * SLOT, D), F32),
             pltpu.VMEM((GROUP, SLOT, D), F32),
             pltpu.VMEM((BLK, GROUP, SLOT, D), BF),
+            pltpu.VMEM((DEVS, SLOT, D), BF),
             pltpu.SemaphoreType.DMA((4,)),
         ],
+        compiler_params=PARAMS,
         name="combine",
     )(received).reshape(DEVS, SLOT, D)
 
@@ -292,24 +341,22 @@
     q_refs, text, refs = refs[:GROUP], refs[GROUP : 3 * GROUP], refs[3 * GROUP :]
     before, own, after, refs = refs[0], refs[1], refs[2], refs[3:]
     o_refs, refs = refs[:GROUP], refs[GROUP:]
-    q_sc, k_sc, v_sc, o_sc, side_sc, sems, o_sems = refs
-
-    def loads(start, count, slot):
-        some = pl.ds(start, count)
-        parts = []
-        for a, sc in ((0, k_sc), (1, v_sc)):
-            pairs = []
-            for base, kv in ((0, before), (SLICE, own), (KEYS, after)):
-                for g in range(GROUP):
-                    pairs.append((kv.at[g, a, some], sc.at[some, pl.ds(base + g * ROWS, ROWS)]))
-            for n, piece in enumerate(text):
-                rows = pl.ds(2 * SLICE + n * HALF, HALF)
-                pairs.append((piece.at[1 + a, pl.ds(first + start, count)], sc.at[some, rows]))
-            parts.append(pairs)
-        asked = pl.ds(first + start, count)
-        queries = [(q_refs[d].at[0, asked], q_sc.at[some, rows_of(place(-d), ROWS)]) for d in range(GROUP)]
-        pairs = queries + parts[0] + parts[1]
-        return copy_list(pairs, sems.at[slot]), len(queries + parts[0])
+    q_sc, k_sc, v_sc, t_sc, o_sc, side_sc, sems, text_sems, o_sems = refs
+
+    def loads(h, a):
+        sc = (k_sc, v_sc)[a]
+        pairs = [(kv.at[:, a, h], sc.at[h, n]) for n, kv in enumerate((before, own, after))]
+        return copy_list(pairs, sems.at[h, a])
+
+    asked = pl.ds(first, heads)
+    pairs = [(q_refs[d].at[0, asked], q_sc.at[:, rows_of(place(-d), ROWS)]) for d in range(GROUP)]
+    shared = copy_list(pairs + text_loads(text, first, heads, None, t_sc), text_sems)
+    run(loads(0, 0))
+    run(shared)
+    run(loads(0, 1))
+    for h in range(1, heads):
+        run(loads(h, 0))
+        run(loads(h, 1))
 
     def stores(h):
         return [
@@ -317,10 +364,6 @@
             for d in range(GROUP)
         ]
 
-    head, keys_only = loads(0, 1, 0)
-    others, _ = loads(1, heads - 1, 1)
-    run(head)
-    run(others)
     limit = (lax.axis_index("blk") + 1) * tiles.shape[0]
     for j in range(tiles.shape[0]):
         last = tiles[j, 0]
@@ -330,26 +373,28 @@
     live = text_bias(length[0])
 
     def step(h, i):
-        f = side_sc[i * RB // TILE]
-        window = pl.ds(pl.multiple_of(f * SLICE, RB), KEYS)
-        masked = [(SLICE, jnp.where(f == 1, live, 0.0)), (2 * SLICE, jnp.where(f == 1, 0.0, live))]
+        f = pl.ds(side_sc[i * RB // TILE], 2)
         q = q_sc[h, i * RB : (i + 1) * RB, :]
-        return weigh(q, lambda: k_sc[h, window], lambda: v_sc[h, window], masked)[1]
+        window = 2 * SLICE
+        return weigh(
+            q,
+            lambda: k_sc[h, f].reshape(window, D),
+            lambda: v_sc[h, f].reshape(window, D),
+            lambda: t_sc[0, h],
+            lambda: t_sc[1, h],
+            live,
+        )
 
     steps = SLICE // RB
-    wait(head[:keys_only])
+    wait(loads(0, 0) + shared)
 
     def one(h, _):
-        @pl.when(h == 1)
+        @pl.when(h > 0)
         def _():
-            wait(others)
+            wait(loads(h, 0))
 
         rest = step(h, 0)
-
-        @pl.when(h == 0)
-        def _():
-            wait(head[keys_only:])
-
+        wait(loads(h, 1))
         for i in range(steps):
             following = step(h, i + 1) if i + 1 < steps else None
             o, _ = rest()
@@ -366,18 +411,21 @@
 def video_attention(first, heads, tiles, length, q, text, before, own, after):
     return pl.pallas_call(
         functools.partial(video_body, first, heads),
-        in_specs=[SMEM, SMEM] + [HBM] * (3 * GROUP + 3),
-        out_specs=[HBM] * GROUP,
+        in_specs=[SMEM, SMEM] + [ANY] * (3 * GROUP + 3),
+        out_specs=[ANY] * GROUP,
         out_shape=[jax.ShapeDtypeStruct((heads, ROWS, D), BF)] * GROUP,
         scratch_shapes=[
             pltpu.VMEM((heads, SLICE, D), BF),
-            pltpu.VMEM((heads, KEYS + SLICE, D), BF),
-            pltpu.VMEM((heads, KEYS + SLICE, D), BF),
+            pltpu.VMEM((heads, 3, GROUP, ROWS, D), BF),
+            pltpu.VMEM((heads, 3, GROUP, ROWS, D), BF),
+            pltpu.VMEM((2, heads, TXT, D), BF),
             pltpu.VMEM((heads, SLICE, D), BF),
             pltpu.SMEM((8,), jnp.int32),
-            pltpu.SemaphoreType.DMA((2, 48)),
+            pltpu.SemaphoreType.DMA((heads, 2, 3)),
+            pltpu.SemaphoreType.DMA((12,)),
             pltpu.SemaphoreType.DMA((heads, GROUP)),
         ],
+        compiler_params=PARAMS,
         name="video_attention",
     )(tiles, length, *q, *text, before, own, after)
 
@@ -400,9 +448,10 @@
 
 
 def first_body(first, heads, *refs):
-    pieces, slots, video_out, text_out, held, sc, in_sems, out_sems = refs[:GROUP], *refs[GROUP:]
+    pieces, slots, video_out, text_out, held, sc, got, in_sems, out_sems, sems = refs[:GROUP], *refs[GROUP:]
     writes = rows_body(first, heads, *pieces, video_out, held, in_sems, out_sems)
-    sc[...] = slots[...].astype(F32).reshape(DEVS * SLOT, D)
+    leave(slots, got, sems)
+    sc[...] = got[...].astype(F32).reshape(DEVS * SLOT, D)
     for p in range(2):
         for u in range(GROUP):
             for i in range(3):
@@ -419,8 +468,8 @@
 def first_rows(pieces, slots, first, heads):
     return pl.pallas_call(
         functools.partial(first_body, first, heads),
-        in_specs=[HBM] * GROUP + [VMEM],
-        out_specs=[HBM, VMEM],
+        in_specs=[ANY] * (GROUP + 1),
+        out_specs=[ANY, VMEM],
         out_shape=[
             jax.ShapeDtypeStruct((ROWS, HEADS * D), BF),
             jax.ShapeDtypeStruct((TROWS, HEADS * D), BF),
@@ -428,9 +477,12 @@
         scratch_shapes=[
             pltpu.VMEM((GROUP * heads, ROWS, D), BF),
             pltpu.VMEM((DEVS * SLOT, D), F32),
+            pltpu.VMEM((DEVS, SLOT, D), BF),
             pltpu.SemaphoreType.DMA((GROUP * heads,)),
             pltpu.SemaphoreType.DMA((GROUP * heads,)),
-        ],
+            pltpu.SemaphoreType.DMA((4,)),
+        ],
+        compiler_params=PARAMS,
         name="first_rows",
     )(*pieces, slots)
 
@@ -438,8 +490,8 @@
 def later_rows(pieces, rows, first, heads):
     return pl.pallas_call(
         functools.partial(later_body, first, heads),
-        in_specs=[HBM] * (GROUP + 1),
-        out_specs=HBM,
+        in_specs=[ANY] * (GROUP + 1),
+        out_specs=ANY,
         out_shape=jax.ShapeDtypeStruct((ROWS, HEADS * D), BF),
         scratch_shapes=[
             pltpu.VMEM((GROUP * heads, ROWS, D), BF),
@@ -447,6 +499,7 @@
             pltpu.SemaphoreType.DMA((GROUP * heads,)),
         ],
         input_output_aliases={GROUP: 0},
+        compiler_params=PARAMS,
         name="later_rows",
     )(*pieces, rows)
 
@@ -474,7 +527,8 @@
         other.append(lax.ppermute(mine[d], "blk", [(i, i ^ 1) for i in range(BLK)]))
     text = mine + other
     q = exchange(q)
-    slots = text_attention(text_len, text, own)
+    early = early_text(text_len, text, own[0])
+    slots = text_attention(text_len, text, own[1], *early)
     slots = swap(slots, ("blk", "uly"))
     slots = combine(slots)
     slots = swap(slots, ("blk", "uly"))

time: 184 us -> 196 us (1.065)
  Pallas kernels: 60.3 us -> 71.7 us
    pallas_call x2, Pallas kernels: 33.7 us -> 40.4 us  [video_attention(): pl.pallas_call(functools.partial(video_body, first, heads), in_specs=[SME...]
    pallas_call x6 -> x7, Pallas kernels: 26.7 us -> 31.3 us  [the longest x2 9.87 us: pack(): pl.pallas_call(body, in_specs=[ANY] * len(arrays), out_specs=[ANY] * len(...]
  transfers between devices with their start and end apart: 22 -> 22, of which waited for: 7 -> 7; matrix products, arithmetic and copies ran while one was open for 0% -> 0% of each run, Pallas kernels for 29% -> 33%
where the time goes in v4:
time: 196 us; the launch traced here: 195 us
  Pallas kernels  71.7 us (37%)
  starting transfers between devices  50.7 us (26%)
  waiting for transfers between devices  37.5 us (19%)
  blocking collectives  33.8 us (17%)
    pallas_call x2, Pallas kernels, video_attention(): pl.pallas_call(functools.partial(video_body, first, heads), in_specs=[SME...  40.4 us
    all_to_all x1, blocking collectives, swap(): return lax.all_to_all(array, axes, 0, 0, tiled=True)  33.8 us
    ppermute x12, waiting for transfers between devices, around(): lax.ppermute(block, 'uly', [(i, (i + distance) % GROUP) for i in range(GR...  26.3 us
    all_to_all x3, starting transfers between devices, swap(): return lax.all_to_all(array, axes, 0, 0, tiled=True)  21.8 us
    ppermute x12, starting transfers between devices, around(): lax.ppermute(block, 'uly', [(i, (i + distance) % GROUP) for i in range(GR...  17.2 us
    ppermute x4, starting transfers between devices, beside(): lax.ppermute(block, 'blk', [(i, i + distance) for i in range(BLK) if 0 <=...  11.1 us
    all_to_all x3, waiting for transfers between devices, swap(): return lax.all_to_all(array, axes, 0, 0, tiled=True)  10.4 us
    pallas_call x2, Pallas kernels, pack(): pl.pallas_call(body, in_specs=[ANY] * len(arrays), out_specs=[ANY] * len(...  9.87 us
  transfers between devices with their start and end apart: 22, of which 7 were waited for; matrix products, arithmetic and copies ran while one was open for 0% of the time, Pallas kernels for 33%

profile of v4, /device:TPU:0, one launch (start us, length us, event | category | flops | bytes accessed | tf_op | source)
XLA Modules:
  0.0 195.5 jit_solution(2231398039066289699)
XLA Ops:
  0.6 4.3 %shard_map.96 = bf16[4,2,4,288,128]{4,3,2,1,0:T(8,128)(2,1)} custom-call(bf16[288,3072]{1,0:T(8,128)(2,1)} %refs_0_.3, bf16[288,3072]{1,0:T(8,128)(2,1)} %refs_1_.3, bf16[288,3072]{1,0:T(8,128)(2,1)} %refs_2_.3), custom_call_target="tpu_custom_call" | custom-call | tf_op jit(solution)/shard_map/pallas_call | solution.py:104
  5.0 33.8 %all_to_all.20.refs_13_.refs_8_ = bf16[4,2,4,288,128]{4,3,2,1,0:T(8,128)(2,1)} all-to-all(bf16[4,2,4,288,128]{4,3,2,1,0:T(8,128)(2,1)} %shard_map.96), channel_id=1, replica_groups=mesh['uly'=4,'blk'=32] {'uly'}, dimensions={0} | all-to-all | bytes 4718592 | tf_op jit(solution)/shard_map/all_to_all | solution.py:133
  38.8 1.3 collective-permute-start.15
  40.1 4.5 %collective-permute-start.14 = (bf16[4,2,4,288,128]{4,3,2,1,0:T(8,128)(2,1)}, bf16[4,2,4,288,128]{4,3,2,1,0:T(8,128)(2,1)}, u32[]{:S(2)}, u32[]{:S(2)}) collective-permute-start(bf16[4,2,4,288,128]{4,3,2,1,0:T(8,128)(2,1)} %all_to_all.20.refs_13_.refs_8_), channel_id=1, source_target_pairs={{0,1},{1,2},{2,3},{3,4},{4,5},{5,6},{6,7},{7,8},{8,9},{9,10},{10,1... | collective-permute-start | bytes 7077896 | tf_op jit(solution)/shard_map/ppermute | solution.py:137
  44.5 5.5 %shard_map.95 = (bf16[3,6,32,128]{3,2,1,0:T(8,128)(2,1)}, bf16[3,6,32,128]{3,2,1,0:T(8,128)(2,1)}, bf16[3,6,32,128]{3,2,1,0:T(8,128)(2,1)}, bf16[3,6,32,128]{3,2...) custom-call(bf16[288,3072]{1,0:T(8,128)(2,1)} %refs_0_.3, ...), custom_call_target="tpu_custom_call" | custom-call | tf_op jit(solution)/shard_map/pallas_call | solution.py:104
  50.1 0.0 copy-start.8
  50.1 0.0 copy-start.7
  50.1 0.0 copy-start.5
  50.1 0.0 copy-start.6
  50.1 4.4 %all-to-all-start = ((bf16[4,2,2,288,128]{4,3,2,1,0:T(8,128)(2,1)}), bf16[4,2,2,288,128]{4,3,2,1,0:T(8,128)(2,1)}, u32[]{:S(2)}, u32[]{:S(2)}) async-start(bf16[4,2,2,288,128]{4,3,2,1,0:T(8,128)(2,1)} %get-tuple-element.33), calls=%async_computation | async-start | bytes 2359296 | tf_op jit(solution)/shard_map/all_to_all | solution.py:133
  54.5 0.0 copy-done.8
  54.5 2.0 %collective-permute-start.3 = (bf16[3,6,32,128]{3,2,1,0:T(8,128)(2,1)S(1)}, bf16[3,6,32,128]{3,2,1,0:T(8,128)(2,1)S(1)}, u32[]{:S(2)}, u32[]{:S(2)}) collective-permute-start(bf16[3,6,32,128]{3,2,1,0:T(8,128)(2,1)S(1)} %copy-done.8), channel_id=1, source_target_pairs={{0,32},{32,64},{64,96},{96,0},{1,33},{33,65},{65,97},{97,1},{2,34}... | collective-permute-start | bytes 442376 | tf_op jit(solution)/shard_map/ppermute | solution.py:122
  56.5 0.0 copy-done.7
  56.5 2.7 %collective-permute-start.4 = (bf16[3,6,32,128]{3,2,1,0:T(8,128)(2,1)S(1)}, bf16[3,6,32,128]{3,2,1,0:T(8,128)(2,1)S(1)}, u32[]{:S(2)}, u32[]{:S(2)}) collective-permute-start(bf16[3,6,32,128]{3,2,1,0:T(8,128)(2,1)S(1)} %copy-done.7), channel_id=1, source_target_pairs={{0,64},{32,96},{64,0},{96,32},{1,65},{33,97},{65,1},{97,33},{2,66}... | collective-permute-start | bytes 442376 | tf_op jit(solution)/shard_map/ppermute | solution.py:122
  59.2 0.0 collective-permute-start
  59.2 18.8 %collective-permute-done.3.refs_5_.refs_1_ = bf16[3,6,32,128]{3,2,1,0:T(8,128)(2,1)S(1)} collective-permute-done((bf16[3,6,32,128]{3,2,1,0:T(8,128)(2,1)S(1)}, bf16[3,6,32,128]{3,2,1,0:T(8,128)(2,1)S(1)}, u32[]{:S(2)}, u32[]{:S(2)}) %collective-permute-start.3) | collective-permute-done | bytes 147488 | tf_op jit(solution)/shard_map/ppermute | solution.py:122
  78.0 0.0 collective-permute-start.5
  78.0 0.8 collective-permute-done.4.refs_6_.refs_2_
  78.8 0.0 copy-done
  78.8 0.0 collective-permute-start.6
  78.8 4.4 %collective-permute-done.5.refs_7_.refs_3_ = bf16[3,6,32,128]{3,2,1,0:T(8,128)(2,1)S(1)} collective-permute-done((bf16[3,6,32,128]{3,2,1,0:T(8,128)(2,1)S(1)}, bf16[3,6,32,128]{3,2,1,0:T(8,128)(2,1)S(1)}, u32[]{:S(2)}, u32[]{:S(2)}) %collective-permute-start.5) | collective-permute-done | bytes 147488 | tf_op jit(solution)/shard_map/ppermute | solution.py:122
  83.2 0.0 collective-permute-start.7
  83.2 0.0 collective-permute-done.6.refs_9_.refs_5_
  83.2 0.0 copy-done.1
  83.2 0.0 copy-start.3
  83.2 0.6 collective-permute-start.8
  83.8 0.8 collective-permute-done.7.refs_10_.refs_6_
  84.6 0.0 copy-done.2
  84.6 1.3 collective-permute-start.1
  85.9 0.0 collective-permute-done.8.refs_11_.refs_7_
  85.9 0.0 all-to-all-done.refs_13_.refs_8_
  85.9 1.3 collective-permute-start.10
  87.2 0.0 collective-permute-done.refs_1_
  87.2 4.0 %collective-permute-start.9 = (bf16[4,2,2,288,128]{4,3,2,1,0:T(8,128)(2,1)}, bf16[4,2,2,288,128]{4,3,2,1,0:T(8,128)(2,1)}, u32[]{:S(2)}, u32[]{:S(2)}) collective-permute-start(bf16[4,2,2,288,128]{4,3,2,1,0:T(8,128)(2,1)} %all-to-all-done.refs_13_.refs_8_), channel_id=1, source_target_pairs={{0,1},{1,2},{2,3},{3,4},{4,5},{5,6},{6,7},{7,8},{8,9},{9,10},{10,1... | collective-permute-start | bytes 3538952 | tf_op jit(solution)/shard_map/ppermute | solution.py:137
  91.9 6.8 %early_text.1 = (bf16[4,256,128]{2,1,0:T(8,128)(2,1)}, f32[4,256,128]{2,1,0:T(8,128)}) custom-call(s32[1]{0:T(128)S(6)} %copy.12.length, bf16[3,6,32,128]{3,2,1,0:T(8,128)(2,1)} %get-tuple-element.28.refs_4_.refs_0_, bf16[3,6,32,128]{3,2,1,0:T(8,128)(2,1)} %copy-done, bf16[3,6,32,128]{3,2,1,0:T(8,128)(2,1)} %copy-done.1, bf16[3,6,32,128]{3,2,1,0:T(8,128)(2,1)} %copy-done.2, ...), custom_call_target="tpu_custom_call" | custom-call | tf_op jit(solution)/shard_map/early_text/pallas_call | solution.py:221
  98.7 5.6 %text_attention.1 = bf16[128,16,128]{2,1,0:T(8,128)(2,1)} custom-call(s32[1]{0:T(128)S(6)} %copy.12.length, bf16[3,6,32,128]{3,2,1,0:T(8,128)(2,1)} %get-tuple-element.28.refs_4_.refs_0_, bf16[3,6,32,128]{3,2,1,0:T(8,128)(2,1)} %copy-done, bf16[3,6,32,128]{3,2,1,0:T(8,128)(2,1)} %copy-done.1, bf16[3,6,32,128]{3,2,1,0:T(8,128)(2,1)} %copy-done.2, ...), custom_call_target="tpu_custom_call" | custom-call | tf_op jit(solution)/shard_map/text_attention/pallas_call | solution.py:262
  104.3 11.6 %all-to-all-start.2 = ((bf16[128,16,128]{2,1,0:T(8,128)(2,1)}), bf16[128,16,128]{2,1,0:T(8,128)(2,1)}, u32[]{:S(2)}, u32[]{:S(2)}) async-start(bf16[128,16,128]{2,1,0:T(8,128)(2,1)} %text_attention.1), calls=%async_computation.2 | async-start | bytes 1048576 | tf_op jit(solution)/shard_map/all_to_all | solution.py:133
  116.0 0.0 collective-permute-done.1.refs_2_
  116.0 2.3 %collective-permute-start.2 = (bf16[1,6,288,128]{3,2,1,0:T(8,128)(2,1)}, bf16[1,6,288,128]{3,2,1,0:T(8,128)(2,1)}, u32[]{:S(2)}, u32[]{:S(2)}) collective-permute-start(bf16[1,6,288,128]{3,2,1,0:T(8,128)(2,1)} %get-tuple-element.27), channel_id=1, source_target_pairs={{0,96},{32,0},{64,32},{96,64},{1,97},{33,1},{65,33},{97,65},{2,98}... | collective-permute-start | bytes 1327112 | tf_op jit(solution)/shard_map/ppermute | solution.py:122
  118.3 10.4 %all-to-all-done.2.in_ref = bf16[128,16,128]{2,1,0:T(8,128)(2,1)} async-done(((bf16[128,16,128]{2,1,0:T(8,128)(2,1)}), bf16[128,16,128]{2,1,0:T(8,128)(2,1)}, u32[]{:S(2)}, u32[]{:S(2)}) %all-to-all-start.2) | async-done | bytes 524320 | tf_op jit(solution)/shard_map/all_to_all | solution.py:133
  128.8 3.0 %combine.1 = bf16[32,4,16,128]{3,2,1,0:T(8,128)(2,1)} custom-call(bf16[128,16,128]{2,1,0:T(8,128)(2,1)} %all-to-all-done.2.in_ref), custom_call_target="tpu_custom_call" | custom-call | tf_op jit(solution)/shard_map/combine/pallas_call | solution.py:323
  131.8 5.8 %all-to-all-start.3 = ((bf16[128,16,128]{2,1,0:T(8,128)(2,1)}), bf16[128,16,128]{2,1,0:T(8,128)(2,1)}, u32[]{:S(2)}, u32[]{:S(2)}) async-start(bf16[128,16,128]{2,1,0:T(8,128)(2,1)} %bitcast.1), calls=%async_computation.3 | async-start | bytes 1048576 | tf_op jit(solution)/shard_map/all_to_all | solution.py:133
  137.5 0.0 collective-permute-done.2.refs_3_
  137.5 0.0 collective-permute-done.15.refs_14_
  137.6 0.0 collective-permute-done.14.refs_12_
  137.6 26.0 %video_attention.3 = (bf16[4,288,128]{2,1,0:T(8,128)(2,1)}, bf16[4,288,128]{2,1,0:T(8,128)(2,1)}, bf16[4,288,128]{2,1,0:T(8,128)(2,1)}, bf16[4,288,128]{2,1,0:T(8,128)(2,1)}) custom-call(s32[3,6]{1,0:T(4,128)} %tiles.3, s32[1]{0:T(128)S(6)} %copy.12.length, bf16[1,6,288,128]{3,2,1,0:T(8,128)(2,1)} %get-tuple-element.24.refs_0_, ...), custom_call_target="tpu_custom_call" | custom-call | tf_op jit(solution)/shard_map/video_attention/pallas_call | solution.py:412
  163.6 0.8 collective-permute-start.16
  164.4 2.7 %collective-permute-start.17 = (bf16[4,288,128]{2,1,0:T(8,128)(2,1)}, bf16[4,288,128]{2,1,0:T(8,128)(2,1)}, u32[]{:S(2)}, u32[]{:S(2)}) collective-permute-start(bf16[4,288,128]{2,1,0:T(8,128)(2,1)} %get-tuple-element.40), channel_id=1, source_target_pairs={{0,64},{32,96},{64,0},{96,32},{1,65},{33,97},{65,1},{97,33},{2,66}... | collective-permute-start | bytes 884744 | tf_op jit(solution)/shard_map/ppermute | solution.py:122
  167.1 1.4 collective-permute-start.18
  168.6 0.0 collective-permute-done.10.refs_14_
  168.6 0.0 collective-permute-done.9.refs_12_
  168.6 14.4 %video_attention.2 = (bf16[2,288,128]{2,1,0:T(8,128)(2,1)}, bf16[2,288,128]{2,1,0:T(8,128)(2,1)}, bf16[2,288,128]{2,1,0:T(8,128)(2,1)}, bf16[2,288,128]{2,1,0:T(8,128)(2,1)}) custom-call(s32[3,6]{1,0:T(4,128)} %tiles.3, s32[1]{0:T(128)S(6)} %copy.12.length, bf16[1,6,288,128]{3,2,1,0:T(8,128)(2,1)} %get-tuple-element.24.refs_0_, ...), custom_call_target="tpu_custom_call" | custom-call | tf_op jit(solution)/shard_map/video_attention/pallas_call | solution.py:412
  183.0 0.6 collective-permute-start.11
  183.6 0.9 collective-permute-start.12
  184.5 0.0 collective-permute-done.16.refs_1_
  184.5 2.4 %collective-permute-start.13 = (bf16[2,288,128]{2,1,0:T(8,128)(2,1)}, bf16[2,288,128]{2,1,0:T(8,128)(2,1)}, u32[]{:S(2)}, u32[]{:S(2)}) collective-permute-start(bf16[2,288,128]{2,1,0:T(8,128)(2,1)} %get-tuple-element.37), channel_id=1, source_target_pairs={{0,96},{32,0},{64,32},{96,64},{1,97},{33,1},{65,33},{97,65},{2,98}... | collective-permute-start | bytes 442376 | tf_op jit(solution)/shard_map/ppermute | solution.py:122
  186.9 0.0 all-to-all-done.3.refs_4_
  186.9 0.0 collective-permute-done.17.refs_2_
  186.9 0.0 collective-permute-done.18.refs_3_
  186.9 4.1 %first_rows.1 = (bf16[288,3072]{1,0:T(8,128)(2,1)}, bf16[64,3072]{1,0:T(8,128)(2,1)}) custom-call(bf16[4,288,128]{2,1,0:T(8,128)(2,1)} %get-tuple-element.38.refs_0_, bf16[4,288,128]{2,1,0:T(8,128)(2,1)} %collective-permute-done.16.refs_1_, bf16[4,288,128]{2,1,0:T(8,128)(2,1)} %collective-permute-done.17.refs_2_, ...), custom_call_target="tpu_custom_call" | custom-call | tf_op jit(solution)/shard_map/first_rows/pallas_call | solution.py:469
  191.0 1.7 collective-permute-done.11.refs_1_
  192.8 0.0 collective-permute-done.12.refs_2_
  192.8 0.6 collective-permute-done.13.refs_3_
  193.4 1.9 later_rows.1
  (8 shorter events, 0.0 us)
Async XLA Ops:
  38.8 98.8 %collective-permute-start.15 = (bf16[4,2,4,288,128]{4,3,2,1,0:T(8,128)(2,1)}, bf16[4,2,4,288,128]{4,3,2,1,0:T(8,128)(2,1)}, u32[]{:S(2)}, u32[]{:S(2)}) collective-permute-start(bf16[4,2,4,288,128]{4,3,2,1,0:T(8,128)(2,1)} %all_to_all.20.refs_13_.refs_8_), channel_id=1, source_target_pairs={{1,0},{2,1},{3,2},{4,3},{5,4},{6,5},{7,6},{8,7},{9,8},{10,9},{11,1... | collective-permute-start | bytes 7077896 | tf_op jit(solution)/shard_map/ppermute | solution.py:137
  40.1 97.5 %collective-permute-start.14 = (bf16[4,2,4,288,128]{4,3,2,1,0:T(8,128)(2,1)}, bf16[4,2,4,288,128]{4,3,2,1,0:T(8,128)(2,1)}, u32[]{:S(2)}, u32[]{:S(2)}) collective-permute-start(bf16[4,2,4,288,128]{4,3,2,1,0:T(8,128)(2,1)} %all_to_all.20.refs_13_.refs_8_), channel_id=1, source_target_pairs={{0,1},{1,2},{2,3},{3,4},{4,5},{5,6},{6,7},{7,8},{8,9},{9,10},{10,1... | collective-permute-start | bytes 7077896 | tf_op jit(solution)/shard_map/ppermute | solution.py:137
  50.1 4.5 %copy-start.8 = (bf16[3,6,32,128]{3,2,1,0:T(8,128)(2,1)S(1)}, bf16[3,6,32,128]{3,2,1,0:T(8,128)(2,1)}, u32[]{:S(2)}) copy-start(bf16[3,6,32,128]{3,2,1,0:T(8,128)(2,1)} %get-tuple-element.29) | copy-start | bytes 442372
  50.1 6.4 %copy-start.7 = (bf16[3,6,32,128]{3,2,1,0:T(8,128)(2,1)S(1)}, bf16[3,6,32,128]{3,2,1,0:T(8,128)(2,1)}, u32[]{:S(2)}) copy-start(bf16[3,6,32,128]{3,2,1,0:T(8,128)(2,1)} %get-tuple-element.30) | copy-start | bytes 442372
  50.1 9.1 %copy-start.5 = (bf16[1,6,288,128]{3,2,1,0:T(8,128)(2,1)S(1)}, bf16[1,6,288,128]{3,2,1,0:T(8,128)(2,1)}, u32[]{:S(2)}) copy-start(bf16[1,6,288,128]{3,2,1,0:T(8,128)(2,1)} %get-tuple-element.25) | copy-start | bytes 1327108
  50.1 27.9 %copy-start.6 = (bf16[3,6,32,128]{3,2,1,0:T(8,128)(2,1)S(1)}, bf16[3,6,32,128]{3,2,1,0:T(8,128)(2,1)}, u32[]{:S(2)}) copy-start(bf16[3,6,32,128]{3,2,1,0:T(8,128)(2,1)} %get-tuple-element.31) | copy-start | bytes 442372
  50.1 35.8 %all-to-all-start = ((bf16[4,2,2,288,128]{4,3,2,1,0:T(8,128)(2,1)}), bf16[4,2,2,288,128]{4,3,2,1,0:T(8,128)(2,1)}, u32[]{:S(2)}, u32[]{:S(2)}) async-start(bf16[4,2,2,288,128]{4,3,2,1,0:T(8,128)(2,1)} %get-tuple-element.33), calls=%async_computation | async-start | bytes 2359296 | tf_op jit(solution)/shard_map/all_to_all | solution.py:133
  54.5 23.5 %collective-permute-start.3 = (bf16[3,6,32,128]{3,2,1,0:T(8,128)(2,1)S(1)}, bf16[3,6,32,128]{3,2,1,0:T(8,128)(2,1)S(1)}, u32[]{:S(2)}, u32[]{:S(2)}) collective-permute-start(bf16[3,6,32,128]{3,2,1,0:T(8,128)(2,1)S(1)} %copy-done.8), channel_id=1, source_target_pairs={{0,32},{32,64},{64,96},{96,0},{1,33},{33,65},{65,97},{97,1},{2,34}... | collective-permute-start | bytes 442376 | tf_op jit(solution)/shard_map/ppermute | solution.py:122
  56.5 22.3 %collective-permute-start.4 = (bf16[3,6,32,128]{3,2,1,0:T(8,128)(2,1)S(1)}, bf16[3,6,32,128]{3,2,1,0:T(8,128)(2,1)S(1)}, u32[]{:S(2)}, u32[]{:S(2)}) collective-permute-start(bf16[3,6,32,128]{3,2,1,0:T(8,128)(2,1)S(1)} %copy-done.7), channel_id=1, source_target_pairs={{0,64},{32,96},{64,0},{96,32},{1,65},{33,97},{65,1},{97,33},{2,66}... | collective-permute-start | bytes 442376 | tf_op jit(solution)/shard_map/ppermute | solution.py:122
  59.2 28.0 %collective-permute-start = (bf16[1,6,288,128]{3,2,1,0:T(8,128)(2,1)S(1)}, bf16[1,6,288,128]{3,2,1,0:T(8,128)(2,1)}, u32[]{:S(2)}, u32[]{:S(2)}) collective-permute-start(bf16[1,6,288,128]{3,2,1,0:T(8,128)(2,1)S(1)} %copy-done.5), channel_id=1, source_target_pairs={{0,32},{32,64},{64,96},{96,0},{1,33},{33,65},{65,97},{97,1},{2,34}... | collective-permute-start | bytes 1327112 | tf_op jit(solution)/shard_map/ppermute | solution.py:122
  78.0 0.8 copy-start
  78.0 5.1 %collective-permute-start.5 = (bf16[3,6,32,128]{3,2,1,0:T(8,128)(2,1)S(1)}, bf16[3,6,32,128]{3,2,1,0:T(8,128)(2,1)S(1)}, u32[]{:S(2)}, u32[]{:S(2)}) collective-permute-start(bf16[3,6,32,128]{3,2,1,0:T(8,128)(2,1)S(1)} %copy-done.6), channel_id=1, source_target_pairs={{0,96},{32,0},{64,32},{96,64},{1,97},{33,1},{65,33},{97,65},{2,98}... | collective-permute-start | bytes 442376 | tf_op jit(solution)/shard_map/ppermute | solution.py:122
  78.8 4.4 %copy-start.1 = (bf16[3,6,32,128]{3,2,1,0:T(8,128)(2,1)}, bf16[3,6,32,128]{3,2,1,0:T(8,128)(2,1)S(1)}, u32[]{:S(2)}) copy-start(bf16[3,6,32,128]{3,2,1,0:T(8,128)(2,1)S(1)} %collective-permute-done.4.refs_6_.refs_2_) | copy-start | bytes 442372
  78.8 4.4 %collective-permute-start.6 = (bf16[3,6,32,128]{3,2,1,0:T(8,128)(2,1)S(1)}, bf16[3,6,32,128]{3,2,1,0:T(8,128)(2,1)S(1)}, u32[]{:S(2)}, u32[]{:S(2)}) collective-permute-start(bf16[3,6,32,128]{3,2,1,0:T(8,128)(2,1)S(1)} %collective-permute-done.3.refs_5_.refs_1_), channel_id=1, source_target_pairs={{0,1},{1,0},{2,3},{3,2},{4,5},{5,4},{6,7},{7,6},{8,9},{9,8},{10,11... | collective-permute-start | bytes 442376 | tf_op jit(solution)/shard_map/ppermute | solution.py:527
  83.2 1.4 copy-start.2
  83.2 1.4 collective-permute-start.7
  83.2 1.4 copy-start.3
  83.2 2.7 %collective-permute-start.8 = (bf16[3,6,32,128]{3,2,1,0:T(8,128)(2,1)S(1)}, bf16[3,6,32,128]{3,2,1,0:T(8,128)(2,1)}, u32[]{:S(2)}, u32[]{:S(2)}) collective-permute-start(bf16[3,6,32,128]{3,2,1,0:T(8,128)(2,1)S(1)} %collective-permute-done.5.refs_7_.refs_3_), channel_id=1, source_target_pairs={{0,1},{1,0},{2,3},{3,2},{4,5},{5,4},{6,7},{7,6},{8,9},{9,8},{10,11... | collective-permute-start | bytes 442376 | tf_op jit(solution)/shard_map/ppermute | solution.py:527
  84.6 1.3 copy-start.4
  84.6 31.4 %collective-permute-start.1 = (bf16[1,6,288,128]{3,2,1,0:T(8,128)(2,1)}, bf16[1,6,288,128]{3,2,1,0:T(8,128)(2,1)}, u32[]{:S(2)}, u32[]{:S(2)}) collective-permute-start(bf16[1,6,288,128]{3,2,1,0:T(8,128)(2,1)} %get-tuple-element.26), channel_id=1, source_target_pairs={{0,64},{32,96},{64,0},{96,32},{1,65},{33,97},{65,1},{97,33},{2,66}... | collective-permute-start | bytes 1327112 | tf_op jit(solution)/shard_map/ppermute | solution.py:122
  85.9 82.7 %collective-permute-start.10 = (bf16[4,2,2,288,128]{4,3,2,1,0:T(8,128)(2,1)}, bf16[4,2,2,288,128]{4,3,2,1,0:T(8,128)(2,1)}, u32[]{:S(2)}, u32[]{:S(2)}) collective-permute-start(bf16[4,2,2,288,128]{4,3,2,1,0:T(8,128)(2,1)} %all-to-all-done.refs_13_.refs_8_), channel_id=1, source_target_pairs={{1,0},{2,1},{3,2},{4,3},{5,4},{6,5},{7,6},{8,7},{9,8},{10,9},{11,1... | collective-permute-start | bytes 3538952 | tf_op jit(solution)/shard_map/ppermute | solution.py:137
  87.2 81.4 %collective-permute-start.9 = (bf16[4,2,2,288,128]{4,3,2,1,0:T(8,128)(2,1)}, bf16[4,2,2,288,128]{4,3,2,1,0:T(8,128)(2,1)}, u32[]{:S(2)}, u32[]{:S(2)}) collective-permute-start(bf16[4,2,2,288,128]{4,3,2,1,0:T(8,128)(2,1)} %all-to-all-done.refs_13_.refs_8_), channel_id=1, source_target_pairs={{0,1},{1,2},{2,3},{3,4},{4,5},{5,6},{6,7},{7,8},{8,9},{9,10},{10,1... | collective-permute-start | bytes 3538952 | tf_op jit(solution)/shard_map/ppermute | solution.py:137
  104.3 24.4 %all-to-all-start.2 = ((bf16[128,16,128]{2,1,0:T(8,128)(2,1)}), bf16[128,16,128]{2,1,0:T(8,128)(2,1)}, u32[]{:S(2)}, u32[]{:S(2)}) async-start(bf16[128,16,128]{2,1,0:T(8,128)(2,1)} %text_attention.1), calls=%async_computation.2 | async-start | bytes 1048576 | tf_op jit(solution)/shard_map/all_to_all | solution.py:133
  116.0 21.6 %collective-permute-start.2 = (bf16[1,6,288,128]{3,2,1,0:T(8,128)(2,1)}, bf16[1,6,288,128]{3,2,1,0:T(8,128)(2,1)}, u32[]{:S(2)}, u32[]{:S(2)}) collective-permute-start(bf16[1,6,288,128]{3,2,1,0:T(8,128)(2,1)} %get-tuple-element.27), channel_id=1, source_target_pairs={{0,96},{32,0},{64,32},{96,64},{1,97},{33,1},{65,33},{97,65},{2,98}... | collective-permute-start | bytes 1327112 | tf_op jit(solution)/shard_map/ppermute | solution.py:122
  131.8 55.2 %all-to-all-start.3 = ((bf16[128,16,128]{2,1,0:T(8,128)(2,1)}), bf16[128,16,128]{2,1,0:T(8,128)(2,1)}, u32[]{:S(2)}, u32[]{:S(2)}) async-start(bf16[128,16,128]{2,1,0:T(8,128)(2,1)} %bitcast.1), calls=%async_computation.3 | async-start | bytes 1048576 | tf_op jit(solution)/shard_map/all_to_all | solution.py:133
  163.6 20.9 %collective-permute-start.16 = (bf16[4,288,128]{2,1,0:T(8,128)(2,1)}, bf16[4,288,128]{2,1,0:T(8,128)(2,1)}, u32[]{:S(2)}, u32[]{:S(2)}) collective-permute-start(bf16[4,288,128]{2,1,0:T(8,128)(2,1)} %get-tuple-element.39), channel_id=1, source_target_pairs={{0,32},{32,64},{64,96},{96,0},{1,33},{33,65},{65,97},{97,1},{2,34}... | collective-permute-start | bytes 884744 | tf_op jit(solution)/shard_map/ppermute | solution.py:122
  164.4 22.5 %collective-permute-start.17 = (bf16[4,288,128]{2,1,0:T(8,128)(2,1)}, bf16[4,288,128]{2,1,0:T(8,128)(2,1)}, u32[]{:S(2)}, u32[]{:S(2)}) collective-permute-start(bf16[4,288,128]{2,1,0:T(8,128)(2,1)} %get-tuple-element.40), channel_id=1, source_target_pairs={{0,64},{32,96},{64,0},{96,32},{1,65},{33,97},{65,1},{97,33},{2,66}... | collective-permute-start | bytes 884744 | tf_op jit(solution)/shard_map/ppermute | solution.py:122
  167.1 19.8 %collective-permute-start.18 = (bf16[4,288,128]{2,1,0:T(8,128)(2,1)}, bf16[4,288,128]{2,1,0:T(8,128)(2,1)}, u32[]{:S(2)}, u32[]{:S(2)}) collective-permute-start(bf16[4,288,128]{2,1,0:T(8,128)(2,1)} %get-tuple-element.41), channel_id=1, source_target_pairs={{0,96},{32,0},{64,32},{96,64},{1,97},{33,1},{65,33},{97,65},{2,98}... | collective-permute-start | bytes 884744 | tf_op jit(solution)/shard_map/ppermute | solution.py:122
  183.0 9.8 %collective-permute-start.11 = (bf16[2,288,128]{2,1,0:T(8,128)(2,1)}, bf16[2,288,128]{2,1,0:T(8,128)(2,1)}, u32[]{:S(2)}, u32[]{:S(2)}) collective-permute-start(bf16[2,288,128]{2,1,0:T(8,128)(2,1)} %get-tuple-element.35), channel_id=1, source_target_pairs={{0,32},{32,64},{64,96},{96,0},{1,33},{33,65},{65,97},{97,1},{2,34}... | collective-permute-start | bytes 442376 | tf_op jit(solution)/shard_map/ppermute | solution.py:122
  183.6 9.1 %collective-permute-start.12 = (bf16[2,288,128]{2,1,0:T(8,128)(2,1)}, bf16[2,288,128]{2,1,0:T(8,128)(2,1)}, u32[]{:S(2)}, u32[]{:S(2)}) collective-permute-start(bf16[2,288,128]{2,1,0:T(8,128)(2,1)} %get-tuple-element.36), channel_id=1, source_target_pairs={{0,64},{32,96},{64,0},{96,32},{1,65},{33,97},{65,1},{97,33},{2,66}... | collective-permute-start | bytes 442376 | tf_op jit(solution)/shard_map/ppermute | solution.py:122
  184.5 8.9 %collective-permute-start.13 = (bf16[2,288,128]{2,1,0:T(8,128)(2,1)}, bf16[2,288,128]{2,1,0:T(8,128)(2,1)}, u32[]{:S(2)}, u32[]{:S(2)}) collective-permute-start(bf16[2,288,128]{2,1,0:T(8,128)(2,1)} %get-tuple-element.37), channel_id=1, source_target_pairs={{0,96},{32,0},{64,32},{96,64},{1,97},{33,1},{65,33},{97,65},{2,98}... | collective-permute-start | bytes 442376 | tf_op jit(solution)/shard_map/ppermute | solution.py:122

commit v5 on v3

--- a/solution.py
+++ b/solution.py
@@ -25,11 +25,13 @@
 KEYS = 2 * SLICE + TXT
 SCALE = math.log2(math.e) / math.sqrt(D)
 CHUNKS = ((0, 4), (4, 2))
+LIMIT = 67043328
 BF = jnp.bfloat16
 F32 = jnp.float32
 
 
-HBM = pl.BlockSpec(memory_space=pltpu.HBM)
+ANY = pl.BlockSpec(memory_space=pl.ANY)
+PARAMS = pltpu.CompilerParams(vmem_limit_bytes=LIMIT)
 SMEM = pl.BlockSpec(memory_space=pltpu.SMEM)
 VMEM = pl.BlockSpec(memory_space=pltpu.VMEM)
 
@@ -102,11 +104,12 @@
 
     got = pl.pallas_call(
         body,
-        in_specs=[HBM] * len(arrays),
-        out_specs=[HBM] * len(outs),
+        in_specs=[ANY] * len(arrays),
+        out_specs=[ANY] * len(outs),
         out_shape=outs,
         scratch_shapes=[pltpu.VMEM(o.shape, BF) for o in outs]
         + [pltpu.SemaphoreType.DMA((160,)), pltpu.SemaphoreType.DMA((32,))],
+        compiler_params=PARAMS,
     )(*arrays)
     result, n = [], 0
     for job in jobs:
@@ -145,22 +148,24 @@
 
 def weigh(q, keys, values, masked):
     s = lax.dot_general(q, keys(), (((1,), (1,)), ((), ())), preferred_element_type=F32)
-    return s, lambda: finish(s, values, masked)
-
-
-def finish(s, values, masked):
-    parts, at = [], 0
-    for start, bias in masked:
-        parts += [s[:, at:start], s[:, start : start + TXT] + bias]
-        at = start + TXT
-    if at < s.shape[1]:
-        parts.append(s[:, at:])
-    s = jnp.concatenate([p for p in parts if p.shape[1]], axis=1)
-    top = jnp.max(s, axis=1, keepdims=True)
-    p = jnp.exp2(s * SCALE - top * SCALE)
-    total = jnp.sum(p, axis=1, keepdims=True)
-    o = jnp.dot(p.astype(BF), values(), preferred_element_type=F32)
-    return o / total, top * SCALE + jnp.log2(total)
+
+    def finish():
+        parts, at = [], 0
+        for start, bias in masked:
+            if start > at:
+                parts.append(s[:, at:start])
+            parts.append(s[:, start : start + TXT] + bias)
+            at = start + TXT
+        if at < s.shape[1]:
+            parts.append(s[:, at:])
+        whole = jnp.concatenate(parts, axis=1)
+        top = jnp.max(whole, axis=1, keepdims=True) * SCALE
+        p = jnp.exp2(whole * SCALE - top)
+        total = jnp.sum(p, axis=1, keepdims=True)
+        o = jnp.dot(p.astype(BF), values(), preferred_element_type=F32)
+        return o / total, top + jnp.log2(total)
+
+    return finish
 
 
 SLOT = 16
@@ -172,7 +177,8 @@
     out_ref, q_sc, kv_sc, o_sc, log_sc, sc, slots, sems = refs
     pairs = []
     for n, piece in enumerate(text):
-        pairs.append((piece.at[0], q_sc.at[:, rows_of(2 * place(-(n % GROUP)) + half(n // GROUP), HALF)]))
+        rows = rows_of(2 * place(-(n % GROUP)) + half(n // GROUP), HALF)
+        pairs.append((piece.at[0], q_sc.at[:, rows]))
         pairs.append((piece.at[pl.ds(1, 2)], kv_sc.at[:, :, pl.ds(SLICE + n * HALF, HALF)]))
     for c, (first, heads) in enumerate(CHUNKS):
         for g in range(GROUP):
@@ -186,7 +192,7 @@
 
     def begin(h, i):
         q = q_sc[h, i * RB : (i + 1) * RB]
-        return weigh(q, lambda: kv_sc[0, h], lambda: kv_sc[1, h], [(SLICE, bias)])[1]
+        return weigh(q, lambda: kv_sc[0, h], lambda: kv_sc[1, h], [(SLICE, bias)])
 
     rest = begin(*steps[0])
     for n, (h, i) in enumerate(steps):
@@ -223,8 +229,8 @@
 def text_attention(length, text, kv):
     return pl.pallas_call(
         text_body,
-        in_specs=[SMEM] + [HBM] * (2 * GROUP + len(CHUNKS)),
-        out_specs=HBM,
+        in_specs=[SMEM] + [ANY] * (2 * GROUP + len(CHUNKS)),
+        out_specs=ANY,
         out_shape=jax.ShapeDtypeStruct((DEVS, SLOT, D), BF),
         scratch_shapes=[
             pltpu.VMEM((HD, TXT, D), BF),
@@ -235,12 +241,14 @@
             pltpu.VMEM((DEVS, SLOT, D), BF),
             pltpu.SemaphoreType.DMA((32,)),
         ],
+        compiler_params=PARAMS,
         name="text_attention",
     )(length, *text, *kv)
 
 
-def combine_body(in_ref, out_ref, sc, res, slots, sems):
-    sc[...] = in_ref[...].astype(F32).reshape(DEVS * SLOT, D)
+def combine_body(in_ref, out_ref, sc, res, slots, got, sems):
+    leave(in_ref, got, sems)
+    sc[...] = got[...].astype(F32).reshape(DEVS * SLOT, D)
     logs = sc[pl.ds(PAIRS, DEVS, stride=SLOT), :]
     for part in range(1, 3):
         logs = logs + sc[pl.ds(PAIRS + part, DEVS, stride=SLOT), :]
@@ -275,15 +283,17 @@
 def combine(received):
     return pl.pallas_call(
         combine_body,
-        in_specs=[VMEM],
-        out_specs=HBM,
+        in_specs=[ANY],
+        out_specs=ANY,
         out_shape=jax.ShapeDtypeStruct((BLK, GROUP, SLOT, D), BF),
         scratch_shapes=[
             pltpu.VMEM((DEVS * SLOT, D), F32),
             pltpu.VMEM((GROUP, SLOT, D), F32),
             pltpu.VMEM((BLK, GROUP, SLOT, D), BF),
+            pltpu.VMEM((DEVS, SLOT, D), BF),
             pltpu.SemaphoreType.DMA((4,)),
         ],
+        compiler_params=PARAMS,
         name="combine",
     )(received).reshape(DEVS, SLOT, D)
 
@@ -292,24 +302,27 @@
     q_refs, text, refs = refs[:GROUP], refs[GROUP : 3 * GROUP], refs[3 * GROUP :]
     before, own, after, refs = refs[0], refs[1], refs[2], refs[3:]
     o_refs, refs = refs[:GROUP], refs[GROUP:]
-    q_sc, k_sc, v_sc, o_sc, side_sc, sems, o_sems = refs
-
-    def loads(start, count, slot):
-        some = pl.ds(start, count)
-        parts = []
-        for a, sc in ((0, k_sc), (1, v_sc)):
-            pairs = []
-            for base, kv in ((0, before), (SLICE, own), (KEYS, after)):
-                for g in range(GROUP):
-                    pairs.append((kv.at[g, a, some], sc.at[some, pl.ds(base + g * ROWS, ROWS)]))
-            for n, piece in enumerate(text):
-                rows = pl.ds(2 * SLICE + n * HALF, HALF)
-                pairs.append((piece.at[1 + a, pl.ds(first + start, count)], sc.at[some, rows]))
-            parts.append(pairs)
-        asked = pl.ds(first + start, count)
-        queries = [(q_refs[d].at[0, asked], q_sc.at[some, rows_of(place(-d), ROWS)]) for d in range(GROUP)]
-        pairs = queries + parts[0] + parts[1]
-        return copy_list(pairs, sems.at[slot]), len(queries + parts[0])
+    q_sc, k_sc, v_sc, o_sc, side_sc, sems, shared_sems, o_sems = refs
+
+    def loads(start, count, a):
+        some, pairs = pl.ds(start, count), []
+        for base, kv in ((0, before), (SLICE, own), (KEYS, after)):
+            for g in range(GROUP):
+                pairs.append((kv.at[g, a, some], (k_sc, v_sc)[a].at[some, pl.ds(base + g * ROWS, ROWS)]))
+        return copy_list(pairs, sems.at[min(start, 1), a])
+
+    others = loads(1, heads - 1, 0) + loads(1, heads - 1, 1)
+    asked = pl.ds(first, heads)
+    shared = [[(q_refs[d].at[0, asked], q_sc.at[:, rows_of(place(-d), ROWS)]) for d in range(GROUP)], []]
+    for a, sc in ((0, k_sc), (1, v_sc)):
+        for n, piece in enumerate(text):
+            shared[a].append((piece.at[1 + a, asked], sc.at[:, pl.ds(2 * SLICE + n * HALF, HALF)]))
+    shared = [copy_list(pairs, shared_sems.at[a]) for a, pairs in enumerate(shared)]
+    run(loads(0, 1, 0))
+    run(shared[0])
+    run(loads(0, 1, 1))
+    run(shared[1])
+    run(others)
 
     def stores(h):
         return [
@@ -317,10 +330,6 @@
             for d in range(GROUP)
         ]
 
-    head, keys_only = loads(0, 1, 0)
-    others, _ = loads(1, heads - 1, 1)
-    run(head)
-    run(others)
     limit = (lax.axis_index("blk") + 1) * tiles.shape[0]
     for j in range(tiles.shape[0]):
         last = tiles[j, 0]
@@ -334,10 +343,10 @@
         window = pl.ds(pl.multiple_of(f * SLICE, RB), KEYS)
         masked = [(SLICE, jnp.where(f == 1, live, 0.0)), (2 * SLICE, jnp.where(f == 1, 0.0, live))]
         q = q_sc[h, i * RB : (i + 1) * RB, :]
-        return weigh(q, lambda: k_sc[h, window], lambda: v_sc[h, window], masked)[1]
+        return weigh(q, lambda: k_sc[h, window], lambda: v_sc[h, window], masked)
 
     steps = SLICE // RB
-    wait(head[:keys_only])
+    wait(loads(0, 1, 0) + shared[0])
 
     def one(h, _):
         @pl.when(h == 1)
@@ -348,7 +357,7 @@
 
         @pl.when(h == 0)
         def _():
-            wait(head[keys_only:])
+            wait(loads(0, 1, 1) + shared[1])
 
         for i in range(steps):
             following = step(h, i + 1) if i + 1 < steps else None
@@ -366,8 +375,8 @@
 def video_attention(first, heads, tiles, length, q, text, before, own, after):
     return pl.pallas_call(
         functools.partial(video_body, first, heads),
-        in_specs=[SMEM, SMEM] + [HBM] * (3 * GROUP + 3),
-        out_specs=[HBM] * GROUP,
+        in_specs=[SMEM, SMEM] + [ANY] * (3 * GROUP + 3),
+        out_specs=[ANY] * GROUP,
         out_shape=[jax.ShapeDtypeStruct((heads, ROWS, D), BF)] * GROUP,
         scratch_shapes=[
             pltpu.VMEM((heads, SLICE, D), BF),
@@ -375,9 +384,11 @@
             pltpu.VMEM((heads, KEYS + SLICE, D), BF),
             pltpu.VMEM((heads, SLICE, D), BF),
             pltpu.SMEM((8,), jnp.int32),
-            pltpu.SemaphoreType.DMA((2, 48)),
+            pltpu.SemaphoreType.DMA((2, 2, 12)),
+            pltpu.SemaphoreType.DMA((2, 12)),
             pltpu.SemaphoreType.DMA((heads, GROUP)),
         ],
+        compiler_params=PARAMS,
         name="video_attention",
     )(tiles, length, *q, *text, before, own, after)
 
@@ -400,9 +411,10 @@
 
 
 def first_body(first, heads, *refs):
-    pieces, slots, video_out, text_out, held, sc, in_sems, out_sems = refs[:GROUP], *refs[GROUP:]
+    pieces, slots, video_out, text_out, held, sc, got, in_sems, out_sems, sems = refs[:GROUP], *refs[GROUP:]
     writes = rows_body(first, heads, *pieces, video_out, held, in_sems, out_sems)
-    sc[...] = slots[...].astype(F32).reshape(DEVS * SLOT, D)
+    leave(slots, got, sems)
+    sc[...] = got[...].astype(F32).reshape(DEVS * SLOT, D)
     for p in range(2):
         for u in range(GROUP):
             for i in range(3):
@@ -419,8 +431,8 @@
 def first_rows(pieces, slots, first, heads):
     return pl.pallas_call(
         functools.partial(first_body, first, heads),
-        in_specs=[HBM] * GROUP + [VMEM],
-        out_specs=[HBM, VMEM],
+        in_specs=[ANY] * (GROUP + 1),
+        out_specs=[ANY, VMEM],
         out_shape=[
             jax.ShapeDtypeStruct((ROWS, HEADS * D), BF),
             jax.ShapeDtypeStruct((TROWS, HEADS * D), BF),
@@ -428,9 +440,12 @@
         scratch_shapes=[
             pltpu.VMEM((GROUP * heads, ROWS, D), BF),
             pltpu.VMEM((DEVS * SLOT, D), F32),
+            pltpu.VMEM((DEVS, SLOT, D), BF),
             pltpu.SemaphoreType.DMA((GROUP * heads,)),
             pltpu.SemaphoreType.DMA((GROUP * heads,)),
-        ],
+            pltpu.SemaphoreType.DMA((4,)),
+        ],
+        compiler_params=PARAMS,
         name="first_rows",
     )(*pieces, slots)
 
@@ -438,8 +453,8 @@
 def later_rows(pieces, rows, first, heads):
     return pl.pallas_call(
         functools.partial(later_body, first, heads),
-        in_specs=[HBM] * (GROUP + 1),
-        out_specs=HBM,
+        in_specs=[ANY] * (GROUP + 1),
+        out_specs=ANY,
         out_shape=jax.ShapeDtypeStruct((ROWS, HEADS * D), BF),
         scratch_shapes=[
             pltpu.VMEM((GROUP * heads, ROWS, D), BF),
@@ -447,6 +462,7 @@
             pltpu.SemaphoreType.DMA((GROUP * heads,)),
         ],
         input_output_aliases={GROUP: 0},
+        compiler_params=PARAMS,
         name="later_rows",
     )(*pieces, rows)
 

time: 184 us -> 185 us (level)
  transfers between devices with their start and end apart: 22 -> 22, of which waited for: 7 -> 7; matrix products, arithmetic and copies ran while one was open for 0% -> 0% of each run, Pallas kernels for 29% -> 30%
where the time goes in v5:
time: 185 us
  Pallas kernels  60.8 us (33%)
  starting transfers between devices  50.6 us (27%)
  waiting for transfers between devices  37.5 us (20%)
  blocking collectives  33.8 us (18%)
    pallas_call x2, Pallas kernels, video_attention(): pl.pallas_call(functools.partial(video_body, first, heads), in_specs=[SME...  34.1 us
    all_to_all x1, blocking collectives, swap(): return lax.all_to_all(array, axes, 0, 0, tiled=True)  33.8 us
    ppermute x12, waiting for transfers between devices, around(): lax.ppermute(block, 'uly', [(i, (i + distance) % GROUP) for i in range(GR...  26.1 us
    all_to_all x3, starting transfers between devices, swap(): return lax.all_to_all(array, axes, 0, 0, tiled=True)  21.8 us
    ppermute x12, starting transfers between devices, around(): lax.ppermute(block, 'uly', [(i, (i + distance) % GROUP) for i in range(GR...  17.1 us
    ppermute x4, starting transfers between devices, beside(): lax.ppermute(block, 'blk', [(i, i + distance) for i in range(BLK) if 0 <=...  11.2 us
    all_to_all x3, waiting for transfers between devices, swap(): return lax.all_to_all(array, axes, 0, 0, tiled=True)  10.6 us
    pallas_call x2, Pallas kernels, pack(): pl.pallas_call(body, in_specs=[ANY] * len(arrays), out_specs=[ANY] * len(...  9.81 us
  transfers between devices with their start and end apart: 22, of which 7 were waited for; matrix products, arithmetic and copies ran while one was open for 0% of the time, Pallas kernels for 30%

profile of v5, /device:TPU:0, one launch (start us, length us, event | category | flops | bytes accessed | tf_op | source)
XLA Modules:
  0.0 184.5 jit_solution(964996799194247830)
XLA Ops:
  0.6 4.3 %shard_map.96 = bf16[4,2,4,288,128]{4,3,2,1,0:T(8,128)(2,1)} custom-call(bf16[288,3072]{1,0:T(8,128)(2,1)} %refs_0_.3, bf16[288,3072]{1,0:T(8,128)(2,1)} %refs_1_.3, bf16[288,3072]{1,0:T(8,128)(2,1)} %refs_2_.3), custom_call_target="tpu_custom_call" | custom-call | tf_op jit(solution)/shard_map/pallas_call | solution.py:105
  5.0 33.8 %all_to_all.20.refs_13_.refs_8_ = bf16[4,2,4,288,128]{4,3,2,1,0:T(8,128)(2,1)} all-to-all(bf16[4,2,4,288,128]{4,3,2,1,0:T(8,128)(2,1)} %shard_map.96), channel_id=1, replica_groups=mesh['uly'=4,'blk'=32] {'uly'}, dimensions={0} | all-to-all | bytes 4718592 | tf_op jit(solution)/shard_map/all_to_all | solution.py:134
  38.8 1.3 collective-permute-start.15
  40.1 4.5 %collective-permute-start.14 = (bf16[4,2,4,288,128]{4,3,2,1,0:T(8,128)(2,1)}, bf16[4,2,4,288,128]{4,3,2,1,0:T(8,128)(2,1)}, u32[]{:S(2)}, u32[]{:S(2)}) collective-permute-start(bf16[4,2,4,288,128]{4,3,2,1,0:T(8,128)(2,1)} %all_to_all.20.refs_13_.refs_8_), channel_id=1, source_target_pairs={{0,1},{1,2},{2,3},{3,4},{4,5},{5,6},{6,7},{7,8},{8,9},{9,10},{10,1... | collective-permute-start | bytes 7077896 | tf_op jit(solution)/shard_map/ppermute | solution.py:138
  44.5 5.5 %shard_map.95 = (bf16[3,6,32,128]{3,2,1,0:T(8,128)(2,1)}, bf16[3,6,32,128]{3,2,1,0:T(8,128)(2,1)}, bf16[3,6,32,128]{3,2,1,0:T(8,128)(2,1)}, bf16[3,6,32,128]{3,2...) custom-call(bf16[288,3072]{1,0:T(8,128)(2,1)} %refs_0_.3, ...), custom_call_target="tpu_custom_call" | custom-call | tf_op jit(solution)/shard_map/pallas_call | solution.py:105
  50.0 0.0 copy-start.8
  50.0 0.0 copy-start.7
  50.1 0.0 copy-start.5
  50.1 0.0 copy-start.6
  50.1 4.4 %all-to-all-start = ((bf16[4,2,2,288,128]{4,3,2,1,0:T(8,128)(2,1)}), bf16[4,2,2,288,128]{4,3,2,1,0:T(8,128)(2,1)}, u32[]{:S(2)}, u32[]{:S(2)}) async-start(bf16[4,2,2,288,128]{4,3,2,1,0:T(8,128)(2,1)} %get-tuple-element.31), calls=%async_computation | async-start | bytes 2359296 | tf_op jit(solution)/shard_map/all_to_all | solution.py:134
  54.5 0.0 copy-done.8
  54.5 2.0 %collective-permute-start.3 = (bf16[3,6,32,128]{3,2,1,0:T(8,128)(2,1)S(1)}, bf16[3,6,32,128]{3,2,1,0:T(8,128)(2,1)S(1)}, u32[]{:S(2)}, u32[]{:S(2)}) collective-permute-start(bf16[3,6,32,128]{3,2,1,0:T(8,128)(2,1)S(1)} %copy-done.8), channel_id=1, source_target_pairs={{0,32},{32,64},{64,96},{96,0},{1,33},{33,65},{65,97},{97,1},{2,34}... | collective-permute-start | bytes 442376 | tf_op jit(solution)/shard_map/ppermute | solution.py:123
  56.5 0.0 copy-done.7
  56.5 2.7 %collective-permute-start.4 = (bf16[3,6,32,128]{3,2,1,0:T(8,128)(2,1)S(1)}, bf16[3,6,32,128]{3,2,1,0:T(8,128)(2,1)S(1)}, u32[]{:S(2)}, u32[]{:S(2)}) collective-permute-start(bf16[3,6,32,128]{3,2,1,0:T(8,128)(2,1)S(1)} %copy-done.7), channel_id=1, source_target_pairs={{0,64},{32,96},{64,0},{96,32},{1,65},{33,97},{65,1},{97,33},{2,66}... | collective-permute-start | bytes 442376 | tf_op jit(solution)/shard_map/ppermute | solution.py:123
  59.1 0.0 copy-done.5
  59.1 0.0 collective-permute-start
  59.2 18.8 %collective-permute-done.3.refs_5_.refs_1_ = bf16[3,6,32,128]{3,2,1,0:T(8,128)(2,1)S(1)} collective-permute-done((bf16[3,6,32,128]{3,2,1,0:T(8,128)(2,1)S(1)}, bf16[3,6,32,128]{3,2,1,0:T(8,128)(2,1)S(1)}, u32[]{:S(2)}, u32[]{:S(2)}) %collective-permute-start.3) | collective-permute-done | bytes 147488 | tf_op jit(solution)/shard_map/ppermute | solution.py:123
  78.0 0.0 copy-done.6
  78.0 0.0 collective-permute-start.5
  78.0 0.8 collective-permute-done.4.refs_6_.refs_2_
  78.8 0.0 copy-done
  78.8 0.0 collective-permute-start.6
  78.8 4.4 %collective-permute-done.5.refs_7_.refs_3_ = bf16[3,6,32,128]{3,2,1,0:T(8,128)(2,1)S(1)} collective-permute-done((bf16[3,6,32,128]{3,2,1,0:T(8,128)(2,1)S(1)}, bf16[3,6,32,128]{3,2,1,0:T(8,128)(2,1)S(1)}, u32[]{:S(2)}, u32[]{:S(2)}) %collective-permute-start.5) | collective-permute-done | bytes 147488 | tf_op jit(solution)/shard_map/ppermute | solution.py:123
  83.1 0.0 collective-permute-start.7
  83.1 0.0 collective-permute-done.6.refs_9_.refs_5_
  83.1 0.0 copy-done.1
  83.2 0.0 copy-start.3
  83.2 0.6 collective-permute-start.8
  83.7 0.8 collective-permute-done.7.refs_10_.refs_6_
  84.5 1.3 collective-permute-start.1
  85.8 0.0 collective-permute-done.8.refs_11_.refs_7_
  85.8 0.0 all-to-all-done.refs_13_.refs_9_
  85.8 1.3 collective-permute-start.10
  87.1 0.0 collective-permute-done.refs_1_
  87.2 4.1 %collective-permute-start.9 = (bf16[4,2,2,288,128]{4,3,2,1,0:T(8,128)(2,1)}, bf16[4,2,2,288,128]{4,3,2,1,0:T(8,128)(2,1)}, u32[]{:S(2)}, u32[]{:S(2)}) collective-permute-start(bf16[4,2,2,288,128]{4,3,2,1,0:T(8,128)(2,1)} %all-to-all-done.refs_13_.refs_9_), channel_id=1, source_target_pairs={{0,1},{1,2},{2,3},{3,4},{4,5},{5,6},{6,7},{7,8},{8,9},{9,10},{10,1... | collective-permute-start | bytes 3538952 | tf_op jit(solution)/shard_map/ppermute | solution.py:138
  91.9 7.8 %text_attention.1 = bf16[128,16,128]{2,1,0:T(8,128)(2,1)} custom-call(s32[1]{0:T(128)S(6)} %copy.12.length, bf16[3,6,32,128]{3,2,1,0:T(8,128)(2,1)} %get-tuple-element.26.refs_4_.refs_0_, bf16[3,6,32,128]{3,2,1,0:T(8,128)(2,1)} %copy-done, bf16[3,6,32,128]{3,2,1,0:T(8,128)(2,1)} %copy-done.1, bf16[3,6,32,128]{3,2,1,0:T(8,128)(2,1)} %copy-done.2, ...), custom_call_target="tpu_custom_call" | custom-call | tf_op jit(solution)/shard_map/text_attention/pallas_call | solution.py:230
  99.8 11.5 %all-to-all-start.2 = ((bf16[128,16,128]{2,1,0:T(8,128)(2,1)}), bf16[128,16,128]{2,1,0:T(8,128)(2,1)}, u32[]{:S(2)}, u32[]{:S(2)}) async-start(bf16[128,16,128]{2,1,0:T(8,128)(2,1)} %text_attention.1), calls=%async_computation.2 | async-start | bytes 1048576 | tf_op jit(solution)/shard_map/all_to_all | solution.py:134
  111.3 0.0 collective-permute-done.1.refs_2_
  111.3 2.2 %collective-permute-start.2 = (bf16[1,6,288,128]{3,2,1,0:T(8,128)(2,1)}, bf16[1,6,288,128]{3,2,1,0:T(8,128)(2,1)}, u32[]{:S(2)}, u32[]{:S(2)}) collective-permute-start(bf16[1,6,288,128]{3,2,1,0:T(8,128)(2,1)} %get-tuple-element.25), channel_id=1, source_target_pairs={{0,96},{32,0},{64,32},{96,64},{1,97},{33,1},{65,33},{97,65},{2,98}... | collective-permute-start | bytes 1327112 | tf_op jit(solution)/shard_map/ppermute | solution.py:123
  113.5 10.6 %all-to-all-done.2.in_ref = bf16[128,16,128]{2,1,0:T(8,128)(2,1)} async-done(((bf16[128,16,128]{2,1,0:T(8,128)(2,1)}), bf16[128,16,128]{2,1,0:T(8,128)(2,1)}, u32[]{:S(2)}, u32[]{:S(2)}) %all-to-all-start.2) | async-done | bytes 524320 | tf_op jit(solution)/shard_map/all_to_all | solution.py:134
  124.1 3.0 %combine.1 = bf16[32,4,16,128]{3,2,1,0:T(8,128)(2,1)} custom-call(bf16[128,16,128]{2,1,0:T(8,128)(2,1)} %all-to-all-done.2.in_ref), custom_call_target="tpu_custom_call" | custom-call | tf_op jit(solution)/shard_map/combine/pallas_call | solution.py:284
  127.1 5.9 %all-to-all-start.3 = ((bf16[128,16,128]{2,1,0:T(8,128)(2,1)}), bf16[128,16,128]{2,1,0:T(8,128)(2,1)}, u32[]{:S(2)}, u32[]{:S(2)}) async-start(bf16[128,16,128]{2,1,0:T(8,128)(2,1)} %bitcast.1), calls=%async_computation.3 | async-start | bytes 1048576 | tf_op jit(solution)/shard_map/all_to_all | solution.py:134
  133.0 0.0 collective-permute-done.2.refs_3_
  133.0 0.0 collective-permute-done.15.refs_14_
  133.1 0.0 collective-permute-done.14.refs_12_
  133.1 21.8 %video_attention.3 = (bf16[4,288,128]{2,1,0:T(8,128)(2,1)}, bf16[4,288,128]{2,1,0:T(8,128)(2,1)}, bf16[4,288,128]{2,1,0:T(8,128)(2,1)}, bf16[4,288,128]{2,1,0:T(8,128)(2,1)}) custom-call(s32[3,6]{1,0:T(4,128)} %tiles.3, s32[1]{0:T(128)S(6)} %copy.12.length, bf16[1,6,288,128]{3,2,1,0:T(8,128)(2,1)} %get-tuple-element.22.refs_0_, ...), custom_call_target="tpu_custom_call" | custom-call | tf_op jit(solution)/shard_map/video_attention/pallas_call | solution.py:376
  154.8 0.7 collective-permute-start.16
  155.5 2.7 %collective-permute-start.17 = (bf16[4,288,128]{2,1,0:T(8,128)(2,1)}, bf16[4,288,128]{2,1,0:T(8,128)(2,1)}, u32[]{:S(2)}, u32[]{:S(2)}) collective-permute-start(bf16[4,288,128]{2,1,0:T(8,128)(2,1)} %get-tuple-element.38), channel_id=1, source_target_pairs={{0,64},{32,96},{64,0},{96,32},{1,65},{33,97},{65,1},{97,33},{2,66}... | collective-permute-start | bytes 884744 | tf_op jit(solution)/shard_map/ppermute | solution.py:123
  158.2 1.4 collective-permute-start.18
  159.7 0.0 collective-permute-done.10.refs_14_
  159.7 0.0 collective-permute-done.9.refs_12_
  159.7 12.3 %video_attention.2 = (bf16[2,288,128]{2,1,0:T(8,128)(2,1)}, bf16[2,288,128]{2,1,0:T(8,128)(2,1)}, bf16[2,288,128]{2,1,0:T(8,128)(2,1)}, bf16[2,288,128]{2,1,0:T(8,128)(2,1)}) custom-call(s32[3,6]{1,0:T(4,128)} %tiles.3, s32[1]{0:T(128)S(6)} %copy.12.length, bf16[1,6,288,128]{3,2,1,0:T(8,128)(2,1)} %get-tuple-element.22.refs_0_, ...), custom_call_target="tpu_custom_call" | custom-call | tf_op jit(solution)/shard_map/video_attention/pallas_call | solution.py:376
  172.0 0.6 collective-permute-start.11
  172.7 0.9 collective-permute-start.12
  173.6 0.0 collective-permute-done.16.refs_1_
  173.6 2.5 %collective-permute-start.13 = (bf16[2,288,128]{2,1,0:T(8,128)(2,1)}, bf16[2,288,128]{2,1,0:T(8,128)(2,1)}, u32[]{:S(2)}, u32[]{:S(2)}) collective-permute-start(bf16[2,288,128]{2,1,0:T(8,128)(2,1)} %get-tuple-element.35), channel_id=1, source_target_pairs={{0,96},{32,0},{64,32},{96,64},{1,97},{33,1},{65,33},{97,65},{2,98}... | collective-permute-start | bytes 442376 | tf_op jit(solution)/shard_map/ppermute | solution.py:123
  176.1 0.0 all-to-all-done.3.refs_4_
  176.2 0.0 collective-permute-done.17.refs_2_
  176.2 0.0 collective-permute-done.18.refs_3_
  176.2 4.1 %first_rows.1 = (bf16[288,3072]{1,0:T(8,128)(2,1)}, bf16[64,3072]{1,0:T(8,128)(2,1)}) custom-call(bf16[4,288,128]{2,1,0:T(8,128)(2,1)} %get-tuple-element.36.refs_0_, bf16[4,288,128]{2,1,0:T(8,128)(2,1)} %collective-permute-done.16.refs_1_, bf16[4,288,128]{2,1,0:T(8,128)(2,1)} %collective-permute-done.17.refs_2_, ...), custom_call_target="tpu_custom_call" | custom-call | tf_op jit(solution)/shard_map/first_rows/pallas_call | solution.py:432
  180.3 1.5 collective-permute-done.11.refs_1_
  181.8 0.0 collective-permute-done.12.refs_2_
  181.8 0.6 collective-permute-done.13.refs_3_
  182.4 1.9 %later_rows.1 = bf16[288,3072]{1,0:T(8,128)(2,1)} custom-call(bf16[2,288,128]{2,1,0:T(8,128)(2,1)} %get-tuple-element.32.refs_0_, bf16[2,288,128]{2,1,0:T(8,128)(2,1)} %collective-permute-done.11.refs_1_, bf16[2,288,128]{2,1,0:T(8,128)(2,1)} %collective-permute-done.12.refs_2_, ...), custom_call_target="tpu_custom_call", output_to_operand_aliasing={{}: (4, {})} | custom-call | tf_op jit(solution)/shard_map/later_rows/pallas_call | solution.py:454
  (7 shorter events, 0.0 us)
Async XLA Ops:
  38.8 94.3 %collective-permute-start.15 = (bf16[4,2,4,288,128]{4,3,2,1,0:T(8,128)(2,1)}, bf16[4,2,4,288,128]{4,3,2,1,0:T(8,128)(2,1)}, u32[]{:S(2)}, u32[]{:S(2)}) collective-permute-start(bf16[4,2,4,288,128]{4,3,2,1,0:T(8,128)(2,1)} %all_to_all.20.refs_13_.refs_8_), channel_id=1, source_target_pairs={{1,0},{2,1},{3,2},{4,3},{5,4},{6,5},{7,6},{8,7},{9,8},{10,9},{11,1... | collective-permute-start | bytes 7077896 | tf_op jit(solution)/shard_map/ppermute | solution.py:138
  40.1 93.0 %collective-permute-start.14 = (bf16[4,2,4,288,128]{4,3,2,1,0:T(8,128)(2,1)}, bf16[4,2,4,288,128]{4,3,2,1,0:T(8,128)(2,1)}, u32[]{:S(2)}, u32[]{:S(2)}) collective-permute-start(bf16[4,2,4,288,128]{4,3,2,1,0:T(8,128)(2,1)} %all_to_all.20.refs_13_.refs_8_), channel_id=1, source_target_pairs={{0,1},{1,2},{2,3},{3,4},{4,5},{5,6},{6,7},{7,8},{8,9},{9,10},{10,1... | collective-permute-start | bytes 7077896 | tf_op jit(solution)/shard_map/ppermute | solution.py:138
  50.0 4.5 %copy-start.8 = (bf16[3,6,32,128]{3,2,1,0:T(8,128)(2,1)S(1)}, bf16[3,6,32,128]{3,2,1,0:T(8,128)(2,1)}, u32[]{:S(2)}) copy-start(bf16[3,6,32,128]{3,2,1,0:T(8,128)(2,1)} %get-tuple-element.27) | copy-start | bytes 442372
  50.0 6.4 %copy-start.7 = (bf16[3,6,32,128]{3,2,1,0:T(8,128)(2,1)S(1)}, bf16[3,6,32,128]{3,2,1,0:T(8,128)(2,1)}, u32[]{:S(2)}) copy-start(bf16[3,6,32,128]{3,2,1,0:T(8,128)(2,1)} %get-tuple-element.28) | copy-start | bytes 442372
  50.1 9.1 %copy-start.5 = (bf16[1,6,288,128]{3,2,1,0:T(8,128)(2,1)S(1)}, bf16[1,6,288,128]{3,2,1,0:T(8,128)(2,1)}, u32[]{:S(2)}) copy-start(bf16[1,6,288,128]{3,2,1,0:T(8,128)(2,1)} %get-tuple-element.23) | copy-start | bytes 1327108
  50.1 27.9 %copy-start.6 = (bf16[3,6,32,128]{3,2,1,0:T(8,128)(2,1)S(1)}, bf16[3,6,32,128]{3,2,1,0:T(8,128)(2,1)}, u32[]{:S(2)}) copy-start(bf16[3,6,32,128]{3,2,1,0:T(8,128)(2,1)} %get-tuple-element.29) | copy-start | bytes 442372
  50.1 35.8 %all-to-all-start = ((bf16[4,2,2,288,128]{4,3,2,1,0:T(8,128)(2,1)}), bf16[4,2,2,288,128]{4,3,2,1,0:T(8,128)(2,1)}, u32[]{:S(2)}, u32[]{:S(2)}) async-start(bf16[4,2,2,288,128]{4,3,2,1,0:T(8,128)(2,1)} %get-tuple-element.31), calls=%async_computation | async-start | bytes 2359296 | tf_op jit(solution)/shard_map/all_to_all | solution.py:134
  54.5 23.5 %collective-permute-start.3 = (bf16[3,6,32,128]{3,2,1,0:T(8,128)(2,1)S(1)}, bf16[3,6,32,128]{3,2,1,0:T(8,128)(2,1)S(1)}, u32[]{:S(2)}, u32[]{:S(2)}) collective-permute-start(bf16[3,6,32,128]{3,2,1,0:T(8,128)(2,1)S(1)} %copy-done.8), channel_id=1, source_target_pairs={{0,32},{32,64},{64,96},{96,0},{1,33},{33,65},{65,97},{97,1},{2,34}... | collective-permute-start | bytes 442376 | tf_op jit(solution)/shard_map/ppermute | solution.py:123
  56.5 22.3 %collective-permute-start.4 = (bf16[3,6,32,128]{3,2,1,0:T(8,128)(2,1)S(1)}, bf16[3,6,32,128]{3,2,1,0:T(8,128)(2,1)S(1)}, u32[]{:S(2)}, u32[]{:S(2)}) collective-permute-start(bf16[3,6,32,128]{3,2,1,0:T(8,128)(2,1)S(1)} %copy-done.7), channel_id=1, source_target_pairs={{0,64},{32,96},{64,0},{96,32},{1,65},{33,97},{65,1},{97,33},{2,66}... | collective-permute-start | bytes 442376 | tf_op jit(solution)/shard_map/ppermute | solution.py:123
  59.1 28.0 %collective-permute-start = (bf16[1,6,288,128]{3,2,1,0:T(8,128)(2,1)S(1)}, bf16[1,6,288,128]{3,2,1,0:T(8,128)(2,1)}, u32[]{:S(2)}, u32[]{:S(2)}) collective-permute-start(bf16[1,6,288,128]{3,2,1,0:T(8,128)(2,1)S(1)} %copy-done.5), channel_id=1, source_target_pairs={{0,32},{32,64},{64,96},{96,0},{1,33},{33,65},{65,97},{97,1},{2,34}... | collective-permute-start | bytes 1327112 | tf_op jit(solution)/shard_map/ppermute | solution.py:123
  78.0 0.8 copy-start
  78.0 5.1 %collective-permute-start.5 = (bf16[3,6,32,128]{3,2,1,0:T(8,128)(2,1)S(1)}, bf16[3,6,32,128]{3,2,1,0:T(8,128)(2,1)S(1)}, u32[]{:S(2)}, u32[]{:S(2)}) collective-permute-start(bf16[3,6,32,128]{3,2,1,0:T(8,128)(2,1)S(1)} %copy-done.6), channel_id=1, source_target_pairs={{0,96},{32,0},{64,32},{96,64},{1,97},{33,1},{65,33},{97,65},{2,98}... | collective-permute-start | bytes 442376 | tf_op jit(solution)/shard_map/ppermute | solution.py:123
  78.8 4.4 %copy-start.1 = (bf16[3,6,32,128]{3,2,1,0:T(8,128)(2,1)}, bf16[3,6,32,128]{3,2,1,0:T(8,128)(2,1)S(1)}, u32[]{:S(2)}) copy-start(bf16[3,6,32,128]{3,2,1,0:T(8,128)(2,1)S(1)} %collective-permute-done.4.refs_6_.refs_2_) | copy-start | bytes 442372
  78.8 4.4 %collective-permute-start.6 = (bf16[3,6,32,128]{3,2,1,0:T(8,128)(2,1)S(1)}, bf16[3,6,32,128]{3,2,1,0:T(8,128)(2,1)S(1)}, u32[]{:S(2)}, u32[]{:S(2)}) collective-permute-start(bf16[3,6,32,128]{3,2,1,0:T(8,128)(2,1)S(1)} %collective-permute-done.3.refs_5_.refs_1_), channel_id=1, source_target_pairs={{0,1},{1,0},{2,3},{3,2},{4,5},{5,4},{6,7},{7,6},{8,9},{9,8},{10,11... | collective-permute-start | bytes 442376 | tf_op jit(solution)/shard_map/ppermute | solution.py:490
  83.1 1.4 copy-start.2
  83.1 1.4 collective-permute-start.7
  83.2 1.4 copy-start.3
  83.2 2.7 %collective-permute-start.8 = (bf16[3,6,32,128]{3,2,1,0:T(8,128)(2,1)S(1)}, bf16[3,6,32,128]{3,2,1,0:T(8,128)(2,1)}, u32[]{:S(2)}, u32[]{:S(2)}) collective-permute-start(bf16[3,6,32,128]{3,2,1,0:T(8,128)(2,1)S(1)} %collective-permute-done.5.refs_7_.refs_3_), channel_id=1, source_target_pairs={{0,1},{1,0},{2,3},{3,2},{4,5},{5,4},{6,7},{7,6},{8,9},{9,8},{10,11... | collective-permute-start | bytes 442376 | tf_op jit(solution)/shard_map/ppermute | solution.py:490
  84.5 1.3 copy-start.4
  84.5 26.8 %collective-permute-start.1 = (bf16[1,6,288,128]{3,2,1,0:T(8,128)(2,1)}, bf16[1,6,288,128]{3,2,1,0:T(8,128)(2,1)}, u32[]{:S(2)}, u32[]{:S(2)}) collective-permute-start(bf16[1,6,288,128]{3,2,1,0:T(8,128)(2,1)} %get-tuple-element.24), channel_id=1, source_target_pairs={{0,64},{32,96},{64,0},{96,32},{1,65},{33,97},{65,1},{97,33},{2,66}... | collective-permute-start | bytes 1327112 | tf_op jit(solution)/shard_map/ppermute | solution.py:123
  85.8 73.8 %collective-permute-start.10 = (bf16[4,2,2,288,128]{4,3,2,1,0:T(8,128)(2,1)}, bf16[4,2,2,288,128]{4,3,2,1,0:T(8,128)(2,1)}, u32[]{:S(2)}, u32[]{:S(2)}) collective-permute-start(bf16[4,2,2,288,128]{4,3,2,1,0:T(8,128)(2,1)} %all-to-all-done.refs_13_.refs_9_), channel_id=1, source_target_pairs={{1,0},{2,1},{3,2},{4,3},{5,4},{6,5},{7,6},{8,7},{9,8},{10,9},{11,1... | collective-permute-start | bytes 3538952 | tf_op jit(solution)/shard_map/ppermute | solution.py:138
  87.2 72.5 %collective-permute-start.9 = (bf16[4,2,2,288,128]{4,3,2,1,0:T(8,128)(2,1)}, bf16[4,2,2,288,128]{4,3,2,1,0:T(8,128)(2,1)}, u32[]{:S(2)}, u32[]{:S(2)}) collective-permute-start(bf16[4,2,2,288,128]{4,3,2,1,0:T(8,128)(2,1)} %all-to-all-done.refs_13_.refs_9_), channel_id=1, source_target_pairs={{0,1},{1,2},{2,3},{3,4},{4,5},{5,6},{6,7},{7,8},{8,9},{9,10},{10,1... | collective-permute-start | bytes 3538952 | tf_op jit(solution)/shard_map/ppermute | solution.py:138
  99.8 24.3 %all-to-all-start.2 = ((bf16[128,16,128]{2,1,0:T(8,128)(2,1)}), bf16[128,16,128]{2,1,0:T(8,128)(2,1)}, u32[]{:S(2)}, u32[]{:S(2)}) async-start(bf16[128,16,128]{2,1,0:T(8,128)(2,1)} %text_attention.1), calls=%async_computation.2 | async-start | bytes 1048576 | tf_op jit(solution)/shard_map/all_to_all | solution.py:134
  111.3 21.7 %collective-permute-start.2 = (bf16[1,6,288,128]{3,2,1,0:T(8,128)(2,1)}, bf16[1,6,288,128]{3,2,1,0:T(8,128)(2,1)}, u32[]{:S(2)}, u32[]{:S(2)}) collective-permute-start(bf16[1,6,288,128]{3,2,1,0:T(8,128)(2,1)} %get-tuple-element.25), channel_id=1, source_target_pairs={{0,96},{32,0},{64,32},{96,64},{1,97},{33,1},{65,33},{97,65},{2,98}... | collective-permute-start | bytes 1327112 | tf_op jit(solution)/shard_map/ppermute | solution.py:123
  127.1 49.1 %all-to-all-start.3 = ((bf16[128,16,128]{2,1,0:T(8,128)(2,1)}), bf16[128,16,128]{2,1,0:T(8,128)(2,1)}, u32[]{:S(2)}, u32[]{:S(2)}) async-start(bf16[128,16,128]{2,1,0:T(8,128)(2,1)} %bitcast.1), calls=%async_computation.3 | async-start | bytes 1048576 | tf_op jit(solution)/shard_map/all_to_all | solution.py:134
  154.8 18.8 %collective-permute-start.16 = (bf16[4,288,128]{2,1,0:T(8,128)(2,1)}, bf16[4,288,128]{2,1,0:T(8,128)(2,1)}, u32[]{:S(2)}, u32[]{:S(2)}) collective-permute-start(bf16[4,288,128]{2,1,0:T(8,128)(2,1)} %get-tuple-element.37), channel_id=1, source_target_pairs={{0,32},{32,64},{64,96},{96,0},{1,33},{33,65},{65,97},{97,1},{2,34}... | collective-permute-start | bytes 884744 | tf_op jit(solution)/shard_map/ppermute | solution.py:123
  155.5 20.6 %collective-permute-start.17 = (bf16[4,288,128]{2,1,0:T(8,128)(2,1)}, bf16[4,288,128]{2,1,0:T(8,128)(2,1)}, u32[]{:S(2)}, u32[]{:S(2)}) collective-permute-start(bf16[4,288,128]{2,1,0:T(8,128)(2,1)} %get-tuple-element.38), channel_id=1, source_target_pairs={{0,64},{32,96},{64,0},{96,32},{1,65},{33,97},{65,1},{97,33},{2,66}... | collective-permute-start | bytes 884744 | tf_op jit(solution)/shard_map/ppermute | solution.py:123
  158.2 17.9 %collective-permute-start.18 = (bf16[4,288,128]{2,1,0:T(8,128)(2,1)}, bf16[4,288,128]{2,1,0:T(8,128)(2,1)}, u32[]{:S(2)}, u32[]{:S(2)}) collective-permute-start(bf16[4,288,128]{2,1,0:T(8,128)(2,1)} %get-tuple-element.39), channel_id=1, source_target_pairs={{0,96},{32,0},{64,32},{96,64},{1,97},{33,1},{65,33},{97,65},{2,98}... | collective-permute-start | bytes 884744 | tf_op jit(solution)/shard_map/ppermute | solution.py:123
  172.0 9.8 %collective-permute-start.11 = (bf16[2,288,128]{2,1,0:T(8,128)(2,1)}, bf16[2,288,128]{2,1,0:T(8,128)(2,1)}, u32[]{:S(2)}, u32[]{:S(2)}) collective-permute-start(bf16[2,288,128]{2,1,0:T(8,128)(2,1)} %get-tuple-element.33), channel_id=1, source_target_pairs={{0,32},{32,64},{64,96},{96,0},{1,33},{33,65},{65,97},{97,1},{2,34}... | collective-permute-start | bytes 442376 | tf_op jit(solution)/shard_map/ppermute | solution.py:123
  172.7 9.2 %collective-permute-start.12 = (bf16[2,288,128]{2,1,0:T(8,128)(2,1)}, bf16[2,288,128]{2,1,0:T(8,128)(2,1)}, u32[]{:S(2)}, u32[]{:S(2)}) collective-permute-start(bf16[2,288,128]{2,1,0:T(8,128)(2,1)} %get-tuple-element.34), channel_id=1, source_target_pairs={{0,64},{32,96},{64,0},{96,32},{1,65},{33,97},{65,1},{97,33},{2,66}... | collective-permute-start | bytes 442376 | tf_op jit(solution)/shard_map/ppermute | solution.py:123
  173.6 8.8 %collective-permute-start.13 = (bf16[2,288,128]{2,1,0:T(8,128)(2,1)}, bf16[2,288,128]{2,1,0:T(8,128)(2,1)}, u32[]{:S(2)}, u32[]{:S(2)}) collective-permute-start(bf16[2,288,128]{2,1,0:T(8,128)(2,1)} %get-tuple-element.35), channel_id=1, source_target_pairs={{0,96},{32,0},{64,32},{96,64},{1,97},{33,1},{65,33},{97,65},{2,98}... | collective-permute-start | bytes 442376 | tf_op jit(solution)/shard_map/ppermute | solution.py:123

commit v6 on v5

--- a/solution.py
+++ b/solution.py
@@ -175,7 +175,7 @@
 def text_body(length, *refs):
     text, kv, refs = refs[: 2 * GROUP], refs[2 * GROUP :][: len(CHUNKS)], refs[2 * GROUP + len(CHUNKS) :]
     out_ref, q_sc, kv_sc, o_sc, log_sc, sc, slots, sems = refs
-    pairs = []
+    pairs, moves = [], []
     for n, piece in enumerate(text):
         rows = rows_of(2 * place(-(n % GROUP)) + half(n // GROUP), HALF)
         pairs.append((piece.at[0], q_sc.at[:, rows]))
@@ -183,14 +183,17 @@
     for c, (first, heads) in enumerate(CHUNKS):
         for g in range(GROUP):
             pairs.append((kv[c].at[g], kv_sc.at[:, pl.ds(first, heads), pl.ds(g * ROWS, ROWS)]))
-    moves = copy_list(pairs, sems)
-    run(moves)
+        moves.append(copy_list(pairs, sems.at[c]))
+        run(moves[-1])
+        pairs = []
     sc[...] = jnp.zeros_like(sc)
     bias = jnp.where(lax.axis_index("blk") == 0, text_bias(length[0]), -jnp.inf)
-    wait(moves)
+    wait(moves[0])
     steps = [(h, i) for h in range(HD) for i in range(TXT // RB)]
 
     def begin(h, i):
+        if (h, i) == (CHUNKS[1][0], 0):
+            wait(moves[1])
         q = q_sc[h, i * RB : (i + 1) * RB]
         return weigh(q, lambda: kv_sc[0, h], lambda: kv_sc[1, h], [(SLICE, bias)])
 
@@ -215,7 +218,7 @@
             sc[pl.ds(SLOT * p + PAIRS + part, TROWS, stride=2 * SLOT), :] = rounded
             logs = logs - rounded
     slots[...] = sc[...].astype(BF).reshape(DEVS, SLOT, D)
-    leave(slots, out_ref, sems)
+    leave(slots, out_ref, sems.at[0])
 
 
 def leave(held, out_ref, sems):
@@ -239,7 +242,7 @@
             pltpu.VMEM((HD, TXT, D), F32),
             pltpu.VMEM((DEVS * SLOT, D), F32),
             pltpu.VMEM((DEVS, SLOT, D), BF),
-            pltpu.SemaphoreType.DMA((32,)),
+            pltpu.SemaphoreType.DMA((2, 24)),
         ],
         compiler_params=PARAMS,
         name="text_attention",
@@ -412,8 +415,10 @@
 
 def first_body(first, heads, *refs):
     pieces, slots, video_out, text_out, held, sc, got, in_sems, out_sems, sems = refs[:GROUP], *refs[GROUP:]
+    fetch = pltpu.make_async_copy(slots, got, sems.at[0])
+    fetch.start()
     writes = rows_body(first, heads, *pieces, video_out, held, in_sems, out_sems)
-    leave(slots, got, sems)
+    fetch.wait()
     sc[...] = got[...].astype(F32).reshape(DEVS * SLOT, D)
     for p in range(2):
         for u in range(GROUP):
@@ -471,14 +476,8 @@
     video, words = (video_q, video_k, video_v), (text_q, text_k, text_v)
     (f0, n0), (f1, n1) = CHUNKS
     (kv0,) = pack(video, [((1, 2), f0, n0, ROWS, True)])
-    text, kv1, q = pack(
-        video + words,
-        [
-            ((3, 4, 5), 0, HD, HALF, False),
-            ((1, 2), f1, n1, ROWS, True),
-            ((0,), 0, HD, ROWS, False),
-        ],
-    )
+    (text,) = pack(words, [((0, 1, 2), 0, HD, HALF, False)])
+    kv1, q = pack(video, [((1, 2), f1, n1, ROWS, True), ((0,), 0, HD, ROWS, False)])
     own, before, after = [], [], []
     for kv in (kv0, kv1):
         own.append(swap(kv, "uly"))

time: 185 us -> 185 us (level)
  waiting for transfers between devices: 37.5 us -> 29.4 us
  starting transfers between devices: 50.6 us -> 57.1 us
    ppermute x12, waiting for transfers between devices: 26.1 us -> 17.9 us  [around(): lax.ppermute(block, 'uly', [(i, (i + distance) % GROUP) for i in range(GR...]
    ppermute x3, starting transfers between devices: 0.57 us -> 5.42 us  [local(): other.append(lax.ppermute(mine[d], 'blk', [(i, i ^ 1) for i in range(BLK)]))]
    pallas_call x2 -> x3, Pallas kernels: 9.81 us -> 12.6 us  [pack(): pl.pallas_call(body, in_specs=[ANY] * len(arrays), out_specs=[ANY] * len(...]
    all_to_all x3, starting transfers between devices: 21.8 us -> 24.5 us  [swap(): return lax.all_to_all(array, axes, 0, 0, tiled=True)]
  transfers between devices with their start and end apart: 22 -> 22, of which waited for: 7 -> 8; matrix products, arithmetic and copies ran while one was open for 0% -> 0% of each run, Pallas kernels for 30% -> 31%
where the time goes in v6:
time: 185 us
  Pallas kernels  62.6 us (34%)
  starting transfers between devices  57.1 us (31%)
  blocking collectives  33.8 us (18%)
  waiting for transfers between devices  29.4 us (16%)
    pallas_call x2, Pallas kernels, video_attention(): pl.pallas_call(functools.partial(video_body, first, heads), in_specs=[SME...  34.1 us
    all_to_all x1, blocking collectives, swap(): return lax.all_to_all(array, axes, 0, 0, tiled=True)  33.8 us
    all_to_all x3, starting transfers between devices, swap(): return lax.all_to_all(array, axes, 0, 0, tiled=True)  24.5 us
    ppermute x12, starting transfers between devices, around(): lax.ppermute(block, 'uly', [(i, (i + distance) % GROUP) for i in range(GR...  17.9 us
    ppermute x12, waiting for transfers between devices, around(): lax.ppermute(block, 'uly', [(i, (i + distance) % GROUP) for i in range(GR...  17.9 us
    pallas_call x3, Pallas kernels, pack(): pl.pallas_call(body, in_specs=[ANY] * len(arrays), out_specs=[ANY] * len(...  12.6 us
    all_to_all x3, waiting for transfers between devices, swap(): return lax.all_to_all(array, axes, 0, 0, tiled=True)  10.6 us
    ppermute x4, starting transfers between devices, beside(): lax.ppermute(block, 'blk', [(i, i + distance) for i in range(BLK) if 0 <=...  9.32 us
  transfers between devices with their start and end apart: 22, of which 8 were waited for; matrix products, arithmetic and copies ran while one was open for 0% of the time, Pallas kernels for 31%

profile of v6, /device:TPU:0, one launch (start us, length us, event | category | flops | bytes accessed | tf_op | source)
XLA Modules:
  0.0 184.6 jit_solution(10904879173376414977)
XLA Ops:
  0.6 4.3 %shard_map.97 = bf16[4,2,4,288,128]{4,3,2,1,0:T(8,128)(2,1)} custom-call(bf16[288,3072]{1,0:T(8,128)(2,1)} %refs_0_.5, bf16[288,3072]{1,0:T(8,128)(2,1)} %refs_1_.5, bf16[288,3072]{1,0:T(8,128)(2,1)} %refs_2_.5), custom_call_target="tpu_custom_call" | custom-call | tf_op jit(solution)/shard_map/pallas_call | solution.py:105
  5.0 33.8 %all_to_all.20.refs_13_.refs_8_ = bf16[4,2,4,288,128]{4,3,2,1,0:T(8,128)(2,1)} all-to-all(bf16[4,2,4,288,128]{4,3,2,1,0:T(8,128)(2,1)} %shard_map.97), channel_id=1, replica_groups=mesh['uly'=4,'blk'=32] {'uly'}, dimensions={0} | all-to-all | bytes 4718592 | tf_op jit(solution)/shard_map/all_to_all | solution.py:134
  38.8 2.7 %collective-permute-start.14 = (bf16[4,2,4,288,128]{4,3,2,1,0:T(8,128)(2,1)}, bf16[4,2,4,288,128]{4,3,2,1,0:T(8,128)(2,1)}, u32[]{:S(2)}, u32[]{:S(2)}) collective-permute-start(bf16[4,2,4,288,128]{4,3,2,1,0:T(8,128)(2,1)} %all_to_all.20.refs_13_.refs_8_), channel_id=1, source_target_pairs={{0,1},{1,2},{2,3},{3,4},{4,5},{5,6},{6,7},{7,8},{8,9},{9,10},{10,1... | collective-permute-start | bytes 7077896 | tf_op jit(solution)/shard_map/ppermute | solution.py:138
  41.5 1.3 collective-permute-start.15
  42.8 4.7 %shard_map.95 = (bf16[4,2,2,288,128]{4,3,2,1,0:T(8,128)(2,1)}, bf16[1,6,288,128]{3,2,1,0:T(8,128)(2,1)}, bf16[1,6,288,128]{3,2,1,0:T(8,128)(2,1)}, bf16[1,6,288,...) custom-call(bf16[288,3072]{1,0:T(8,128)(2,1)} %refs_0_.5, bf16[288,3072]{1,0:T(8,128)(2,1)} %refs_1_.5, bf16[288,3072]{1,0:T(8,128)(2,1)} %refs_2_.5), custom_call_target="tpu_custom_call" | custom-call | tf_op jit(solution)/shard_map/pallas_call | solution.py:105
  47.4 4.3 %all-to-all-start = ((bf16[4,2,2,288,128]{4,3,2,1,0:T(8,128)(2,1)}), bf16[4,2,2,288,128]{4,3,2,1,0:T(8,128)(2,1)}, u32[]{:S(2)}, u32[]{:S(2)}) async-start(bf16[4,2,2,288,128]{4,3,2,1,0:T(8,128)(2,1)} %get-tuple-element.31), calls=%async_computation | async-start | bytes 2359296 | tf_op jit(solution)/shard_map/all_to_all | solution.py:134
  51.7 3.6 %shard_map.96 = (bf16[3,6,32,128]{3,2,1,0:T(8,128)(2,1)}, bf16[3,6,32,128]{3,2,1,0:T(8,128)(2,1)}, bf16[3,6,32,128]{3,2,1,0:T(8,128)(2,1)}, bf16[3,6,32,128]{3,2,1,0:T(8,128)(2,1)}, bf16[3,6,32,128]{3,2,1,0:T(8,128)(2,1)}) custom-call(bf16[64,3072]{1,0:T(8,128)(2,1)} %refs_0_.4, bf16[64,3072]{1,0:T(8,128)(2,1)} %refs_1_.4, bf16[64,3072]{1,0:T(8,128)(2,1)} %refs_2_.4), custom_call_target="tpu_custom_call" | custom-call | tf_op jit(solution)/shard_map/pallas_call | solution.py:105
  55.3 2.0 %collective-permute-start.3 = (bf16[3,6,32,128]{3,2,1,0:T(8,128)(2,1)}, bf16[3,6,32,128]{3,2,1,0:T(8,128)(2,1)S(1)}, u32[]{:S(2)}, u32[]{:S(2)}) collective-permute-start(bf16[3,6,32,128]{3,2,1,0:T(8,128)(2,1)} %get-tuple-element.27), channel_id=1, source_target_pairs={{0,32},{32,64},{64,96},{96,0},{1,33},{33,65},{65,97},{97,1},{2,34}... | collective-permute-start | bytes 442376 | tf_op jit(solution)/shard_map/ppermute | solution.py:123
  57.3 2.7 %collective-permute-start.4 = (bf16[3,6,32,128]{3,2,1,0:T(8,128)(2,1)}, bf16[3,6,32,128]{3,2,1,0:T(8,128)(2,1)S(1)}, u32[]{:S(2)}, u32[]{:S(2)}) collective-permute-start(bf16[3,6,32,128]{3,2,1,0:T(8,128)(2,1)} %get-tuple-element.28), channel_id=1, source_target_pairs={{0,64},{32,96},{64,0},{96,32},{1,65},{33,97},{65,1},{97,33},{2,66}... | collective-permute-start | bytes 442376 | tf_op jit(solution)/shard_map/ppermute | solution.py:123
  60.0 0.0 collective-permute-start
  60.0 11.7 %collective-permute-done.3.refs_5_.refs_1_ = bf16[3,6,32,128]{3,2,1,0:T(8,128)(2,1)S(1)} collective-permute-done((bf16[3,6,32,128]{3,2,1,0:T(8,128)(2,1)}, bf16[3,6,32,128]{3,2,1,0:T(8,128)(2,1)S(1)}, u32[]{:S(2)}, u32[]{:S(2)}) %collective-permute-start.3) | collective-permute-done | bytes 147488 | tf_op jit(solution)/shard_map/ppermute | solution.py:123
  71.7 0.0 copy-start
  71.7 0.9 collective-permute-start.5
  72.6 2.7 %collective-permute-done.4.refs_6_.refs_2_ = bf16[3,6,32,128]{3,2,1,0:T(8,128)(2,1)S(1)} collective-permute-done((bf16[3,6,32,128]{3,2,1,0:T(8,128)(2,1)}, bf16[3,6,32,128]{3,2,1,0:T(8,128)(2,1)S(1)}, u32[]{:S(2)}, u32[]{:S(2)}) %collective-permute-start.4) | collective-permute-done | bytes 147488 | tf_op jit(solution)/shard_map/ppermute | solution.py:123
  75.3 0.0 copy-done
  75.3 0.0 copy-start.1
  75.3 1.6 collective-permute-start.6
  76.9 0.2 collective-permute-done.5.refs_7_.refs_3_
  77.1 0.0 copy-start.2
  77.1 3.8 %collective-permute-start.7 = (bf16[3,6,32,128]{3,2,1,0:T(8,128)(2,1)S(1)}, bf16[3,6,32,128]{3,2,1,0:T(8,128)(2,1)S(1)}, u32[]{:S(2)}, u32[]{:S(2)}) collective-permute-start(bf16[3,6,32,128]{3,2,1,0:T(8,128)(2,1)S(1)} %collective-permute-done.4.refs_6_.refs_2_), channel_id=1, source_target_pairs={{0,1},{1,0},{2,3},{3,2},{4,5},{5,4},{6,7},{7,6},{8,9},{9,8},{10,11... | collective-permute-start | bytes 442376 | tf_op jit(solution)/shard_map/ppermute | solution.py:489
  80.8 0.0 collective-permute-done.6.refs_9_.refs_5_
  80.8 0.0 copy-done.1
  80.8 0.0 copy-start.3
  80.8 0.1 collective-permute-start.8
  80.9 0.9 collective-permute-done.7.refs_10_.refs_6_
  81.8 0.0 copy-done.2
  81.8 0.0 copy-start.4
  81.8 0.0 copy-done.3
  81.8 1.2 collective-permute-start.1
  83.1 0.0 copy-done.4
  83.1 0.0 collective-permute-done.8.refs_11_.refs_7_
  83.1 0.0 all-to-all-done.refs_13_.refs_9_
  83.1 1.3 collective-permute-start.10
  84.4 0.1 collective-permute-done.refs_1_
  84.5 4.0 %collective-permute-start.9 = (bf16[4,2,2,288,128]{4,3,2,1,0:T(8,128)(2,1)}, bf16[4,2,2,288,128]{4,3,2,1,0:T(8,128)(2,1)}, u32[]{:S(2)}, u32[]{:S(2)}) collective-permute-start(bf16[4,2,2,288,128]{4,3,2,1,0:T(8,128)(2,1)} %all-to-all-done.refs_13_.refs_9_), channel_id=1, source_target_pairs={{0,1},{1,2},{2,3},{3,4},{4,5},{5,6},{6,7},{7,8},{8,9},{9,10},{10,1... | collective-permute-start | bytes 3538952 | tf_op jit(solution)/shard_map/ppermute | solution.py:138
  89.1 7.8 %text_attention.1 = bf16[128,16,128]{2,1,0:T(8,128)(2,1)} custom-call(s32[1]{0:T(128)S(6)} %copy.12.length, bf16[3,6,32,128]{3,2,1,0:T(8,128)(2,1)} %get-tuple-element.26.refs_4_.refs_0_, bf16[3,6,32,128]{3,2,1,0:T(8,128)(2,1)} %copy-done, bf16[3,6,32,128]{3,2,1,0:T(8,128)(2,1)} %copy-done.1, bf16[3,6,32,128]{3,2,1,0:T(8,128)(2,1)} %copy-done.2, ...), custom_call_target="tpu_custom_call" | custom-call | tf_op jit(solution)/shard_map/text_attention/pallas_call | solution.py:233
  97.0 14.3 %all-to-all-start.2 = ((bf16[128,16,128]{2,1,0:T(8,128)(2,1)}), bf16[128,16,128]{2,1,0:T(8,128)(2,1)}, u32[]{:S(2)}, u32[]{:S(2)}) async-start(bf16[128,16,128]{2,1,0:T(8,128)(2,1)} %text_attention.1), calls=%async_computation.2 | async-start | bytes 1048576 | tf_op jit(solution)/shard_map/all_to_all | solution.py:134
  111.2 0.0 collective-permute-done.1.refs_2_
  111.2 2.2 %collective-permute-start.2 = (bf16[1,6,288,128]{3,2,1,0:T(8,128)(2,1)}, bf16[1,6,288,128]{3,2,1,0:T(8,128)(2,1)}, u32[]{:S(2)}, u32[]{:S(2)}) collective-permute-start(bf16[1,6,288,128]{3,2,1,0:T(8,128)(2,1)} %get-tuple-element.25), channel_id=1, source_target_pairs={{0,96},{32,0},{64,32},{96,64},{1,97},{33,1},{65,33},{97,65},{2,98}... | collective-permute-start | bytes 1327112 | tf_op jit(solution)/shard_map/ppermute | solution.py:123
  113.4 10.6 %all-to-all-done.2.in_ref = bf16[128,16,128]{2,1,0:T(8,128)(2,1)} async-done(((bf16[128,16,128]{2,1,0:T(8,128)(2,1)}), bf16[128,16,128]{2,1,0:T(8,128)(2,1)}, u32[]{:S(2)}, u32[]{:S(2)}) %all-to-all-start.2) | async-done | bytes 524320 | tf_op jit(solution)/shard_map/all_to_all | solution.py:134
  124.0 3.0 %combine.1 = bf16[32,4,16,128]{3,2,1,0:T(8,128)(2,1)} custom-call(bf16[128,16,128]{2,1,0:T(8,128)(2,1)} %all-to-all-done.2.in_ref), custom_call_target="tpu_custom_call" | custom-call | tf_op jit(solution)/shard_map/combine/pallas_call | solution.py:287
  127.0 5.9 %all-to-all-start.3 = ((bf16[128,16,128]{2,1,0:T(8,128)(2,1)}), bf16[128,16,128]{2,1,0:T(8,128)(2,1)}, u32[]{:S(2)}, u32[]{:S(2)}) async-start(bf16[128,16,128]{2,1,0:T(8,128)(2,1)} %bitcast.1), calls=%async_computation.3 | async-start | bytes 1048576 | tf_op jit(solution)/shard_map/all_to_all | solution.py:134
  133.0 0.0 collective-permute-done.2.refs_3_
  133.0 0.0 collective-permute-done.14.refs_12_
  133.0 0.0 collective-permute-done.15.refs_14_
  133.0 21.8 %video_attention.3 = (bf16[4,288,128]{2,1,0:T(8,128)(2,1)}, bf16[4,288,128]{2,1,0:T(8,128)(2,1)}, bf16[4,288,128]{2,1,0:T(8,128)(2,1)}, bf16[4,288,128]{2,1,0:T(8,128)(2,1)}) custom-call(s32[3,6]{1,0:T(4,128)} %tiles.3, s32[1]{0:T(128)S(6)} %copy.12.length, bf16[1,6,288,128]{3,2,1,0:T(8,128)(2,1)} %get-tuple-element.22.refs_0_, ...), custom_call_target="tpu_custom_call" | custom-call | tf_op jit(solution)/shard_map/video_attention/pallas_call | solution.py:379
  154.8 0.8 collective-permute-start.16
  155.6 2.7 %collective-permute-start.17 = (bf16[4,288,128]{2,1,0:T(8,128)(2,1)}, bf16[4,288,128]{2,1,0:T(8,128)(2,1)}, u32[]{:S(2)}, u32[]{:S(2)}) collective-permute-start(bf16[4,288,128]{2,1,0:T(8,128)(2,1)} %get-tuple-element.38), channel_id=1, source_target_pairs={{0,64},{32,96},{64,0},{96,32},{1,65},{33,97},{65,1},{97,33},{2,66}... | collective-permute-start | bytes 884744 | tf_op jit(solution)/shard_map/ppermute | solution.py:123
  158.3 1.4 collective-permute-start.18
  159.8 0.0 collective-permute-done.10.refs_14_
  159.8 0.0 collective-permute-done.9.refs_12_
  159.8 12.3 %video_attention.2 = (bf16[2,288,128]{2,1,0:T(8,128)(2,1)}, bf16[2,288,128]{2,1,0:T(8,128)(2,1)}, bf16[2,288,128]{2,1,0:T(8,128)(2,1)}, bf16[2,288,128]{2,1,0:T(8,128)(2,1)}) custom-call(s32[3,6]{1,0:T(4,128)} %tiles.3, s32[1]{0:T(128)S(6)} %copy.12.length, bf16[1,6,288,128]{3,2,1,0:T(8,128)(2,1)} %get-tuple-element.22.refs_0_, ...), custom_call_target="tpu_custom_call" | custom-call | tf_op jit(solution)/shard_map/video_attention/pallas_call | solution.py:379
  172.1 0.6 collective-permute-start.11
  172.8 0.9 collective-permute-start.12
  173.7 0.0 collective-permute-done.16.refs_1_
  173.7 2.4 %collective-permute-start.13 = (bf16[2,288,128]{2,1,0:T(8,128)(2,1)}, bf16[2,288,128]{2,1,0:T(8,128)(2,1)}, u32[]{:S(2)}, u32[]{:S(2)}) collective-permute-start(bf16[2,288,128]{2,1,0:T(8,128)(2,1)} %get-tuple-element.35), channel_id=1, source_target_pairs={{0,96},{32,0},{64,32},{96,64},{1,97},{33,1},{65,33},{97,65},{2,98}... | collective-permute-start | bytes 442376 | tf_op jit(solution)/shard_map/ppermute | solution.py:123
  176.1 0.0 all-to-all-done.3.refs_4_
  176.1 0.0 collective-permute-done.17.refs_2_
  176.1 0.0 collective-permute-done.18.refs_3_
  176.1 3.2 %first_rows.1 = (bf16[288,3072]{1,0:T(8,128)(2,1)}, bf16[64,3072]{1,0:T(8,128)(2,1)}) custom-call(bf16[4,288,128]{2,1,0:T(8,128)(2,1)} %get-tuple-element.36.refs_0_, bf16[4,288,128]{2,1,0:T(8,128)(2,1)} %collective-permute-done.16.refs_1_, bf16[4,288,128]{2,1,0:T(8,128)(2,1)} %collective-permute-done.17.refs_2_, ...), custom_call_target="tpu_custom_call" | custom-call | tf_op jit(solution)/shard_map/first_rows/pallas_call | solution.py:437
  179.3 2.6 %collective-permute-done.11.refs_1_ = bf16[2,288,128]{2,1,0:T(8,128)(2,1)} collective-permute-done((bf16[2,288,128]{2,1,0:T(8,128)(2,1)}, bf16[2,288,128]{2,1,0:T(8,128)(2,1)}, u32[]{:S(2)}, u32[]{:S(2)}) %collective-permute-start.11) | collective-permute-done | bytes 147488 | tf_op jit(solution)/shard_map/ppermute | solution.py:123
  181.9 0.0 collective-permute-done.12.refs_2_
  181.9 0.6 collective-permute-done.13.refs_3_
  182.5 1.9 %later_rows.1 = bf16[288,3072]{1,0:T(8,128)(2,1)} custom-call(bf16[2,288,128]{2,1,0:T(8,128)(2,1)} %get-tuple-element.32.refs_0_, bf16[2,288,128]{2,1,0:T(8,128)(2,1)} %collective-permute-done.11.refs_1_, bf16[2,288,128]{2,1,0:T(8,128)(2,1)} %collective-permute-done.12.refs_2_, ...), custom_call_target="tpu_custom_call", output_to_operand_aliasing={{}: (4, {})} | custom-call | tf_op jit(solution)/shard_map/later_rows/pallas_call | solution.py:459
Async XLA Ops:
  38.8 94.2 %collective-permute-start.14 = (bf16[4,2,4,288,128]{4,3,2,1,0:T(8,128)(2,1)}, bf16[4,2,4,288,128]{4,3,2,1,0:T(8,128)(2,1)}, u32[]{:S(2)}, u32[]{:S(2)}) collective-permute-start(bf16[4,2,4,288,128]{4,3,2,1,0:T(8,128)(2,1)} %all_to_all.20.refs_13_.refs_8_), channel_id=1, source_target_pairs={{0,1},{1,2},{2,3},{3,4},{4,5},{5,6},{6,7},{7,8},{8,9},{9,10},{10,1... | collective-permute-start | bytes 7077896 | tf_op jit(solution)/shard_map/ppermute | solution.py:138
  41.5 91.5 %collective-permute-start.15 = (bf16[4,2,4,288,128]{4,3,2,1,0:T(8,128)(2,1)}, bf16[4,2,4,288,128]{4,3,2,1,0:T(8,128)(2,1)}, u32[]{:S(2)}, u32[]{:S(2)}) collective-permute-start(bf16[4,2,4,288,128]{4,3,2,1,0:T(8,128)(2,1)} %all_to_all.20.refs_13_.refs_8_), channel_id=1, source_target_pairs={{1,0},{2,1},{3,2},{4,3},{5,4},{6,5},{7,6},{8,7},{9,8},{10,9},{11,1... | collective-permute-start | bytes 7077896 | tf_op jit(solution)/shard_map/ppermute | solution.py:138
  47.4 35.6 %all-to-all-start = ((bf16[4,2,2,288,128]{4,3,2,1,0:T(8,128)(2,1)}), bf16[4,2,2,288,128]{4,3,2,1,0:T(8,128)(2,1)}, u32[]{:S(2)}, u32[]{:S(2)}) async-start(bf16[4,2,2,288,128]{4,3,2,1,0:T(8,128)(2,1)} %get-tuple-element.31), calls=%async_computation | async-start | bytes 2359296 | tf_op jit(solution)/shard_map/all_to_all | solution.py:134
  55.3 16.4 %collective-permute-start.3 = (bf16[3,6,32,128]{3,2,1,0:T(8,128)(2,1)}, bf16[3,6,32,128]{3,2,1,0:T(8,128)(2,1)S(1)}, u32[]{:S(2)}, u32[]{:S(2)}) collective-permute-start(bf16[3,6,32,128]{3,2,1,0:T(8,128)(2,1)} %get-tuple-element.27), channel_id=1, source_target_pairs={{0,32},{32,64},{64,96},{96,0},{1,33},{33,65},{65,97},{97,1},{2,34}... | collective-permute-start | bytes 442376 | tf_op jit(solution)/shard_map/ppermute | solution.py:123
  57.3 18.0 %collective-permute-start.4 = (bf16[3,6,32,128]{3,2,1,0:T(8,128)(2,1)}, bf16[3,6,32,128]{3,2,1,0:T(8,128)(2,1)S(1)}, u32[]{:S(2)}, u32[]{:S(2)}) collective-permute-start(bf16[3,6,32,128]{3,2,1,0:T(8,128)(2,1)} %get-tuple-element.28), channel_id=1, source_target_pairs={{0,64},{32,96},{64,0},{96,32},{1,65},{33,97},{65,1},{97,33},{2,66}... | collective-permute-start | bytes 442376 | tf_op jit(solution)/shard_map/ppermute | solution.py:123
  60.0 24.4 %collective-permute-start = (bf16[1,6,288,128]{3,2,1,0:T(8,128)(2,1)}, bf16[1,6,288,128]{3,2,1,0:T(8,128)(2,1)}, u32[]{:S(2)}, u32[]{:S(2)}) collective-permute-start(bf16[1,6,288,128]{3,2,1,0:T(8,128)(2,1)} %get-tuple-element.23), channel_id=1, source_target_pairs={{0,32},{32,64},{64,96},{96,0},{1,33},{33,65},{65,97},{97,1},{2,34}... | collective-permute-start | bytes 1327112 | tf_op jit(solution)/shard_map/ppermute | solution.py:123
  71.7 3.6 %copy-start = (bf16[3,6,32,128]{3,2,1,0:T(8,128)(2,1)}, bf16[3,6,32,128]{3,2,1,0:T(8,128)(2,1)S(1)}, u32[]{:S(2)}) copy-start(bf16[3,6,32,128]{3,2,1,0:T(8,128)(2,1)S(1)} %collective-permute-done.3.refs_5_.refs_1_) | copy-start | bytes 442372
  71.7 5.4 %collective-permute-start.5 = (bf16[3,6,32,128]{3,2,1,0:T(8,128)(2,1)}, bf16[3,6,32,128]{3,2,1,0:T(8,128)(2,1)S(1)}, u32[]{:S(2)}, u32[]{:S(2)}) collective-permute-start(bf16[3,6,32,128]{3,2,1,0:T(8,128)(2,1)} %get-tuple-element.29), channel_id=1, source_target_pairs={{0,96},{32,0},{64,32},{96,64},{1,97},{33,1},{65,33},{97,65},{2,98}... | collective-permute-start | bytes 442376 | tf_op jit(solution)/shard_map/ppermute | solution.py:123
  75.3 5.5 %copy-start.1 = (bf16[3,6,32,128]{3,2,1,0:T(8,128)(2,1)}, bf16[3,6,32,128]{3,2,1,0:T(8,128)(2,1)S(1)}, u32[]{:S(2)}) copy-start(bf16[3,6,32,128]{3,2,1,0:T(8,128)(2,1)S(1)} %collective-permute-done.4.refs_6_.refs_2_) | copy-start | bytes 442372
  75.3 5.5 %collective-permute-start.6 = (bf16[3,6,32,128]{3,2,1,0:T(8,128)(2,1)S(1)}, bf16[3,6,32,128]{3,2,1,0:T(8,128)(2,1)S(1)}, u32[]{:S(2)}, u32[]{:S(2)}) collective-permute-start(bf16[3,6,32,128]{3,2,1,0:T(8,128)(2,1)S(1)} %collective-permute-done.3.refs_5_.refs_1_), channel_id=1, source_target_pairs={{0,1},{1,0},{2,3},{3,2},{4,5},{5,4},{6,7},{7,6},{8,9},{9,8},{10,11... | collective-permute-start | bytes 442376 | tf_op jit(solution)/shard_map/ppermute | solution.py:489
  77.1 4.8 %copy-start.2 = (bf16[3,6,32,128]{3,2,1,0:T(8,128)(2,1)}, bf16[3,6,32,128]{3,2,1,0:T(8,128)(2,1)S(1)}, u32[]{:S(2)}) copy-start(bf16[3,6,32,128]{3,2,1,0:T(8,128)(2,1)S(1)} %collective-permute-done.5.refs_7_.refs_3_) | copy-start | bytes 442372
  77.1 4.8 %collective-permute-start.7 = (bf16[3,6,32,128]{3,2,1,0:T(8,128)(2,1)S(1)}, bf16[3,6,32,128]{3,2,1,0:T(8,128)(2,1)S(1)}, u32[]{:S(2)}, u32[]{:S(2)}) collective-permute-start(bf16[3,6,32,128]{3,2,1,0:T(8,128)(2,1)S(1)} %collective-permute-done.4.refs_6_.refs_2_), channel_id=1, source_target_pairs={{0,1},{1,0},{2,3},{3,2},{4,5},{5,4},{6,7},{7,6},{8,9},{9,8},{10,11... | collective-permute-start | bytes 442376 | tf_op jit(solution)/shard_map/ppermute | solution.py:489
  80.8 1.0 copy-start.3
  80.8 2.3 %collective-permute-start.8 = (bf16[3,6,32,128]{3,2,1,0:T(8,128)(2,1)S(1)}, bf16[3,6,32,128]{3,2,1,0:T(8,128)(2,1)}, u32[]{:S(2)}, u32[]{:S(2)}) collective-permute-start(bf16[3,6,32,128]{3,2,1,0:T(8,128)(2,1)S(1)} %collective-permute-done.5.refs_7_.refs_3_), channel_id=1, source_target_pairs={{0,1},{1,0},{2,3},{3,2},{4,5},{5,4},{6,7},{7,6},{8,9},{9,8},{10,11... | collective-permute-start | bytes 442376 | tf_op jit(solution)/shard_map/ppermute | solution.py:489
  81.8 1.2 copy-start.4
  81.8 29.4 %collective-permute-start.1 = (bf16[1,6,288,128]{3,2,1,0:T(8,128)(2,1)}, bf16[1,6,288,128]{3,2,1,0:T(8,128)(2,1)}, u32[]{:S(2)}, u32[]{:S(2)}) collective-permute-start(bf16[1,6,288,128]{3,2,1,0:T(8,128)(2,1)} %get-tuple-element.24), channel_id=1, source_target_pairs={{0,64},{32,96},{64,0},{96,32},{1,65},{33,97},{65,1},{97,33},{2,66}... | collective-permute-start | bytes 1327112 | tf_op jit(solution)/shard_map/ppermute | solution.py:123
  83.1 76.7 %collective-permute-start.10 = (bf16[4,2,2,288,128]{4,3,2,1,0:T(8,128)(2,1)}, bf16[4,2,2,288,128]{4,3,2,1,0:T(8,128)(2,1)}, u32[]{:S(2)}, u32[]{:S(2)}) collective-permute-start(bf16[4,2,2,288,128]{4,3,2,1,0:T(8,128)(2,1)} %all-to-all-done.refs_13_.refs_9_), channel_id=1, source_target_pairs={{1,0},{2,1},{3,2},{4,3},{5,4},{6,5},{7,6},{8,7},{9,8},{10,9},{11,1... | collective-permute-start | bytes 3538952 | tf_op jit(solution)/shard_map/ppermute | solution.py:138
  84.5 75.3 %collective-permute-start.9 = (bf16[4,2,2,288,128]{4,3,2,1,0:T(8,128)(2,1)}, bf16[4,2,2,288,128]{4,3,2,1,0:T(8,128)(2,1)}, u32[]{:S(2)}, u32[]{:S(2)}) collective-permute-start(bf16[4,2,2,288,128]{4,3,2,1,0:T(8,128)(2,1)} %all-to-all-done.refs_13_.refs_9_), channel_id=1, source_target_pairs={{0,1},{1,2},{2,3},{3,4},{4,5},{5,6},{6,7},{7,8},{8,9},{9,10},{10,1... | collective-permute-start | bytes 3538952 | tf_op jit(solution)/shard_map/ppermute | solution.py:138
  97.0 27.1 %all-to-all-start.2 = ((bf16[128,16,128]{2,1,0:T(8,128)(2,1)}), bf16[128,16,128]{2,1,0:T(8,128)(2,1)}, u32[]{:S(2)}, u32[]{:S(2)}) async-start(bf16[128,16,128]{2,1,0:T(8,128)(2,1)} %text_attention.1), calls=%async_computation.2 | async-start | bytes 1048576 | tf_op jit(solution)/shard_map/all_to_all | solution.py:134
  111.2 21.7 %collective-permute-start.2 = (bf16[1,6,288,128]{3,2,1,0:T(8,128)(2,1)}, bf16[1,6,288,128]{3,2,1,0:T(8,128)(2,1)}, u32[]{:S(2)}, u32[]{:S(2)}) collective-permute-start(bf16[1,6,288,128]{3,2,1,0:T(8,128)(2,1)} %get-tuple-element.25), channel_id=1, source_target_pairs={{0,96},{32,0},{64,32},{96,64},{1,97},{33,1},{65,33},{97,65},{2,98}... | collective-permute-start | bytes 1327112 | tf_op jit(solution)/shard_map/ppermute | solution.py:123
  127.0 49.1 %all-to-all-start.3 = ((bf16[128,16,128]{2,1,0:T(8,128)(2,1)}), bf16[128,16,128]{2,1,0:T(8,128)(2,1)}, u32[]{:S(2)}, u32[]{:S(2)}) async-start(bf16[128,16,128]{2,1,0:T(8,128)(2,1)} %bitcast.1), calls=%async_computation.3 | async-start | bytes 1048576 | tf_op jit(solution)/shard_map/all_to_all | solution.py:134
  154.8 18.9 %collective-permute-start.16 = (bf16[4,288,128]{2,1,0:T(8,128)(2,1)}, bf16[4,288,128]{2,1,0:T(8,128)(2,1)}, u32[]{:S(2)}, u32[]{:S(2)}) collective-permute-start(bf16[4,288,128]{2,1,0:T(8,128)(2,1)} %get-tuple-element.37), channel_id=1, source_target_pairs={{0,32},{32,64},{64,96},{96,0},{1,33},{33,65},{65,97},{97,1},{2,34}... | collective-permute-start | bytes 884744 | tf_op jit(solution)/shard_map/ppermute | solution.py:123
  155.6 20.5 %collective-permute-start.17 = (bf16[4,288,128]{2,1,0:T(8,128)(2,1)}, bf16[4,288,128]{2,1,0:T(8,128)(2,1)}, u32[]{:S(2)}, u32[]{:S(2)}) collective-permute-start(bf16[4,288,128]{2,1,0:T(8,128)(2,1)} %get-tuple-element.38), channel_id=1, source_target_pairs={{0,64},{32,96},{64,0},{96,32},{1,65},{33,97},{65,1},{97,33},{2,66}... | collective-permute-start | bytes 884744 | tf_op jit(solution)/shard_map/ppermute | solution.py:123
  158.3 17.8 %collective-permute-start.18 = (bf16[4,288,128]{2,1,0:T(8,128)(2,1)}, bf16[4,288,128]{2,1,0:T(8,128)(2,1)}, u32[]{:S(2)}, u32[]{:S(2)}) collective-permute-start(bf16[4,288,128]{2,1,0:T(8,128)(2,1)} %get-tuple-element.39), channel_id=1, source_target_pairs={{0,96},{32,0},{64,32},{96,64},{1,97},{33,1},{65,33},{97,65},{2,98}... | collective-permute-start | bytes 884744 | tf_op jit(solution)/shard_map/ppermute | solution.py:123
  172.1 9.8 %collective-permute-start.11 = (bf16[2,288,128]{2,1,0:T(8,128)(2,1)}, bf16[2,288,128]{2,1,0:T(8,128)(2,1)}, u32[]{:S(2)}, u32[]{:S(2)}) collective-permute-start(bf16[2,288,128]{2,1,0:T(8,128)(2,1)} %get-tuple-element.33), channel_id=1, source_target_pairs={{0,32},{32,64},{64,96},{96,0},{1,33},{33,65},{65,97},{97,1},{2,34}... | collective-permute-start | bytes 442376 | tf_op jit(solution)/shard_map/ppermute | solution.py:123
  172.8 9.1 %collective-permute-start.12 = (bf16[2,288,128]{2,1,0:T(8,128)(2,1)}, bf16[2,288,128]{2,1,0:T(8,128)(2,1)}, u32[]{:S(2)}, u32[]{:S(2)}) collective-permute-start(bf16[2,288,128]{2,1,0:T(8,128)(2,1)} %get-tuple-element.34), channel_id=1, source_target_pairs={{0,64},{32,96},{64,0},{96,32},{1,65},{33,97},{65,1},{97,33},{2,66}... | collective-permute-start | bytes 442376 | tf_op jit(solution)/shard_map/ppermute | solution.py:123
  173.7 8.9 %collective-permute-start.13 = (bf16[2,288,128]{2,1,0:T(8,128)(2,1)}, bf16[2,288,128]{2,1,0:T(8,128)(2,1)}, u32[]{:S(2)}, u32[]{:S(2)}) collective-permute-start(bf16[2,288,128]{2,1,0:T(8,128)(2,1)} %get-tuple-element.35), channel_id=1, source_target_pairs={{0,96},{32,0},{64,32},{96,64},{1,97},{33,1},{65,33},{97,65},{2,98}... | collective-permute-start | bytes 442376 | tf_op jit(solution)/shard_map/ppermute | solution.py:123

commit v7 on v6

--- a/solution.py
+++ b/solution.py
@@ -476,8 +476,14 @@
     video, words = (video_q, video_k, video_v), (text_q, text_k, text_v)
     (f0, n0), (f1, n1) = CHUNKS
     (kv0,) = pack(video, [((1, 2), f0, n0, ROWS, True)])
-    (text,) = pack(words, [((0, 1, 2), 0, HD, HALF, False)])
-    kv1, q = pack(video, [((1, 2), f1, n1, ROWS, True), ((0,), 0, HD, ROWS, False)])
+    text, kv1, q = pack(
+        video + words,
+        [
+            ((3, 4, 5), 0, HD, HALF, False),
+            ((1, 2), f1, n1, ROWS, True),
+            ((0,), 0, HD, ROWS, False),
+        ],
+    )
     own, before, after = [], [], []
     for kv in (kv0, kv1):
         own.append(swap(kv, "uly"))

time: 185 us -> 185 us (level)
  waiting for transfers between devices: 29.4 us -> 38.5 us
  starting transfers between devices: 57.1 us -> 50.6 us
  Pallas kernels: 62.6 us -> 59.8 us
    ppermute x12, waiting for transfers between devices: 17.9 us -> 27.1 us  [around(): lax.ppermute(block, 'uly', [(i, (i + distance) % GROUP) for i in range(GR...]
    ppermute x3, starting transfers between devices: 5.42 us -> 0.57 us  [local(): other.append(lax.ppermute(mine[d], 'blk', [(i, i ^ 1) for i in range(BLK)]))]
    pallas_call x3 -> x2, Pallas kernels: 12.6 us -> 9.81 us  [pack(): pl.pallas_call(body, in_specs=[ANY] * len(arrays), out_specs=[ANY] * len(...]
    all_to_all x3, starting transfers between devices: 24.5 us -> 21.8 us  [swap(): return lax.all_to_all(array, axes, 0, 0, tiled=True)]
  transfers between devices with their start and end apart: 22 -> 22, of which waited for: 8 -> 7; matrix products, arithmetic and copies ran while one was open for 0% -> 0% of each run, Pallas kernels for 31% -> 29%
where the time goes in v7:
time: 185 us; the launch traced here: 184 us
  Pallas kernels  59.8 us (32%)
  starting transfers between devices  50.6 us (27%)
  waiting for transfers between devices  38.5 us (21%)
  blocking collectives  33.8 us (18%)
    pallas_call x2, Pallas kernels, video_attention(): pl.pallas_call(functools.partial(video_body, first, heads), in_specs=[SME...  34.1 us
    all_to_all x1, blocking collectives, swap(): return lax.all_to_all(array, axes, 0, 0, tiled=True)  33.8 us
    ppermute x12, waiting for transfers between devices, around(): lax.ppermute(block, 'uly', [(i, (i + distance) % GROUP) for i in range(GR...  27.1 us
    all_to_all x3, starting transfers between devices, swap(): return lax.all_to_all(array, axes, 0, 0, tiled=True)  21.8 us
    ppermute x12, starting transfers between devices, around(): lax.ppermute(block, 'uly', [(i, (i + distance) % GROUP) for i in range(GR...  17.1 us
    ppermute x4, starting transfers between devices, beside(): lax.ppermute(block, 'blk', [(i, i + distance) for i in range(BLK) if 0 <=...  11.2 us
    all_to_all x3, waiting for transfers between devices, swap(): return lax.all_to_all(array, axes, 0, 0, tiled=True)  10.6 us
    pallas_call x2, Pallas kernels, pack(): pl.pallas_call(body, in_specs=[ANY] * len(arrays), out_specs=[ANY] * len(...  9.81 us
  transfers between devices with their start and end apart: 22, of which 7 were waited for; matrix products, arithmetic and copies ran while one was open for 0% of the time, Pallas kernels for 29%

profile of v7, /device:TPU:0, one launch (start us, length us, event | category | flops | bytes accessed | tf_op | source)
XLA Modules:
  0.0 184.5 jit_solution(7577621677994829059)
XLA Ops:
  0.6 4.3 %shard_map.96 = bf16[4,2,4,288,128]{4,3,2,1,0:T(8,128)(2,1)} custom-call(bf16[288,3072]{1,0:T(8,128)(2,1)} %refs_0_.3, bf16[288,3072]{1,0:T(8,128)(2,1)} %refs_1_.3, bf16[288,3072]{1,0:T(8,128)(2,1)} %refs_2_.3), custom_call_target="tpu_custom_call" | custom-call | tf_op jit(solution)/shard_map/pallas_call | solution.py:105
  5.0 33.8 %all_to_all.20.refs_13_.refs_8_ = bf16[4,2,4,288,128]{4,3,2,1,0:T(8,128)(2,1)} all-to-all(bf16[4,2,4,288,128]{4,3,2,1,0:T(8,128)(2,1)} %shard_map.96), channel_id=1, replica_groups=mesh['uly'=4,'blk'=32] {'uly'}, dimensions={0} | all-to-all | bytes 4718592 | tf_op jit(solution)/shard_map/all_to_all | solution.py:134
  38.8 1.3 collective-permute-start.15
  40.1 4.5 %collective-permute-start.14 = (bf16[4,2,4,288,128]{4,3,2,1,0:T(8,128)(2,1)}, bf16[4,2,4,288,128]{4,3,2,1,0:T(8,128)(2,1)}, u32[]{:S(2)}, u32[]{:S(2)}) collective-permute-start(bf16[4,2,4,288,128]{4,3,2,1,0:T(8,128)(2,1)} %all_to_all.20.refs_13_.refs_8_), channel_id=1, source_target_pairs={{0,1},{1,2},{2,3},{3,4},{4,5},{5,6},{6,7},{7,8},{8,9},{9,10},{10,1... | collective-permute-start | bytes 7077896 | tf_op jit(solution)/shard_map/ppermute | solution.py:138
  44.5 5.5 %shard_map.95 = (bf16[3,6,32,128]{3,2,1,0:T(8,128)(2,1)}, bf16[3,6,32,128]{3,2,1,0:T(8,128)(2,1)}, bf16[3,6,32,128]{3,2,1,0:T(8,128)(2,1)}, bf16[3,6,32,128]{3,2...) custom-call(bf16[288,3072]{1,0:T(8,128)(2,1)} %refs_0_.3, ...), custom_call_target="tpu_custom_call" | custom-call | tf_op jit(solution)/shard_map/pallas_call | solution.py:105
  50.0 0.0 copy-start.8
  50.0 0.0 copy-start.7
  50.1 0.0 copy-start.5
  50.1 0.0 copy-start.6
  50.1 4.4 %all-to-all-start = ((bf16[4,2,2,288,128]{4,3,2,1,0:T(8,128)(2,1)}), bf16[4,2,2,288,128]{4,3,2,1,0:T(8,128)(2,1)}, u32[]{:S(2)}, u32[]{:S(2)}) async-start(bf16[4,2,2,288,128]{4,3,2,1,0:T(8,128)(2,1)} %get-tuple-element.31), calls=%async_computation | async-start | bytes 2359296 | tf_op jit(solution)/shard_map/all_to_all | solution.py:134
  54.5 0.0 copy-done.8
  54.5 2.0 %collective-permute-start.3 = (bf16[3,6,32,128]{3,2,1,0:T(8,128)(2,1)S(1)}, bf16[3,6,32,128]{3,2,1,0:T(8,128)(2,1)S(1)}, u32[]{:S(2)}, u32[]{:S(2)}) collective-permute-start(bf16[3,6,32,128]{3,2,1,0:T(8,128)(2,1)S(1)} %copy-done.8), channel_id=1, source_target_pairs={{0,32},{32,64},{64,96},{96,0},{1,33},{33,65},{65,97},{97,1},{2,34}... | collective-permute-start | bytes 442376 | tf_op jit(solution)/shard_map/ppermute | solution.py:123
  56.5 0.0 copy-done.7
  56.5 2.7 %collective-permute-start.4 = (bf16[3,6,32,128]{3,2,1,0:T(8,128)(2,1)S(1)}, bf16[3,6,32,128]{3,2,1,0:T(8,128)(2,1)S(1)}, u32[]{:S(2)}, u32[]{:S(2)}) collective-permute-start(bf16[3,6,32,128]{3,2,1,0:T(8,128)(2,1)S(1)} %copy-done.7), channel_id=1, source_target_pairs={{0,64},{32,96},{64,0},{96,32},{1,65},{33,97},{65,1},{97,33},{2,66}... | collective-permute-start | bytes 442376 | tf_op jit(solution)/shard_map/ppermute | solution.py:123
  59.1 0.0 copy-done.5
  59.1 0.0 collective-permute-start
  59.2 18.8 %collective-permute-done.3.refs_5_.refs_1_ = bf16[3,6,32,128]{3,2,1,0:T(8,128)(2,1)S(1)} collective-permute-done((bf16[3,6,32,128]{3,2,1,0:T(8,128)(2,1)S(1)}, bf16[3,6,32,128]{3,2,1,0:T(8,128)(2,1)S(1)}, u32[]{:S(2)}, u32[]{:S(2)}) %collective-permute-start.3) | collective-permute-done | bytes 147488 | tf_op jit(solution)/shard_map/ppermute | solution.py:123
  78.0 0.0 copy-done.6
  78.0 0.0 collective-permute-start.5
  78.0 0.8 collective-permute-done.4.refs_6_.refs_2_
  78.8 0.0 copy-done
  78.8 0.0 collective-permute-start.6
  78.8 4.4 %collective-permute-done.5.refs_7_.refs_3_ = bf16[3,6,32,128]{3,2,1,0:T(8,128)(2,1)S(1)} collective-permute-done((bf16[3,6,32,128]{3,2,1,0:T(8,128)(2,1)S(1)}, bf16[3,6,32,128]{3,2,1,0:T(8,128)(2,1)S(1)}, u32[]{:S(2)}, u32[]{:S(2)}) %collective-permute-start.5) | collective-permute-done | bytes 147488 | tf_op jit(solution)/shard_map/ppermute | solution.py:123
  83.1 0.0 collective-permute-start.7
  83.1 0.0 collective-permute-done.6.refs_9_.refs_5_
  83.1 0.0 copy-done.1
  83.2 0.0 copy-start.3
  83.2 0.6 collective-permute-start.8
  83.7 0.8 collective-permute-done.7.refs_10_.refs_6_
  84.5 1.3 collective-permute-start.1
  85.8 0.0 collective-permute-done.8.refs_11_.refs_7_
  85.8 0.0 all-to-all-done.refs_13_.refs_9_
  85.8 1.3 collective-permute-start.10
  87.1 0.0 collective-permute-done.refs_1_
  87.2 4.1 %collective-permute-start.9 = (bf16[4,2,2,288,128]{4,3,2,1,0:T(8,128)(2,1)}, bf16[4,2,2,288,128]{4,3,2,1,0:T(8,128)(2,1)}, u32[]{:S(2)}, u32[]{:S(2)}) collective-permute-start(bf16[4,2,2,288,128]{4,3,2,1,0:T(8,128)(2,1)} %all-to-all-done.refs_13_.refs_9_), channel_id=1, source_target_pairs={{0,1},{1,2},{2,3},{3,4},{4,5},{5,6},{6,7},{7,8},{8,9},{9,10},{10,1... | collective-permute-start | bytes 3538952 | tf_op jit(solution)/shard_map/ppermute | solution.py:138
  91.9 7.8 %text_attention.1 = bf16[128,16,128]{2,1,0:T(8,128)(2,1)} custom-call(s32[1]{0:T(128)S(6)} %copy.12.length, bf16[3,6,32,128]{3,2,1,0:T(8,128)(2,1)} %get-tuple-element.26.refs_4_.refs_0_, bf16[3,6,32,128]{3,2,1,0:T(8,128)(2,1)} %copy-done, bf16[3,6,32,128]{3,2,1,0:T(8,128)(2,1)} %copy-done.1, bf16[3,6,32,128]{3,2,1,0:T(8,128)(2,1)} %copy-done.2, ...), custom_call_target="tpu_custom_call" | custom-call | tf_op jit(solution)/shard_map/text_attention/pallas_call | solution.py:233
  99.8 11.5 %all-to-all-start.2 = ((bf16[128,16,128]{2,1,0:T(8,128)(2,1)}), bf16[128,16,128]{2,1,0:T(8,128)(2,1)}, u32[]{:S(2)}, u32[]{:S(2)}) async-start(bf16[128,16,128]{2,1,0:T(8,128)(2,1)} %text_attention.1), calls=%async_computation.2 | async-start | bytes 1048576 | tf_op jit(solution)/shard_map/all_to_all | solution.py:134
  111.3 0.0 collective-permute-done.1.refs_2_
  111.3 2.2 %collective-permute-start.2 = (bf16[1,6,288,128]{3,2,1,0:T(8,128)(2,1)}, bf16[1,6,288,128]{3,2,1,0:T(8,128)(2,1)}, u32[]{:S(2)}, u32[]{:S(2)}) collective-permute-start(bf16[1,6,288,128]{3,2,1,0:T(8,128)(2,1)} %get-tuple-element.25), channel_id=1, source_target_pairs={{0,96},{32,0},{64,32},{96,64},{1,97},{33,1},{65,33},{97,65},{2,98}... | collective-permute-start | bytes 1327112 | tf_op jit(solution)/shard_map/ppermute | solution.py:123
  113.4 10.6 %all-to-all-done.2.in_ref = bf16[128,16,128]{2,1,0:T(8,128)(2,1)} async-done(((bf16[128,16,128]{2,1,0:T(8,128)(2,1)}), bf16[128,16,128]{2,1,0:T(8,128)(2,1)}, u32[]{:S(2)}, u32[]{:S(2)}) %all-to-all-start.2) | async-done | bytes 524320 | tf_op jit(solution)/shard_map/all_to_all | solution.py:134
  124.0 3.0 %combine.1 = bf16[32,4,16,128]{3,2,1,0:T(8,128)(2,1)} custom-call(bf16[128,16,128]{2,1,0:T(8,128)(2,1)} %all-to-all-done.2.in_ref), custom_call_target="tpu_custom_call" | custom-call | tf_op jit(solution)/shard_map/combine/pallas_call | solution.py:287
  127.1 5.9 %all-to-all-start.3 = ((bf16[128,16,128]{2,1,0:T(8,128)(2,1)}), bf16[128,16,128]{2,1,0:T(8,128)(2,1)}, u32[]{:S(2)}, u32[]{:S(2)}) async-start(bf16[128,16,128]{2,1,0:T(8,128)(2,1)} %bitcast.1), calls=%async_computation.3 | async-start | bytes 1048576 | tf_op jit(solution)/shard_map/all_to_all | solution.py:134
  133.0 0.0 collective-permute-done.2.refs_3_
  133.0 0.0 collective-permute-done.15.refs_14_
  133.0 0.0 collective-permute-done.14.refs_12_
  133.0 21.8 %video_attention.3 = (bf16[4,288,128]{2,1,0:T(8,128)(2,1)}, bf16[4,288,128]{2,1,0:T(8,128)(2,1)}, bf16[4,288,128]{2,1,0:T(8,128)(2,1)}, bf16[4,288,128]{2,1,0:T(8,128)(2,1)}) custom-call(s32[3,6]{1,0:T(4,128)} %tiles.3, s32[1]{0:T(128)S(6)} %copy.12.length, bf16[1,6,288,128]{3,2,1,0:T(8,128)(2,1)} %get-tuple-element.22.refs_0_, ...), custom_call_target="tpu_custom_call" | custom-call | tf_op jit(solution)/shard_map/video_attention/pallas_call | solution.py:379
  154.8 0.7 collective-permute-start.16
  155.5 2.7 %collective-permute-start.17 = (bf16[4,288,128]{2,1,0:T(8,128)(2,1)}, bf16[4,288,128]{2,1,0:T(8,128)(2,1)}, u32[]{:S(2)}, u32[]{:S(2)}) collective-permute-start(bf16[4,288,128]{2,1,0:T(8,128)(2,1)} %get-tuple-element.38), channel_id=1, source_target_pairs={{0,64},{32,96},{64,0},{96,32},{1,65},{33,97},{65,1},{97,33},{2,66}... | collective-permute-start | bytes 884744 | tf_op jit(solution)/shard_map/ppermute | solution.py:123
  158.2 1.4 collective-permute-start.18
  159.6 0.0 collective-permute-done.10.refs_14_
  159.6 0.0 collective-permute-done.9.refs_12_
  159.6 12.3 %video_attention.2 = (bf16[2,288,128]{2,1,0:T(8,128)(2,1)}, bf16[2,288,128]{2,1,0:T(8,128)(2,1)}, bf16[2,288,128]{2,1,0:T(8,128)(2,1)}, bf16[2,288,128]{2,1,0:T(8,128)(2,1)}) custom-call(s32[3,6]{1,0:T(4,128)} %tiles.3, s32[1]{0:T(128)S(6)} %copy.12.length, bf16[1,6,288,128]{3,2,1,0:T(8,128)(2,1)} %get-tuple-element.22.refs_0_, ...), custom_call_target="tpu_custom_call" | custom-call | tf_op jit(solution)/shard_map/video_attention/pallas_call | solution.py:379
  172.0 0.7 collective-permute-start.11
  172.6 0.9 collective-permute-start.12
  173.6 0.0 collective-permute-done.16.refs_1_
  173.6 2.5 %collective-permute-start.13 = (bf16[2,288,128]{2,1,0:T(8,128)(2,1)}, bf16[2,288,128]{2,1,0:T(8,128)(2,1)}, u32[]{:S(2)}, u32[]{:S(2)}) collective-permute-start(bf16[2,288,128]{2,1,0:T(8,128)(2,1)} %get-tuple-element.35), channel_id=1, source_target_pairs={{0,96},{32,0},{64,32},{96,64},{1,97},{33,1},{65,33},{97,65},{2,98}... | collective-permute-start | bytes 442376 | tf_op jit(solution)/shard_map/ppermute | solution.py:123
  176.1 0.0 all-to-all-done.3.refs_4_
  176.1 0.0 collective-permute-done.17.refs_2_
  176.1 0.0 collective-permute-done.18.refs_3_
  176.1 3.2 %first_rows.1 = (bf16[288,3072]{1,0:T(8,128)(2,1)}, bf16[64,3072]{1,0:T(8,128)(2,1)}) custom-call(bf16[4,288,128]{2,1,0:T(8,128)(2,1)} %get-tuple-element.36.refs_0_, bf16[4,288,128]{2,1,0:T(8,128)(2,1)} %collective-permute-done.16.refs_1_, bf16[4,288,128]{2,1,0:T(8,128)(2,1)} %collective-permute-done.17.refs_2_, ...), custom_call_target="tpu_custom_call" | custom-call | tf_op jit(solution)/shard_map/first_rows/pallas_call | solution.py:437
  179.3 2.5 %collective-permute-done.11.refs_1_ = bf16[2,288,128]{2,1,0:T(8,128)(2,1)} collective-permute-done((bf16[2,288,128]{2,1,0:T(8,128)(2,1)}, bf16[2,288,128]{2,1,0:T(8,128)(2,1)}, u32[]{:S(2)}, u32[]{:S(2)}) %collective-permute-start.11) | collective-permute-done | bytes 147488 | tf_op jit(solution)/shard_map/ppermute | solution.py:123
  181.8 0.0 collective-permute-done.12.refs_2_
  181.8 0.6 collective-permute-done.13.refs_3_
  182.4 1.9 %later_rows.1 = bf16[288,3072]{1,0:T(8,128)(2,1)} custom-call(bf16[2,288,128]{2,1,0:T(8,128)(2,1)} %get-tuple-element.32.refs_0_, bf16[2,288,128]{2,1,0:T(8,128)(2,1)} %collective-permute-done.11.refs_1_, bf16[2,288,128]{2,1,0:T(8,128)(2,1)} %collective-permute-done.12.refs_2_, ...), custom_call_target="tpu_custom_call", output_to_operand_aliasing={{}: (4, {})} | custom-call | tf_op jit(solution)/shard_map/later_rows/pallas_call | solution.py:459
  (7 shorter events, 0.0 us)
Async XLA Ops:
  38.8 94.2 %collective-permute-start.15 = (bf16[4,2,4,288,128]{4,3,2,1,0:T(8,128)(2,1)}, bf16[4,2,4,288,128]{4,3,2,1,0:T(8,128)(2,1)}, u32[]{:S(2)}, u32[]{:S(2)}) collective-permute-start(bf16[4,2,4,288,128]{4,3,2,1,0:T(8,128)(2,1)} %all_to_all.20.refs_13_.refs_8_), channel_id=1, source_target_pairs={{1,0},{2,1},{3,2},{4,3},{5,4},{6,5},{7,6},{8,7},{9,8},{10,9},{11,1... | collective-permute-start | bytes 7077896 | tf_op jit(solution)/shard_map/ppermute | solution.py:138
  40.1 93.0 %collective-permute-start.14 = (bf16[4,2,4,288,128]{4,3,2,1,0:T(8,128)(2,1)}, bf16[4,2,4,288,128]{4,3,2,1,0:T(8,128)(2,1)}, u32[]{:S(2)}, u32[]{:S(2)}) collective-permute-start(bf16[4,2,4,288,128]{4,3,2,1,0:T(8,128)(2,1)} %all_to_all.20.refs_13_.refs_8_), channel_id=1, source_target_pairs={{0,1},{1,2},{2,3},{3,4},{4,5},{5,6},{6,7},{7,8},{8,9},{9,10},{10,1... | collective-permute-start | bytes 7077896 | tf_op jit(solution)/shard_map/ppermute | solution.py:138
  50.0 4.5 %copy-start.8 = (bf16[3,6,32,128]{3,2,1,0:T(8,128)(2,1)S(1)}, bf16[3,6,32,128]{3,2,1,0:T(8,128)(2,1)}, u32[]{:S(2)}) copy-start(bf16[3,6,32,128]{3,2,1,0:T(8,128)(2,1)} %get-tuple-element.27) | copy-start | bytes 442372
  50.0 6.4 %copy-start.7 = (bf16[3,6,32,128]{3,2,1,0:T(8,128)(2,1)S(1)}, bf16[3,6,32,128]{3,2,1,0:T(8,128)(2,1)}, u32[]{:S(2)}) copy-start(bf16[3,6,32,128]{3,2,1,0:T(8,128)(2,1)} %get-tuple-element.28) | copy-start | bytes 442372
  50.1 9.1 %copy-start.5 = (bf16[1,6,288,128]{3,2,1,0:T(8,128)(2,1)S(1)}, bf16[1,6,288,128]{3,2,1,0:T(8,128)(2,1)}, u32[]{:S(2)}) copy-start(bf16[1,6,288,128]{3,2,1,0:T(8,128)(2,1)} %get-tuple-element.23) | copy-start | bytes 1327108
  50.1 27.9 %copy-start.6 = (bf16[3,6,32,128]{3,2,1,0:T(8,128)(2,1)S(1)}, bf16[3,6,32,128]{3,2,1,0:T(8,128)(2,1)}, u32[]{:S(2)}) copy-start(bf16[3,6,32,128]{3,2,1,0:T(8,128)(2,1)} %get-tuple-element.29) | copy-start | bytes 442372
  50.1 35.8 %all-to-all-start = ((bf16[4,2,2,288,128]{4,3,2,1,0:T(8,128)(2,1)}), bf16[4,2,2,288,128]{4,3,2,1,0:T(8,128)(2,1)}, u32[]{:S(2)}, u32[]{:S(2)}) async-start(bf16[4,2,2,288,128]{4,3,2,1,0:T(8,128)(2,1)} %get-tuple-element.31), calls=%async_computation | async-start | bytes 2359296 | tf_op jit(solution)/shard_map/all_to_all | solution.py:134
  54.5 23.5 %collective-permute-start.3 = (bf16[3,6,32,128]{3,2,1,0:T(8,128)(2,1)S(1)}, bf16[3,6,32,128]{3,2,1,0:T(8,128)(2,1)S(1)}, u32[]{:S(2)}, u32[]{:S(2)}) collective-permute-start(bf16[3,6,32,128]{3,2,1,0:T(8,128)(2,1)S(1)} %copy-done.8), channel_id=1, source_target_pairs={{0,32},{32,64},{64,96},{96,0},{1,33},{33,65},{65,97},{97,1},{2,34}... | collective-permute-start | bytes 442376 | tf_op jit(solution)/shard_map/ppermute | solution.py:123
  56.5 22.3 %collective-permute-start.4 = (bf16[3,6,32,128]{3,2,1,0:T(8,128)(2,1)S(1)}, bf16[3,6,32,128]{3,2,1,0:T(8,128)(2,1)S(1)}, u32[]{:S(2)}, u32[]{:S(2)}) collective-permute-start(bf16[3,6,32,128]{3,2,1,0:T(8,128)(2,1)S(1)} %copy-done.7), channel_id=1, source_target_pairs={{0,64},{32,96},{64,0},{96,32},{1,65},{33,97},{65,1},{97,33},{2,66}... | collective-permute-start | bytes 442376 | tf_op jit(solution)/shard_map/ppermute | solution.py:123
  59.1 28.0 %collective-permute-start = (bf16[1,6,288,128]{3,2,1,0:T(8,128)(2,1)S(1)}, bf16[1,6,288,128]{3,2,1,0:T(8,128)(2,1)}, u32[]{:S(2)}, u32[]{:S(2)}) collective-permute-start(bf16[1,6,288,128]{3,2,1,0:T(8,128)(2,1)S(1)} %copy-done.5), channel_id=1, source_target_pairs={{0,32},{32,64},{64,96},{96,0},{1,33},{33,65},{65,97},{97,1},{2,34}... | collective-permute-start | bytes 1327112 | tf_op jit(solution)/shard_map/ppermute | solution.py:123
  78.0 0.8 copy-start
  78.0 5.1 %collective-permute-start.5 = (bf16[3,6,32,128]{3,2,1,0:T(8,128)(2,1)S(1)}, bf16[3,6,32,128]{3,2,1,0:T(8,128)(2,1)S(1)}, u32[]{:S(2)}, u32[]{:S(2)}) collective-permute-start(bf16[3,6,32,128]{3,2,1,0:T(8,128)(2,1)S(1)} %copy-done.6), channel_id=1, source_target_pairs={{0,96},{32,0},{64,32},{96,64},{1,97},{33,1},{65,33},{97,65},{2,98}... | collective-permute-start | bytes 442376 | tf_op jit(solution)/shard_map/ppermute | solution.py:123
  78.8 4.4 %copy-start.1 = (bf16[3,6,32,128]{3,2,1,0:T(8,128)(2,1)}, bf16[3,6,32,128]{3,2,1,0:T(8,128)(2,1)S(1)}, u32[]{:S(2)}) copy-start(bf16[3,6,32,128]{3,2,1,0:T(8,128)(2,1)S(1)} %collective-permute-done.4.refs_6_.refs_2_) | copy-start | bytes 442372
  78.8 4.4 %collective-permute-start.6 = (bf16[3,6,32,128]{3,2,1,0:T(8,128)(2,1)S(1)}, bf16[3,6,32,128]{3,2,1,0:T(8,128)(2,1)S(1)}, u32[]{:S(2)}, u32[]{:S(2)}) collective-permute-start(bf16[3,6,32,128]{3,2,1,0:T(8,128)(2,1)S(1)} %collective-permute-done.3.refs_5_.refs_1_), channel_id=1, source_target_pairs={{0,1},{1,0},{2,3},{3,2},{4,5},{5,4},{6,7},{7,6},{8,9},{9,8},{10,11... | collective-permute-start | bytes 442376 | tf_op jit(solution)/shard_map/ppermute | solution.py:495
  83.1 1.4 copy-start.2
  83.1 1.4 collective-permute-start.7
  83.2 1.4 copy-start.3
  83.2 2.7 %collective-permute-start.8 = (bf16[3,6,32,128]{3,2,1,0:T(8,128)(2,1)S(1)}, bf16[3,6,32,128]{3,2,1,0:T(8,128)(2,1)}, u32[]{:S(2)}, u32[]{:S(2)}) collective-permute-start(bf16[3,6,32,128]{3,2,1,0:T(8,128)(2,1)S(1)} %collective-permute-done.5.refs_7_.refs_3_), channel_id=1, source_target_pairs={{0,1},{1,0},{2,3},{3,2},{4,5},{5,4},{6,7},{7,6},{8,9},{9,8},{10,11... | collective-permute-start | bytes 442376 | tf_op jit(solution)/shard_map/ppermute | solution.py:495
  84.5 1.3 copy-start.4
  84.5 26.7 %collective-permute-start.1 = (bf16[1,6,288,128]{3,2,1,0:T(8,128)(2,1)}, bf16[1,6,288,128]{3,2,1,0:T(8,128)(2,1)}, u32[]{:S(2)}, u32[]{:S(2)}) collective-permute-start(bf16[1,6,288,128]{3,2,1,0:T(8,128)(2,1)} %get-tuple-element.24), channel_id=1, source_target_pairs={{0,64},{32,96},{64,0},{96,32},{1,65},{33,97},{65,1},{97,33},{2,66}... | collective-permute-start | bytes 1327112 | tf_op jit(solution)/shard_map/ppermute | solution.py:123
  85.8 73.8 %collective-permute-start.10 = (bf16[4,2,2,288,128]{4,3,2,1,0:T(8,128)(2,1)}, bf16[4,2,2,288,128]{4,3,2,1,0:T(8,128)(2,1)}, u32[]{:S(2)}, u32[]{:S(2)}) collective-permute-start(bf16[4,2,2,288,128]{4,3,2,1,0:T(8,128)(2,1)} %all-to-all-done.refs_13_.refs_9_), channel_id=1, source_target_pairs={{1,0},{2,1},{3,2},{4,3},{5,4},{6,5},{7,6},{8,7},{9,8},{10,9},{11,1... | collective-permute-start | bytes 3538952 | tf_op jit(solution)/shard_map/ppermute | solution.py:138
  87.2 72.5 %collective-permute-start.9 = (bf16[4,2,2,288,128]{4,3,2,1,0:T(8,128)(2,1)}, bf16[4,2,2,288,128]{4,3,2,1,0:T(8,128)(2,1)}, u32[]{:S(2)}, u32[]{:S(2)}) collective-permute-start(bf16[4,2,2,288,128]{4,3,2,1,0:T(8,128)(2,1)} %all-to-all-done.refs_13_.refs_9_), channel_id=1, source_target_pairs={{0,1},{1,2},{2,3},{3,4},{4,5},{5,6},{6,7},{7,8},{8,9},{9,10},{10,1... | collective-permute-start | bytes 3538952 | tf_op jit(solution)/shard_map/ppermute | solution.py:138
  99.8 24.3 %all-to-all-start.2 = ((bf16[128,16,128]{2,1,0:T(8,128)(2,1)}), bf16[128,16,128]{2,1,0:T(8,128)(2,1)}, u32[]{:S(2)}, u32[]{:S(2)}) async-start(bf16[128,16,128]{2,1,0:T(8,128)(2,1)} %text_attention.1), calls=%async_computation.2 | async-start | bytes 1048576 | tf_op jit(solution)/shard_map/all_to_all | solution.py:134
  111.3 21.7 %collective-permute-start.2 = (bf16[1,6,288,128]{3,2,1,0:T(8,128)(2,1)}, bf16[1,6,288,128]{3,2,1,0:T(8,128)(2,1)}, u32[]{:S(2)}, u32[]{:S(2)}) collective-permute-start(bf16[1,6,288,128]{3,2,1,0:T(8,128)(2,1)} %get-tuple-element.25), channel_id=1, source_target_pairs={{0,96},{32,0},{64,32},{96,64},{1,97},{33,1},{65,33},{97,65},{2,98}... | collective-permute-start | bytes 1327112 | tf_op jit(solution)/shard_map/ppermute | solution.py:123
  127.1 49.1 %all-to-all-start.3 = ((bf16[128,16,128]{2,1,0:T(8,128)(2,1)}), bf16[128,16,128]{2,1,0:T(8,128)(2,1)}, u32[]{:S(2)}, u32[]{:S(2)}) async-start(bf16[128,16,128]{2,1,0:T(8,128)(2,1)} %bitcast.1), calls=%async_computation.3 | async-start | bytes 1048576 | tf_op jit(solution)/shard_map/all_to_all | solution.py:134
  154.8 18.8 %collective-permute-start.16 = (bf16[4,288,128]{2,1,0:T(8,128)(2,1)}, bf16[4,288,128]{2,1,0:T(8,128)(2,1)}, u32[]{:S(2)}, u32[]{:S(2)}) collective-permute-start(bf16[4,288,128]{2,1,0:T(8,128)(2,1)} %get-tuple-element.37), channel_id=1, source_target_pairs={{0,32},{32,64},{64,96},{96,0},{1,33},{33,65},{65,97},{97,1},{2,34}... | collective-permute-start | bytes 884744 | tf_op jit(solution)/shard_map/ppermute | solution.py:123
  155.5 20.6 %collective-permute-start.17 = (bf16[4,288,128]{2,1,0:T(8,128)(2,1)}, bf16[4,288,128]{2,1,0:T(8,128)(2,1)}, u32[]{:S(2)}, u32[]{:S(2)}) collective-permute-start(bf16[4,288,128]{2,1,0:T(8,128)(2,1)} %get-tuple-element.38), channel_id=1, source_target_pairs={{0,64},{32,96},{64,0},{96,32},{1,65},{33,97},{65,1},{97,33},{2,66}... | collective-permute-start | bytes 884744 | tf_op jit(solution)/shard_map/ppermute | solution.py:123
  158.2 17.9 %collective-permute-start.18 = (bf16[4,288,128]{2,1,0:T(8,128)(2,1)}, bf16[4,288,128]{2,1,0:T(8,128)(2,1)}, u32[]{:S(2)}, u32[]{:S(2)}) collective-permute-start(bf16[4,288,128]{2,1,0:T(8,128)(2,1)} %get-tuple-element.39), channel_id=1, source_target_pairs={{0,96},{32,0},{64,32},{96,64},{1,97},{33,1},{65,33},{97,65},{2,98}... | collective-permute-start | bytes 884744 | tf_op jit(solution)/shard_map/ppermute | solution.py:123
  172.0 9.8 %collective-permute-start.11 = (bf16[2,288,128]{2,1,0:T(8,128)(2,1)}, bf16[2,288,128]{2,1,0:T(8,128)(2,1)}, u32[]{:S(2)}, u32[]{:S(2)}) collective-permute-start(bf16[2,288,128]{2,1,0:T(8,128)(2,1)} %get-tuple-element.33), channel_id=1, source_target_pairs={{0,32},{32,64},{64,96},{96,0},{1,33},{33,65},{65,97},{97,1},{2,34}... | collective-permute-start | bytes 442376 | tf_op jit(solution)/shard_map/ppermute | solution.py:123
  172.6 9.1 %collective-permute-start.12 = (bf16[2,288,128]{2,1,0:T(8,128)(2,1)}, bf16[2,288,128]{2,1,0:T(8,128)(2,1)}, u32[]{:S(2)}, u32[]{:S(2)}) collective-permute-start(bf16[2,288,128]{2,1,0:T(8,128)(2,1)} %get-tuple-element.34), channel_id=1, source_target_pairs={{0,64},{32,96},{64,0},{96,32},{1,65},{33,97},{65,1},{97,33},{2,66}... | collective-permute-start | bytes 442376 | tf_op jit(solution)/shard_map/ppermute | solution.py:123
  173.6 8.8 %collective-permute-start.13 = (bf16[2,288,128]{2,1,0:T(8,128)(2,1)}, bf16[2,288,128]{2,1,0:T(8,128)(2,1)}, u32[]{:S(2)}, u32[]{:S(2)}) collective-permute-start(bf16[2,288,128]{2,1,0:T(8,128)(2,1)} %get-tuple-element.35), channel_id=1, source_target_pairs={{0,96},{32,0},{64,32},{96,64},{1,97},{33,1},{65,33},{97,65},{2,98}... | collective-permute-start | bytes 442376 | tf_op jit(solution)/shard_map/ppermute | solution.py:123

commit v8 on v7

--- a/solution.py
+++ b/solution.py
@@ -85,14 +85,19 @@
                 group = d if together else place(d % GROUP)
                 here = held[n].at[d] if together else held[n]
                 there = dst[n].at[d] if together else dst[n]
-                pairs = [
-                    (ins[k].at[which, column(group * HD + first + h)], here.at[i, h])
-                    for i, k in enumerate(numbers)
-                    for h in range(heads)
-                ]
-                base = sum(len(r) for r in reads)
-                reads.append([pltpu.make_async_copy(x, y, in_sems.at[base + i]) for i, (x, y) in enumerate(pairs)])
-                writes.append(pltpu.make_async_copy(here, there, out_sems.at[len(writes)]))
+                for i, k in enumerate(numbers):
+                    base = sum(len(r) for r in reads)
+                    reads.append(
+                        [
+                            pltpu.make_async_copy(
+                                ins[k].at[which, column(group * HD + first + h)],
+                                here.at[i, h],
+                                in_sems.at[base + h],
+                            )
+                            for h in range(heads)
+                        ]
+                    )
+                    writes.append(pltpu.make_async_copy(here.at[i], there.at[i], out_sems.at[len(writes)]))
                 n += not together
             n += together
         for read in reads:

time: 185 us -> 185 us (level)
  no operation moved by 1% of the time
where the time goes in v8:
time: 185 us; the launch traced here: 184 us
  Pallas kernels  59.8 us (32%)
  starting transfers between devices  50.6 us (27%)
  waiting for transfers between devices  38.5 us (21%)
  blocking collectives  33.8 us (18%)
    pallas_call x2, Pallas kernels, video_attention(): pl.pallas_call(functools.partial(video_body, first, heads), in_specs=[SME...  34.1 us
    all_to_all x1, blocking collectives, swap(): return lax.all_to_all(array, axes, 0, 0, tiled=True)  33.8 us
    ppermute x12, waiting for transfers between devices, around(): lax.ppermute(block, 'uly', [(i, (i + distance) % GROUP) for i in range(GR...  27.1 us
    all_to_all x3, starting transfers between devices, swap(): return lax.all_to_all(array, axes, 0, 0, tiled=True)  21.8 us
    ppermute x12, starting transfers between devices, around(): lax.ppermute(block, 'uly', [(i, (i + distance) % GROUP) for i in range(GR...  17.1 us
    ppermute x4, starting transfers between devices, beside(): lax.ppermute(block, 'blk', [(i, i + distance) for i in range(BLK) if 0 <=...  11.2 us
    all_to_all x3, waiting for transfers between devices, swap(): return lax.all_to_all(array, axes, 0, 0, tiled=True)  10.6 us
    pallas_call x2, Pallas kernels, pack(): pl.pallas_call(body, in_specs=[ANY] * len(arrays), out_specs=[ANY] * len(...  9.72 us
  transfers between devices with their start and end apart: 22, of which 7 were waited for; matrix products, arithmetic and copies ran while one was open for 0% of the time, Pallas kernels for 29%

profile of v8, /device:TPU:0, one launch (start us, length us, event | category | flops | bytes accessed | tf_op | source)
XLA Modules:
  0.0 184.4 jit_solution(7792372403135932868)
XLA Ops:
  0.6 4.2 %shard_map.96 = bf16[4,2,4,288,128]{4,3,2,1,0:T(8,128)(2,1)} custom-call(bf16[288,3072]{1,0:T(8,128)(2,1)} %refs_0_.3, bf16[288,3072]{1,0:T(8,128)(2,1)} %refs_1_.3, bf16[288,3072]{1,0:T(8,128)(2,1)} %refs_2_.3), custom_call_target="tpu_custom_call" | custom-call | tf_op jit(solution)/shard_map/pallas_call | solution.py:110
  4.9 33.8 %all_to_all.20.refs_13_.refs_8_ = bf16[4,2,4,288,128]{4,3,2,1,0:T(8,128)(2,1)} all-to-all(bf16[4,2,4,288,128]{4,3,2,1,0:T(8,128)(2,1)} %shard_map.96), channel_id=1, replica_groups=mesh['uly'=4,'blk'=32] {'uly'}, dimensions={0} | all-to-all | bytes 4718592 | tf_op jit(solution)/shard_map/all_to_all | solution.py:139
  38.7 1.3 collective-permute-start.15
  40.0 4.5 %collective-permute-start.14 = (bf16[4,2,4,288,128]{4,3,2,1,0:T(8,128)(2,1)}, bf16[4,2,4,288,128]{4,3,2,1,0:T(8,128)(2,1)}, u32[]{:S(2)}, u32[]{:S(2)}) collective-permute-start(bf16[4,2,4,288,128]{4,3,2,1,0:T(8,128)(2,1)} %all_to_all.20.refs_13_.refs_8_), channel_id=1, source_target_pairs={{0,1},{1,2},{2,3},{3,4},{4,5},{5,6},{6,7},{7,8},{8,9},{9,10},{10,1... | collective-permute-start | bytes 7077896 | tf_op jit(solution)/shard_map/ppermute | solution.py:143
  44.4 5.5 %shard_map.95 = (bf16[3,6,32,128]{3,2,1,0:T(8,128)(2,1)}, bf16[3,6,32,128]{3,2,1,0:T(8,128)(2,1)}, bf16[3,6,32,128]{3,2,1,0:T(8,128)(2,1)}, bf16[3,6,32,128]{3,2...) custom-call(bf16[288,3072]{1,0:T(8,128)(2,1)} %refs_0_.3, ...), custom_call_target="tpu_custom_call" | custom-call | tf_op jit(solution)/shard_map/pallas_call | solution.py:110
  49.9 0.0 copy-start.8
  49.9 0.0 copy-start.7
  50.0 0.0 copy-start.5
  50.0 0.0 copy-start.6
  50.0 4.4 %all-to-all-start = ((bf16[4,2,2,288,128]{4,3,2,1,0:T(8,128)(2,1)}), bf16[4,2,2,288,128]{4,3,2,1,0:T(8,128)(2,1)}, u32[]{:S(2)}, u32[]{:S(2)}) async-start(bf16[4,2,2,288,128]{4,3,2,1,0:T(8,128)(2,1)} %get-tuple-element.31), calls=%async_computation | async-start | bytes 2359296 | tf_op jit(solution)/shard_map/all_to_all | solution.py:139
  54.4 0.0 copy-done.8
  54.4 2.0 %collective-permute-start.3 = (bf16[3,6,32,128]{3,2,1,0:T(8,128)(2,1)S(1)}, bf16[3,6,32,128]{3,2,1,0:T(8,128)(2,1)S(1)}, u32[]{:S(2)}, u32[]{:S(2)}) collective-permute-start(bf16[3,6,32,128]{3,2,1,0:T(8,128)(2,1)S(1)} %copy-done.8), channel_id=1, source_target_pairs={{0,32},{32,64},{64,96},{96,0},{1,33},{33,65},{65,97},{97,1},{2,34}... | collective-permute-start | bytes 442376 | tf_op jit(solution)/shard_map/ppermute | solution.py:128
  56.4 0.0 copy-done.7
  56.4 2.7 %collective-permute-start.4 = (bf16[3,6,32,128]{3,2,1,0:T(8,128)(2,1)S(1)}, bf16[3,6,32,128]{3,2,1,0:T(8,128)(2,1)S(1)}, u32[]{:S(2)}, u32[]{:S(2)}) collective-permute-start(bf16[3,6,32,128]{3,2,1,0:T(8,128)(2,1)S(1)} %copy-done.7), channel_id=1, source_target_pairs={{0,64},{32,96},{64,0},{96,32},{1,65},{33,97},{65,1},{97,33},{2,66}... | collective-permute-start | bytes 442376 | tf_op jit(solution)/shard_map/ppermute | solution.py:128
  59.0 0.0 copy-done.5
  59.1 0.0 collective-permute-start
  59.1 18.8 %collective-permute-done.3.refs_5_.refs_1_ = bf16[3,6,32,128]{3,2,1,0:T(8,128)(2,1)S(1)} collective-permute-done((bf16[3,6,32,128]{3,2,1,0:T(8,128)(2,1)S(1)}, bf16[3,6,32,128]{3,2,1,0:T(8,128)(2,1)S(1)}, u32[]{:S(2)}, u32[]{:S(2)}) %collective-permute-start.3) | collective-permute-done | bytes 147488 | tf_op jit(solution)/shard_map/ppermute | solution.py:128
  77.9 0.0 copy-done.6
  77.9 0.0 collective-permute-start.5
  77.9 0.8 collective-permute-done.4.refs_6_.refs_2_
  78.7 0.0 copy-done
  78.7 0.0 collective-permute-start.6
  78.7 4.4 %collective-permute-done.5.refs_7_.refs_3_ = bf16[3,6,32,128]{3,2,1,0:T(8,128)(2,1)S(1)} collective-permute-done((bf16[3,6,32,128]{3,2,1,0:T(8,128)(2,1)S(1)}, bf16[3,6,32,128]{3,2,1,0:T(8,128)(2,1)S(1)}, u32[]{:S(2)}, u32[]{:S(2)}) %collective-permute-start.5) | collective-permute-done | bytes 147488 | tf_op jit(solution)/shard_map/ppermute | solution.py:128
  83.0 0.0 collective-permute-start.7
  83.0 0.0 collective-permute-done.6.refs_9_.refs_5_
  83.1 0.0 copy-done.1
  83.1 0.0 copy-start.3
  83.1 0.6 collective-permute-start.8
  83.6 0.8 collective-permute-done.7.refs_10_.refs_6_
  84.4 1.3 collective-permute-start.1
  85.7 0.0 collective-permute-done.8.refs_11_.refs_7_
  85.7 0.0 all-to-all-done.refs_13_.refs_9_
  85.8 1.3 collective-permute-start.10
  87.1 0.0 collective-permute-done.refs_1_
  87.1 4.1 %collective-permute-start.9 = (bf16[4,2,2,288,128]{4,3,2,1,0:T(8,128)(2,1)}, bf16[4,2,2,288,128]{4,3,2,1,0:T(8,128)(2,1)}, u32[]{:S(2)}, u32[]{:S(2)}) collective-permute-start(bf16[4,2,2,288,128]{4,3,2,1,0:T(8,128)(2,1)} %all-to-all-done.refs_13_.refs_9_), channel_id=1, source_target_pairs={{0,1},{1,2},{2,3},{3,4},{4,5},{5,6},{6,7},{7,8},{8,9},{9,10},{10,1... | collective-permute-start | bytes 3538952 | tf_op jit(solution)/shard_map/ppermute | solution.py:143
  91.8 7.8 %text_attention.1 = bf16[128,16,128]{2,1,0:T(8,128)(2,1)} custom-call(s32[1]{0:T(128)S(6)} %copy.12.length, bf16[3,6,32,128]{3,2,1,0:T(8,128)(2,1)} %get-tuple-element.26.refs_4_.refs_0_, bf16[3,6,32,128]{3,2,1,0:T(8,128)(2,1)} %copy-done, bf16[3,6,32,128]{3,2,1,0:T(8,128)(2,1)} %copy-done.1, bf16[3,6,32,128]{3,2,1,0:T(8,128)(2,1)} %copy-done.2, ...), custom_call_target="tpu_custom_call" | custom-call | tf_op jit(solution)/shard_map/text_attention/pallas_call | solution.py:238
  99.7 11.5 %all-to-all-start.2 = ((bf16[128,16,128]{2,1,0:T(8,128)(2,1)}), bf16[128,16,128]{2,1,0:T(8,128)(2,1)}, u32[]{:S(2)}, u32[]{:S(2)}) async-start(bf16[128,16,128]{2,1,0:T(8,128)(2,1)} %text_attention.1), calls=%async_computation.2 | async-start | bytes 1048576 | tf_op jit(solution)/shard_map/all_to_all | solution.py:139
  111.2 0.0 collective-permute-done.1.refs_2_
  111.2 2.2 %collective-permute-start.2 = (bf16[1,6,288,128]{3,2,1,0:T(8,128)(2,1)}, bf16[1,6,288,128]{3,2,1,0:T(8,128)(2,1)}, u32[]{:S(2)}, u32[]{:S(2)}) collective-permute-start(bf16[1,6,288,128]{3,2,1,0:T(8,128)(2,1)} %get-tuple-element.25), channel_id=1, source_target_pairs={{0,96},{32,0},{64,32},{96,64},{1,97},{33,1},{65,33},{97,65},{2,98}... | collective-permute-start | bytes 1327112 | tf_op jit(solution)/shard_map/ppermute | solution.py:128
  113.3 10.6 %all-to-all-done.2.in_ref = bf16[128,16,128]{2,1,0:T(8,128)(2,1)} async-done(((bf16[128,16,128]{2,1,0:T(8,128)(2,1)}), bf16[128,16,128]{2,1,0:T(8,128)(2,1)}, u32[]{:S(2)}, u32[]{:S(2)}) %all-to-all-start.2) | async-done | bytes 524320 | tf_op jit(solution)/shard_map/all_to_all | solution.py:139
  124.0 3.0 %combine.1 = bf16[32,4,16,128]{3,2,1,0:T(8,128)(2,1)} custom-call(bf16[128,16,128]{2,1,0:T(8,128)(2,1)} %all-to-all-done.2.in_ref), custom_call_target="tpu_custom_call" | custom-call | tf_op jit(solution)/shard_map/combine/pallas_call | solution.py:292
  127.0 5.9 %all-to-all-start.3 = ((bf16[128,16,128]{2,1,0:T(8,128)(2,1)}), bf16[128,16,128]{2,1,0:T(8,128)(2,1)}, u32[]{:S(2)}, u32[]{:S(2)}) async-start(bf16[128,16,128]{2,1,0:T(8,128)(2,1)} %bitcast.1), calls=%async_computation.3 | async-start | bytes 1048576 | tf_op jit(solution)/shard_map/all_to_all | solution.py:139
  132.9 0.0 collective-permute-done.2.refs_3_
  132.9 0.0 collective-permute-done.15.refs_14_
  132.9 0.0 collective-permute-done.14.refs_12_
  132.9 21.8 %video_attention.3 = (bf16[4,288,128]{2,1,0:T(8,128)(2,1)}, bf16[4,288,128]{2,1,0:T(8,128)(2,1)}, bf16[4,288,128]{2,1,0:T(8,128)(2,1)}, bf16[4,288,128]{2,1,0:T(8,128)(2,1)}) custom-call(s32[3,6]{1,0:T(4,128)} %tiles.3, s32[1]{0:T(128)S(6)} %copy.12.length, bf16[1,6,288,128]{3,2,1,0:T(8,128)(2,1)} %get-tuple-element.22.refs_0_, ...), custom_call_target="tpu_custom_call" | custom-call | tf_op jit(solution)/shard_map/video_attention/pallas_call | solution.py:384
  154.7 0.7 collective-permute-start.16
  155.4 2.7 %collective-permute-start.17 = (bf16[4,288,128]{2,1,0:T(8,128)(2,1)}, bf16[4,288,128]{2,1,0:T(8,128)(2,1)}, u32[]{:S(2)}, u32[]{:S(2)}) collective-permute-start(bf16[4,288,128]{2,1,0:T(8,128)(2,1)} %get-tuple-element.38), channel_id=1, source_target_pairs={{0,64},{32,96},{64,0},{96,32},{1,65},{33,97},{65,1},{97,33},{2,66}... | collective-permute-start | bytes 884744 | tf_op jit(solution)/shard_map/ppermute | solution.py:128
  158.1 1.4 collective-permute-start.18
  159.5 0.0 collective-permute-done.10.refs_14_
  159.5 0.0 collective-permute-done.9.refs_12_
  159.5 12.3 %video_attention.2 = (bf16[2,288,128]{2,1,0:T(8,128)(2,1)}, bf16[2,288,128]{2,1,0:T(8,128)(2,1)}, bf16[2,288,128]{2,1,0:T(8,128)(2,1)}, bf16[2,288,128]{2,1,0:T(8,128)(2,1)}) custom-call(s32[3,6]{1,0:T(4,128)} %tiles.3, s32[1]{0:T(128)S(6)} %copy.12.length, bf16[1,6,288,128]{3,2,1,0:T(8,128)(2,1)} %get-tuple-element.22.refs_0_, ...), custom_call_target="tpu_custom_call" | custom-call | tf_op jit(solution)/shard_map/video_attention/pallas_call | solution.py:384
  171.9 0.7 collective-permute-start.11
  172.5 0.9 collective-permute-start.12
  173.5 0.0 collective-permute-done.16.refs_1_
  173.5 2.5 %collective-permute-start.13 = (bf16[2,288,128]{2,1,0:T(8,128)(2,1)}, bf16[2,288,128]{2,1,0:T(8,128)(2,1)}, u32[]{:S(2)}, u32[]{:S(2)}) collective-permute-start(bf16[2,288,128]{2,1,0:T(8,128)(2,1)} %get-tuple-element.35), channel_id=1, source_target_pairs={{0,96},{32,0},{64,32},{96,64},{1,97},{33,1},{65,33},{97,65},{2,98}... | collective-permute-start | bytes 442376 | tf_op jit(solution)/shard_map/ppermute | solution.py:128
  176.0 0.0 all-to-all-done.3.refs_4_
  176.0 0.0 collective-permute-done.17.refs_2_
  176.0 0.0 collective-permute-done.18.refs_3_
  176.0 3.2 %first_rows.1 = (bf16[288,3072]{1,0:T(8,128)(2,1)}, bf16[64,3072]{1,0:T(8,128)(2,1)}) custom-call(bf16[4,288,128]{2,1,0:T(8,128)(2,1)} %get-tuple-element.36.refs_0_, bf16[4,288,128]{2,1,0:T(8,128)(2,1)} %collective-permute-done.16.refs_1_, bf16[4,288,128]{2,1,0:T(8,128)(2,1)} %collective-permute-done.17.refs_2_, ...), custom_call_target="tpu_custom_call" | custom-call | tf_op jit(solution)/shard_map/first_rows/pallas_call | solution.py:442
  179.2 2.5 %collective-permute-done.11.refs_1_ = bf16[2,288,128]{2,1,0:T(8,128)(2,1)} collective-permute-done((bf16[2,288,128]{2,1,0:T(8,128)(2,1)}, bf16[2,288,128]{2,1,0:T(8,128)(2,1)}, u32[]{:S(2)}, u32[]{:S(2)}) %collective-permute-start.11) | collective-permute-done | bytes 147488 | tf_op jit(solution)/shard_map/ppermute | solution.py:128
  181.7 0.0 collective-permute-done.12.refs_2_
  181.7 0.6 collective-permute-done.13.refs_3_
  182.3 1.9 %later_rows.1 = bf16[288,3072]{1,0:T(8,128)(2,1)} custom-call(bf16[2,288,128]{2,1,0:T(8,128)(2,1)} %get-tuple-element.32.refs_0_, bf16[2,288,128]{2,1,0:T(8,128)(2,1)} %collective-permute-done.11.refs_1_, bf16[2,288,128]{2,1,0:T(8,128)(2,1)} %collective-permute-done.12.refs_2_, ...), custom_call_target="tpu_custom_call", output_to_operand_aliasing={{}: (4, {})} | custom-call | tf_op jit(solution)/shard_map/later_rows/pallas_call | solution.py:464
  (7 shorter events, 0.0 us)
Async XLA Ops:
  38.7 94.2 %collective-permute-start.15 = (bf16[4,2,4,288,128]{4,3,2,1,0:T(8,128)(2,1)}, bf16[4,2,4,288,128]{4,3,2,1,0:T(8,128)(2,1)}, u32[]{:S(2)}, u32[]{:S(2)}) collective-permute-start(bf16[4,2,4,288,128]{4,3,2,1,0:T(8,128)(2,1)} %all_to_all.20.refs_13_.refs_8_), channel_id=1, source_target_pairs={{1,0},{2,1},{3,2},{4,3},{5,4},{6,5},{7,6},{8,7},{9,8},{10,9},{11,1... | collective-permute-start | bytes 7077896 | tf_op jit(solution)/shard_map/ppermute | solution.py:143
  40.0 93.0 %collective-permute-start.14 = (bf16[4,2,4,288,128]{4,3,2,1,0:T(8,128)(2,1)}, bf16[4,2,4,288,128]{4,3,2,1,0:T(8,128)(2,1)}, u32[]{:S(2)}, u32[]{:S(2)}) collective-permute-start(bf16[4,2,4,288,128]{4,3,2,1,0:T(8,128)(2,1)} %all_to_all.20.refs_13_.refs_8_), channel_id=1, source_target_pairs={{0,1},{1,2},{2,3},{3,4},{4,5},{5,6},{6,7},{7,8},{8,9},{9,10},{10,1... | collective-permute-start | bytes 7077896 | tf_op jit(solution)/shard_map/ppermute | solution.py:143
  49.9 4.5 %copy-start.8 = (bf16[3,6,32,128]{3,2,1,0:T(8,128)(2,1)S(1)}, bf16[3,6,32,128]{3,2,1,0:T(8,128)(2,1)}, u32[]{:S(2)}) copy-start(bf16[3,6,32,128]{3,2,1,0:T(8,128)(2,1)} %get-tuple-element.27) | copy-start | bytes 442372
  49.9 6.4 %copy-start.7 = (bf16[3,6,32,128]{3,2,1,0:T(8,128)(2,1)S(1)}, bf16[3,6,32,128]{3,2,1,0:T(8,128)(2,1)}, u32[]{:S(2)}) copy-start(bf16[3,6,32,128]{3,2,1,0:T(8,128)(2,1)} %get-tuple-element.28) | copy-start | bytes 442372
  50.0 9.1 %copy-start.5 = (bf16[1,6,288,128]{3,2,1,0:T(8,128)(2,1)S(1)}, bf16[1,6,288,128]{3,2,1,0:T(8,128)(2,1)}, u32[]{:S(2)}) copy-start(bf16[1,6,288,128]{3,2,1,0:T(8,128)(2,1)} %get-tuple-element.23) | copy-start | bytes 1327108
  50.0 27.9 %copy-start.6 = (bf16[3,6,32,128]{3,2,1,0:T(8,128)(2,1)S(1)}, bf16[3,6,32,128]{3,2,1,0:T(8,128)(2,1)}, u32[]{:S(2)}) copy-start(bf16[3,6,32,128]{3,2,1,0:T(8,128)(2,1)} %get-tuple-element.29) | copy-start | bytes 442372
  50.0 35.8 %all-to-all-start = ((bf16[4,2,2,288,128]{4,3,2,1,0:T(8,128)(2,1)}), bf16[4,2,2,288,128]{4,3,2,1,0:T(8,128)(2,1)}, u32[]{:S(2)}, u32[]{:S(2)}) async-start(bf16[4,2,2,288,128]{4,3,2,1,0:T(8,128)(2,1)} %get-tuple-element.31), calls=%async_computation | async-start | bytes 2359296 | tf_op jit(solution)/shard_map/all_to_all | solution.py:139
  54.4 23.5 %collective-permute-start.3 = (bf16[3,6,32,128]{3,2,1,0:T(8,128)(2,1)S(1)}, bf16[3,6,32,128]{3,2,1,0:T(8,128)(2,1)S(1)}, u32[]{:S(2)}, u32[]{:S(2)}) collective-permute-start(bf16[3,6,32,128]{3,2,1,0:T(8,128)(2,1)S(1)} %copy-done.8), channel_id=1, source_target_pairs={{0,32},{32,64},{64,96},{96,0},{1,33},{33,65},{65,97},{97,1},{2,34}... | collective-permute-start | bytes 442376 | tf_op jit(solution)/shard_map/ppermute | solution.py:128
  56.4 22.3 %collective-permute-start.4 = (bf16[3,6,32,128]{3,2,1,0:T(8,128)(2,1)S(1)}, bf16[3,6,32,128]{3,2,1,0:T(8,128)(2,1)S(1)}, u32[]{:S(2)}, u32[]{:S(2)}) collective-permute-start(bf16[3,6,32,128]{3,2,1,0:T(8,128)(2,1)S(1)} %copy-done.7), channel_id=1, source_target_pairs={{0,64},{32,96},{64,0},{96,32},{1,65},{33,97},{65,1},{97,33},{2,66}... | collective-permute-start | bytes 442376 | tf_op jit(solution)/shard_map/ppermute | solution.py:128
  59.1 28.0 %collective-permute-start = (bf16[1,6,288,128]{3,2,1,0:T(8,128)(2,1)S(1)}, bf16[1,6,288,128]{3,2,1,0:T(8,128)(2,1)}, u32[]{:S(2)}, u32[]{:S(2)}) collective-permute-start(bf16[1,6,288,128]{3,2,1,0:T(8,128)(2,1)S(1)} %copy-done.5), channel_id=1, source_target_pairs={{0,32},{32,64},{64,96},{96,0},{1,33},{33,65},{65,97},{97,1},{2,34}... | collective-permute-start | bytes 1327112 | tf_op jit(solution)/shard_map/ppermute | solution.py:128
  77.9 0.8 copy-start
  77.9 5.1 %collective-permute-start.5 = (bf16[3,6,32,128]{3,2,1,0:T(8,128)(2,1)S(1)}, bf16[3,6,32,128]{3,2,1,0:T(8,128)(2,1)S(1)}, u32[]{:S(2)}, u32[]{:S(2)}) collective-permute-start(bf16[3,6,32,128]{3,2,1,0:T(8,128)(2,1)S(1)} %copy-done.6), channel_id=1, source_target_pairs={{0,96},{32,0},{64,32},{96,64},{1,97},{33,1},{65,33},{97,65},{2,98}... | collective-permute-start | bytes 442376 | tf_op jit(solution)/shard_map/ppermute | solution.py:128
  78.7 4.4 %copy-start.1 = (bf16[3,6,32,128]{3,2,1,0:T(8,128)(2,1)}, bf16[3,6,32,128]{3,2,1,0:T(8,128)(2,1)S(1)}, u32[]{:S(2)}) copy-start(bf16[3,6,32,128]{3,2,1,0:T(8,128)(2,1)S(1)} %collective-permute-done.4.refs_6_.refs_2_) | copy-start | bytes 442372
  78.7 4.4 %collective-permute-start.6 = (bf16[3,6,32,128]{3,2,1,0:T(8,128)(2,1)S(1)}, bf16[3,6,32,128]{3,2,1,0:T(8,128)(2,1)S(1)}, u32[]{:S(2)}, u32[]{:S(2)}) collective-permute-start(bf16[3,6,32,128]{3,2,1,0:T(8,128)(2,1)S(1)} %collective-permute-done.3.refs_5_.refs_1_), channel_id=1, source_target_pairs={{0,1},{1,0},{2,3},{3,2},{4,5},{5,4},{6,7},{7,6},{8,9},{9,8},{10,11... | collective-permute-start | bytes 442376 | tf_op jit(solution)/shard_map/ppermute | solution.py:500
  83.0 1.4 copy-start.2
  83.0 1.4 collective-permute-start.7
  83.1 1.4 copy-start.3
  83.1 2.7 %collective-permute-start.8 = (bf16[3,6,32,128]{3,2,1,0:T(8,128)(2,1)S(1)}, bf16[3,6,32,128]{3,2,1,0:T(8,128)(2,1)}, u32[]{:S(2)}, u32[]{:S(2)}) collective-permute-start(bf16[3,6,32,128]{3,2,1,0:T(8,128)(2,1)S(1)} %collective-permute-done.5.refs_7_.refs_3_), channel_id=1, source_target_pairs={{0,1},{1,0},{2,3},{3,2},{4,5},{5,4},{6,7},{7,6},{8,9},{9,8},{10,11... | collective-permute-start | bytes 442376 | tf_op jit(solution)/shard_map/ppermute | solution.py:500
  84.4 1.3 copy-start.4
  84.4 26.7 %collective-permute-start.1 = (bf16[1,6,288,128]{3,2,1,0:T(8,128)(2,1)}, bf16[1,6,288,128]{3,2,1,0:T(8,128)(2,1)}, u32[]{:S(2)}, u32[]{:S(2)}) collective-permute-start(bf16[1,6,288,128]{3,2,1,0:T(8,128)(2,1)} %get-tuple-element.24), channel_id=1, source_target_pairs={{0,64},{32,96},{64,0},{96,32},{1,65},{33,97},{65,1},{97,33},{2,66}... | collective-permute-start | bytes 1327112 | tf_op jit(solution)/shard_map/ppermute | solution.py:128
  85.8 73.8 %collective-permute-start.10 = (bf16[4,2,2,288,128]{4,3,2,1,0:T(8,128)(2,1)}, bf16[4,2,2,288,128]{4,3,2,1,0:T(8,128)(2,1)}, u32[]{:S(2)}, u32[]{:S(2)}) collective-permute-start(bf16[4,2,2,288,128]{4,3,2,1,0:T(8,128)(2,1)} %all-to-all-done.refs_13_.refs_9_), channel_id=1, source_target_pairs={{1,0},{2,1},{3,2},{4,3},{5,4},{6,5},{7,6},{8,7},{9,8},{10,9},{11,1... | collective-permute-start | bytes 3538952 | tf_op jit(solution)/shard_map/ppermute | solution.py:143
  87.1 72.5 %collective-permute-start.9 = (bf16[4,2,2,288,128]{4,3,2,1,0:T(8,128)(2,1)}, bf16[4,2,2,288,128]{4,3,2,1,0:T(8,128)(2,1)}, u32[]{:S(2)}, u32[]{:S(2)}) collective-permute-start(bf16[4,2,2,288,128]{4,3,2,1,0:T(8,128)(2,1)} %all-to-all-done.refs_13_.refs_9_), channel_id=1, source_target_pairs={{0,1},{1,2},{2,3},{3,4},{4,5},{5,6},{6,7},{7,8},{8,9},{9,10},{10,1... | collective-permute-start | bytes 3538952 | tf_op jit(solution)/shard_map/ppermute | solution.py:143
  99.7 24.3 %all-to-all-start.2 = ((bf16[128,16,128]{2,1,0:T(8,128)(2,1)}), bf16[128,16,128]{2,1,0:T(8,128)(2,1)}, u32[]{:S(2)}, u32[]{:S(2)}) async-start(bf16[128,16,128]{2,1,0:T(8,128)(2,1)} %text_attention.1), calls=%async_computation.2 | async-start | bytes 1048576 | tf_op jit(solution)/shard_map/all_to_all | solution.py:139
  111.2 21.7 %collective-permute-start.2 = (bf16[1,6,288,128]{3,2,1,0:T(8,128)(2,1)}, bf16[1,6,288,128]{3,2,1,0:T(8,128)(2,1)}, u32[]{:S(2)}, u32[]{:S(2)}) collective-permute-start(bf16[1,6,288,128]{3,2,1,0:T(8,128)(2,1)} %get-tuple-element.25), channel_id=1, source_target_pairs={{0,96},{32,0},{64,32},{96,64},{1,97},{33,1},{65,33},{97,65},{2,98}... | collective-permute-start | bytes 1327112 | tf_op jit(solution)/shard_map/ppermute | solution.py:128
  127.0 49.1 %all-to-all-start.3 = ((bf16[128,16,128]{2,1,0:T(8,128)(2,1)}), bf16[128,16,128]{2,1,0:T(8,128)(2,1)}, u32[]{:S(2)}, u32[]{:S(2)}) async-start(bf16[128,16,128]{2,1,0:T(8,128)(2,1)} %bitcast.1), calls=%async_computation.3 | async-start | bytes 1048576 | tf_op jit(solution)/shard_map/all_to_all | solution.py:139
  154.7 18.8 %collective-permute-start.16 = (bf16[4,288,128]{2,1,0:T(8,128)(2,1)}, bf16[4,288,128]{2,1,0:T(8,128)(2,1)}, u32[]{:S(2)}, u32[]{:S(2)}) collective-permute-start(bf16[4,288,128]{2,1,0:T(8,128)(2,1)} %get-tuple-element.37), channel_id=1, source_target_pairs={{0,32},{32,64},{64,96},{96,0},{1,33},{33,65},{65,97},{97,1},{2,34}... | collective-permute-start | bytes 884744 | tf_op jit(solution)/shard_map/ppermute | solution.py:128
  155.4 20.6 %collective-permute-start.17 = (bf16[4,288,128]{2,1,0:T(8,128)(2,1)}, bf16[4,288,128]{2,1,0:T(8,128)(2,1)}, u32[]{:S(2)}, u32[]{:S(2)}) collective-permute-start(bf16[4,288,128]{2,1,0:T(8,128)(2,1)} %get-tuple-element.38), channel_id=1, source_target_pairs={{0,64},{32,96},{64,0},{96,32},{1,65},{33,97},{65,1},{97,33},{2,66}... | collective-permute-start | bytes 884744 | tf_op jit(solution)/shard_map/ppermute | solution.py:128
  158.1 17.9 %collective-permute-start.18 = (bf16[4,288,128]{2,1,0:T(8,128)(2,1)}, bf16[4,288,128]{2,1,0:T(8,128)(2,1)}, u32[]{:S(2)}, u32[]{:S(2)}) collective-permute-start(bf16[4,288,128]{2,1,0:T(8,128)(2,1)} %get-tuple-element.39), channel_id=1, source_target_pairs={{0,96},{32,0},{64,32},{96,64},{1,97},{33,1},{65,33},{97,65},{2,98}... | collective-permute-start | bytes 884744 | tf_op jit(solution)/shard_map/ppermute | solution.py:128
  171.9 9.8 %collective-permute-start.11 = (bf16[2,288,128]{2,1,0:T(8,128)(2,1)}, bf16[2,288,128]{2,1,0:T(8,128)(2,1)}, u32[]{:S(2)}, u32[]{:S(2)}) collective-permute-start(bf16[2,288,128]{2,1,0:T(8,128)(2,1)} %get-tuple-element.33), channel_id=1, source_target_pairs={{0,32},{32,64},{64,96},{96,0},{1,33},{33,65},{65,97},{97,1},{2,34}... | collective-permute-start | bytes 442376 | tf_op jit(solution)/shard_map/ppermute | solution.py:128
  172.5 9.1 %collective-permute-start.12 = (bf16[2,288,128]{2,1,0:T(8,128)(2,1)}, bf16[2,288,128]{2,1,0:T(8,128)(2,1)}, u32[]{:S(2)}, u32[]{:S(2)}) collective-permute-start(bf16[2,288,128]{2,1,0:T(8,128)(2,1)} %get-tuple-element.34), channel_id=1, source_target_pairs={{0,64},{32,96},{64,0},{96,32},{1,65},{33,97},{65,1},{97,33},{2,66}... | collective-permute-start | bytes 442376 | tf_op jit(solution)/shard_map/ppermute | solution.py:128
  173.5 8.8 %collective-permute-start.13 = (bf16[2,288,128]{2,1,0:T(8,128)(2,1)}, bf16[2,288,128]{2,1,0:T(8,128)(2,1)}, u32[]{:S(2)}, u32[]{:S(2)}) collective-permute-start(bf16[2,288,128]{2,1,0:T(8,128)(2,1)} %get-tuple-element.35), channel_id=1, source_target_pairs={{0,96},{32,0},{64,32},{96,64},{1,97},{33,1},{65,33},{97,65},{2,98}... | collective-permute-start | bytes 442376 | tf_op jit(solution)/shard_map/ppermute | solution.py:128
